TPU v7x, 512 devices: a whole 4x8x8 slice. The times are simulated.
512 devices in a mesh: space: 128 (over x, y, z_lo, core), band: 4 (over z_hi).
Axes of the slice: x: 4, y: 8, z: 8 (z_hi: 4, z_lo: 2; z = z_hi * 2 + z_lo), core: 2. Of those that a mesh axis runs over, the one named last changes fastest.
Arguments:
- states_in: bfloat16 [256, 262144], P('band', 'space'), may hold values from -6 to 6
- kinetic: bfloat16 [64, 64], replicated, may hold values from -0.75 to 0.75
- cell_scale: float32 [32768], P('space'), may hold values from 0.5 to 2
- cell_nodes: int32 [64, 32768], P(None, 'space'), may hold values from 0 to 4095
- boundary: int32 [65536], P('space'), may hold values from 0 to 2047, as said below
- potential: float32 [262144], P('space'), may hold values from -2 to 2
- inv_mass_root: float32 [262144], P('space'), may hold values from 0.2 to 1.875
Outputs:
- filtered: bfloat16 [256, 262144], P('band', 'space')
- margin: float32 [256, 256], P('band')
Inputs may be any that keep to these rules, and one draw needn't show every extreme that they name: `boundary`: each partition's 512 entries are distinct node numbers of that partition. `cell_nodes`: A value below 2048 is a node of the cell's own partition; a value 2048 + j * 512 + b is entry b of the boundary list of the partition whose space index is the cell's own plus (-2, -1, 1, 2)[j], taken modulo the number of partitions.
All inputs are finite; a program needn't handle non-finite values.
Results may differ from a plain program's by a relative error of at most 0.0095.
Values may be sent and summed in bfloat16 or wider, within the bound.
No kernel may reach another device: no remote copies, remote signals or barrier semaphores. Data moves between devices by JAX's collectives and lax.ppermute only.
A program may use at most 64 MiB of HBM per device.

v0:
```python
import jax
import jax.numpy as jnp
from jax import lax
from jax.sharding import Mesh
from jax.sharding import PartitionSpec as P

SPACE = ("space_0", "space_1", "space_2", "space_3")


OFFSETS = (-2, -1, 1, 2)
CENTER = 0.5
HALF = 6.0


def from_behind(x, axis, by):
    count = lax.axis_size(axis)
    return lax.ppermute(x, axis, [(i, (i + by) % count) for i in range(count)])


def in_blocks(x, dim, count):
    dims = x.shape
    blocks = x.reshape(*dims[:dim], count, dims[dim] // count, *dims[dim + 1 :])
    return jnp.moveaxis(blocks, dim, 0)


def sum_at_owner(x, axis, dim):
    count = lax.axis_size(axis)
    blocks = lax.all_to_all(in_blocks(x, dim, count), axis, 0, 0, tiled=True)
    return jnp.sum(blocks.astype(jnp.float32), axis=0)


def sent_and_summed(x, axis, dim):
    blocks = in_blocks(x, dim, lax.axis_size(axis))
    arrived = lax.all_to_all(blocks, axis, split_axis=0, concat_axis=0, tiled=True)
    return arrived.sum(axis=0)


def summed_rows(x, axes, dim):
    far, near = axes
    blocks = in_blocks(x, dim, lax.axis_size(far))
    nearer = sent_and_summed(blocks, near, dim + 1)
    arrived = lax.all_to_all(nearer, far, split_axis=0, concat_axis=0, tiled=True)
    return arrived.sum(axis=0)


def rows_for(lines, count):
    spare = -len(lines) % count
    return jnp.pad(lines, [(0, spare)] + [(0, 0)] * (lines.ndim - 1))


def from_everyone(x, axis):
    count = lax.axis_size(axis)
    return lax.all_to_all(jnp.broadcast_to(x[None], (count, *x.shape)), axis, 0, 0, tiled=True)


def laid_out(blocks, dim):
    blocks = jnp.moveaxis(blocks, 0, dim)
    dims = blocks.shape
    return blocks.reshape(*dims[:dim], dims[dim] * dims[dim + 1], *dims[dim + 2 :])


def gather_axes(x, axes, dim):
    far, near = axes
    leading = from_everyone(x, far)
    blocks = jnp.swapaxes(from_everyone(leading, near), 0, 1)
    return laid_out(blocks.reshape(-1, *x.shape), dim)


def total_of(x, axes):
    lines = x.reshape(-1)
    own = summed_rows(rows_for(lines, lax.axis_size(axes[0]) * lax.axis_size(axes[1])), axes, 0)
    whole = gather_axes(own, axes, 0)
    return whole[: len(lines)].reshape(x.shape)


def apply_operator(values, kinetic, cell_nodes, cell_scale, potential, inv_root, boundary):
    owned_count = values.shape[1]
    rim_width = boundary.shape[0]
    state_rows = values.shape[0]
    scaled = (inv_root[None, :] * values.astype(jnp.float32)).astype(jnp.bfloat16)
    rim_values = jnp.take(scaled, boundary, axis=1)
    ext_pieces = [scaled]
    for offset in OFFSETS:
        ext_pieces.append(from_behind(rim_values, SPACE, -offset))
    extended = jnp.concatenate(ext_pieces, axis=1)
    gathered = jnp.take(extended, cell_nodes, axis=1)
    cell_terms = jnp.einsum("ij,sjc->sic", kinetic, gathered, preferred_element_type=jnp.float32)
    cell_terms = cell_terms * cell_scale[None, None, :]
    totals = jnp.zeros((state_rows, extended.shape[1]), jnp.float32)
    totals = totals.at[:, cell_nodes.reshape(-1)].add(cell_terms.reshape(state_rows, -1))
    result = totals[:, :owned_count]
    for slot_index, offset in enumerate(OFFSETS):
        lower = owned_count + slot_index * rim_width
        ghost_part = totals[:, lower : lower + rim_width]
        arrived = from_behind(ghost_part, SPACE, offset)
        result = result.at[:, boundary].add(arrived)
    return inv_root[None, :] * (result + potential[None, :] * scaled.astype(jnp.float32))


def inner_rows(left, right):
    return lax.dot_general(
        left,
        right,
        (((1,), (1,)), ((), ())),
        precision=lax.Precision.HIGHEST,
        preferred_element_type=jnp.float32,
    )


def body(states_in, kinetic, cell_scale, cell_nodes, boundary, potential, inv_mass_root):

    def operate(values):
        return apply_operator(
            values, kinetic, cell_nodes, cell_scale, potential, inv_mass_root, boundary
        )

    start_f = states_in.astype(jnp.float32)
    first = ((operate(states_in) - CENTER * start_f) / HALF).astype(jnp.bfloat16)
    second = 2.0 * (operate(first) - CENTER * first.astype(jnp.float32)) / HALF - start_f
    filtered = second.astype(jnp.bfloat16)
    node_total = states_in.shape[1] * lax.axis_size(SPACE)
    regrouped = lax.all_to_all(
        second.astype(jnp.bfloat16), "band", split_axis=1, concat_axis=0, tiled=True
    ).astype(second.dtype)
    partial_sum = inner_rows(regrouped, regrouped)
    reduced = sum_at_owner(partial_sum.astype(jnp.bfloat16), "band", 0)
    mine = total_of(reduced, (("space_0", "space_1", "space_2"), "space_3"))
    return (filtered, mine / node_total)


def solution(mesh):
    split = Mesh(
        mesh.devices.reshape(4, 8, 2, 2, mesh.shape["band"]),
        ("space_0", "space_1", "space_2", "space_3", "band"),
    )
    in_specs = (P("band", SPACE), P(), P(SPACE), P(None, SPACE), P(SPACE), P(SPACE), P(SPACE))
    out_specs = (P("band", SPACE), P("band", None))
    return jax.shard_map(body, mesh=split, in_specs=in_specs, out_specs=out_specs, check_vma=False)
```

profile of v0, /device:TPU:1, one launch (start us, length us, event | category | flops | bytes accessed | tf_op | source)
XLA Modules:
  0.0 539.6 jit_solution(1915339490819838997)
XLA Ops:
  0.7 0.7 compare_and_fusion.1
  1.4 0.7 compare_select_fusion.2
  2.1 1.2 copy.29
  3.3 1.0 constant_dynamic-update-slice_fusion.4
  4.3 1.3 gather_fusion
  5.7 0.1 select_bitcast_fusion.1
  5.8 9.9 %collective-permute-start.3 = (bf16[64,512]{0,1:T(8,128)(2,1)S(1)}, bf16[64,512]{0,1:T(8,128)(2,1)S(1)}, u32[]{:S(2)}, u32[]{:S(2)}) collective-permute-start(bf16[64,512]{0,1:T(8,128)(2,1)S(1)} %select_bitcast_fusion.1), channel_id=1, source_target_pairs={{0,504},{4,508},{8,0},{12,4},{16,8},{20,12},{24,16},{28,20},{32,24... | collective-permute-start | bytes 196616 | tf_op jit(solution)/shard_map/ppermute | solution.py:17
  15.8 2.9 collective-permute-start.2
  18.6 2.7 collective-permute-start.1
  21.3 1.9 collective-permute-start
  23.4 0.7 compare_select_fusion
  24.2 8.6 %collective-permute-done = bf16[64,512]{0,1:T(8,128)(2,1)S(1)} collective-permute-done((bf16[64,512]{0,1:T(8,128)(2,1)S(1)}, bf16[64,512]{0,1:T(8,128)(2,1)S(1)}, u32[]{:S(2)}, u32[]{:S(2)}) %collective-permute-start) | collective-permute-done | bytes 65568 | tf_op jit(solution)/shard_map/ppermute | solution.py:17
  32.9 57.4 %gather_fusion.1 = bf16[16384,64]{1,0:T(8,128)(2,1)} fusion(bf16[64,4096]{0,1:T(8,128)(2,1)S(1)} %constant_dynamic-update-slice_fusion, s32[16384]{0:T(1024)S(1)} %broadcast_clamp_fusion), kind=kCustom, calls=%fused_computation.1.clone | custom fusion | bytes 4259840 | tf_op jit(solution)/shard_map/jit(_take)/gather | solution.py:86
  90.3 4.7 copy.30
  95.1 2.7 multiply_bitcast_fusion.1
  97.7 7.0 %copy.38 = f32[64,64,256]{0,2,1:T(8,128)} copy(f32[64,64,256]{2,1,0:T(8,128)} %multiply_bitcast_fusion.1) | data formatting | bytes 8388608 | tf_op jit(solution)/shard_map/reshape | solution.py:90
  104.7 88.1 %scatter_custom_fusion = f32[64,4096]{0,1:T(8,128)S(1)} fusion(s32[16384]{0:T(1024)} %bitcast.88, f32[16384,64]{1,0:T(8,128)} %bitcast.78, f32[]{:T(128)} %constant.24.clone.1), kind=kCustom, calls=%fused_computation.42 | custom fusion | flops 1048576 | bytes 1049088 | tf_op jit(solution)/shard_map/scatter-add | solution.py:90
  192.8 1.0 fusion.44
  193.8 1.9 collective-permute-start.7
  195.7 1.9 collective-permute-start.6
  197.6 2.5 collective-permute-start.5
  200.1 7.9 %collective-permute-start.4 = (f32[64,512]{0,1:T(8,128)S(1)}, f32[64,512]{0,1:T(8,128)}, u32[]{:S(2)}, u32[]{:S(2)}) collective-permute-start(f32[64,512]{0,1:T(8,128)S(1)} %get-tuple-element.23), channel_id=1, source_target_pairs={{0,504},{4,508},{8,0},{12,4},{16,8},{20,12},{24,16},{28,20},{32,24... | collective-permute-start | bytes 393224 | tf_op jit(solution)/shard_map/ppermute | solution.py:17
  208.0 1.6 slice_add_fusion.1
  209.6 4.5 collective-permute-done.4
  214.1 4.1 scatter_custom_fusion.1
  218.2 4.1 scatter_custom_fusion.2
  222.3 4.3 scatter_custom_fusion.3
  226.6 3.7 scatter_custom_fusion.4
  230.4 0.3 constant_dynamic-update-slice_fusion.9
  230.7 1.3 gather_fusion.2
  232.2 1.9 collective-permute-start.8
  234.1 8.4 %collective-permute-start.11 = (bf16[64,512]{0,1:T(8,128)(2,1)S(1)}, bf16[64,512]{0,1:T(8,128)(2,1)S(1)}, u32[]{:S(2)}, u32[]{:S(2)}) collective-permute-start(bf16[64,512]{0,1:T(8,128)(2,1)S(1)} %select_bitcast_fusion), channel_id=1, source_target_pairs={{0,504},{4,508},{8,0},{12,4},{16,8},{20,12},{24,16},{28,20},{32,24... | collective-permute-start | bytes 196616 | tf_op jit(solution)/shard_map/ppermute | solution.py:17
  242.6 3.9 collective-permute-start.10
  246.4 1.9 collective-permute-start.9
  248.4 1.9 collective-permute-done.9
  250.4 57.4 %gather_fusion.3 = bf16[16384,64]{1,0:T(8,128)(2,1)} fusion(bf16[64,4096]{0,1:T(8,128)(2,1)S(1)} %constant_dynamic-update-slice_fusion.5, s32[16384]{0:T(1024)S(1)} %broadcast_clamp_fusion), kind=kCustom, calls=%fused_computation.3.clone | custom fusion | bytes 4259840 | tf_op jit(solution)/shard_map/jit(_take)/gather | solution.py:86
  307.8 5.7 %copy.32 = bf16[64,256,64]{1,0,2:T(8,128)(2,1)} copy(bf16[64,256,64]{2,1,0:T(8,128)(2,1)} %bitcast.75) | data formatting | bytes 4194304 | tf_op jit(solution)/shard_map/jit(_take)/gather | solution.py:86
  313.5 4.3 multiply_bitcast_fusion
  317.7 7.0 %copy.39 = f32[64,64,256]{0,2,1:T(8,128)} copy(f32[64,64,256]{2,1,0:T(8,128)} %multiply_bitcast_fusion) | data formatting | bytes 8388608 | tf_op jit(solution)/shard_map/reshape | solution.py:90
  324.7 89.1 %scatter_custom_fusion.5 = f32[64,4096]{0,1:T(8,128)} fusion(s32[16384]{0:T(1024)} %bitcast.89, f32[16384,64]{1,0:T(8,128)} %bitcast.77, f32[]{:T(128)} %constant.24.clone.1), kind=kCustom, calls=%fused_computation.40 | custom fusion | flops 1048576 | bytes 1049088 | tf_op jit(solution)/shard_map/scatter-add | solution.py:90
  413.8 2.2 fusion.43
  416.0 1.9 collective-permute-start.15
  417.9 4.4 collective-permute-start.14
  422.2 6.1 %collective-permute-start.13 = (f32[64,512]{0,1:T(8,128)}, f32[64,512]{0,1:T(8,128)S(1)}, u32[]{:S(2)}, u32[]{:S(2)}) collective-permute-start(f32[64,512]{0,1:T(8,128)} %get-tuple-element.18), channel_id=1, source_target_pairs={{0,508},{4,0},{8,4},{12,8},{16,12},{20,16},{24,20},{28,24},{32,28}... | collective-permute-start | bytes 393224 | tf_op jit(solution)/shard_map/ppermute | solution.py:17
  428.4 8.1 %collective-permute-start.12 = (f32[64,512]{0,1:T(8,128)S(1)}, f32[64,512]{0,1:T(8,128)S(1)}, u32[]{:S(2)}, u32[]{:S(2)}) collective-permute-start(f32[64,512]{0,1:T(8,128)S(1)} %get-tuple-element.19), channel_id=1, source_target_pairs={{0,504},{4,508},{8,0},{12,4},{16,8},{20,12},{24,16},{28,20},{32,24... | collective-permute-start | bytes 393224 | tf_op jit(solution)/shard_map/ppermute | solution.py:17
  436.5 1.3 slice_add_fusion
  437.8 4.5 collective-permute-done.12
  442.4 5.2 scatter_custom_fusion.6
  447.6 5.2 scatter_custom_fusion.7
  452.8 5.2 scatter_custom_fusion.8
  458.0 5.2 scatter_custom_fusion.9
  463.2 1.7 fusion.13
  464.9 0.2 copy.34
  465.1 17.3 %all_to_all.49 = bf16[64,4,512]{2,0,1:T(8,128)(2,1)S(1)} all-to-all(bf16[64,4,512]{2,0,1:T(8,128)(2,1)S(1)} %copy.34), channel_id=1, replica_groups=mesh['space_0'=4,'space_1'=8,'space_2'=2,'space_3'=2,'band'=4] {'band'}, dimensions={1} | all-to-all | bytes 524288 | tf_op jit(solution)/shard_map/all_to_all | solution.py:122
  482.4 0.3 convolution_convert_fusion
  482.7 9.6 %all_to_all.50 = bf16[4,64,256]{2,1,0:T(8,128)(2,1)S(1)} all-to-all(bf16[4,64,256]{2,1,0:T(8,128)(2,1)S(1)} %bitcast.82), channel_id=1, replica_groups=mesh['space_0'=4,'space_1'=8,'space_2'=2,'space_3'=2,'band'=4] {'band'}, dimensions={0} | all-to-all | bytes 262144 | tf_op jit(solution)/shard_map/all_to_all | solution.py:28
  492.4 8.0 %all_to_all.51 = f32[2,64,128]{2,1,0:T(8,128)S(1)} all-to-all(f32[2,64,128]{2,1,0:T(8,128)S(1)} %copy.35), channel_id=1, replica_groups=mesh['space_0'=4,'space_1'=8,'space_2'=2,'space_3'=2,'band'=4] {'space_3'}, dimensions={0} | all-to-all | bytes 131072 | tf_op jit(solution)/shard_map/all_to_all | solution.py:34
  500.4 17.7 %all_to_all.52 = f32[64,1,128]{2,1,0:T(1,128)S(1)} all-to-all(f32[64,1,128]{2,1,0:T(1,128)S(1)} %bitcast.87), channel_id=1, replica_groups=mesh['space_0'=4,'space_1'=8,'space_2'=2,'space_3'=2,'band'=4] {'space_0..., dimensions={0} | all-to-all | bytes 65536 | tf_op jit(solution)/shard_map/all_to_all | solution.py:42
  518.2 0.6 broadcast_in_dim.27
  518.8 4.6 all-to-all-start.4
  523.4 0.9 copy.37
  524.3 8.3 %all-to-all-done.4 = f32[64,1,128]{2,1,0:T(1,128)S(1)} async-done(((f32[64,1,128]{2,1,0:T(1,128)}), f32[64,1,128]{2,1,0:T(1,128)S(1)}, u32[]{:S(2)}, u32[]{:S(2)}) %all-to-all-start.4) | async-done | bytes 32800 | tf_op jit(solution)/shard_map/all_to_all | solution.py:53
  532.6 6.4 %all_to_all.53 = f32[2,64,128]{2,1,0:T(8,128)S(1)} all-to-all(f32[2,64,128]{2,1,0:T(8,128)S(1)} %broadcast_in_dim.29), channel_id=1, replica_groups=mesh['space_0'=4,'space_1'=8,'space_2'=2,'space_3'=2,'band'=4] {'space_3'}, dimensions={0} | all-to-all | bytes 131072 | tf_op jit(solution)/shard_map/all_to_all | solution.py:53
  538.9 0.6 copy_bitcast_fusion
  (47 shorter events, 0.7 us)
Async XLA Ops:
  0.6 94.4 %copy-start = (bf16[64,64]{1,0:T(8,128)(2,1)S(1)}, bf16[64,64]{1,0:T(8,128)(2,1)}, u32[]{:S(2)}) copy-start(bf16[64,64]{1,0:T(8,128)(2,1)} %param.12) | copy-start | bytes 24580
  0.6 22.6 %copy-start.3 = (s32[64,256]{1,0:T(8,128)S(1)}, s32[64,256]{1,0:T(8,128)}, u32[]{:S(2)}) copy-start(s32[64,256]{1,0:T(8,128)} %param.14) | copy-start | bytes 196612
  5.8 27.1 %collective-permute-start.3 = (bf16[64,512]{0,1:T(8,128)(2,1)S(1)}, bf16[64,512]{0,1:T(8,128)(2,1)S(1)}, u32[]{:S(2)}, u32[]{:S(2)}) collective-permute-start(bf16[64,512]{0,1:T(8,128)(2,1)S(1)} %select_bitcast_fusion.1), channel_id=1, source_target_pairs={{0,504},{4,508},{8,0},{12,4},{16,8},{20,12},{24,16},{28,20},{32,24... | collective-permute-start | bytes 196616 | tf_op jit(solution)/shard_map/ppermute | solution.py:17
  15.8 17.1 %collective-permute-start.2 = (bf16[64,512]{0,1:T(8,128)(2,1)S(1)}, bf16[64,512]{0,1:T(8,128)(2,1)S(1)}, u32[]{:S(2)}, u32[]{:S(2)}) collective-permute-start(bf16[64,512]{0,1:T(8,128)(2,1)S(1)} %select_bitcast_fusion.1), channel_id=1, source_target_pairs={{0,508},{4,0},{8,4},{12,8},{16,12},{20,16},{24,20},{28,24},{32,28}... | collective-permute-start | bytes 196616 | tf_op jit(solution)/shard_map/ppermute | solution.py:17
  18.6 14.2 %collective-permute-start.1 = (bf16[64,512]{0,1:T(8,128)(2,1)S(1)}, bf16[64,512]{0,1:T(8,128)(2,1)S(1)}, u32[]{:S(2)}, u32[]{:S(2)}) collective-permute-start(bf16[64,512]{0,1:T(8,128)(2,1)S(1)} %select_bitcast_fusion.1), channel_id=1, source_target_pairs={{0,4},{4,8},{8,12},{12,16},{16,20},{20,24},{24,28},{28,32},{32,36}... | collective-permute-start | bytes 196616 | tf_op jit(solution)/shard_map/ppermute | solution.py:17
  21.3 11.4 %collective-permute-start = (bf16[64,512]{0,1:T(8,128)(2,1)S(1)}, bf16[64,512]{0,1:T(8,128)(2,1)S(1)}, u32[]{:S(2)}, u32[]{:S(2)}) collective-permute-start(bf16[64,512]{0,1:T(8,128)(2,1)S(1)} %select_bitcast_fusion.1), channel_id=1, source_target_pairs={{0,8},{4,12},{8,16},{12,20},{16,24},{20,28},{24,32},{28,36},{32,40... | collective-permute-start | bytes 196616 | tf_op jit(solution)/shard_map/ppermute | solution.py:17
  90.3 4.7 copy-start.6
  104.7 103.3 %copy-start.5 = (f32[2048]{0:T(1024)S(1)}, f32[2048]{0:T(1024)}, u32[]{:S(2)}) copy-start(f32[2048]{0:T(1024)} %param.16) | copy-start | bytes 24580
  192.8 7.3 %copy-start.2 = (f32[64,4096]{0,1:T(8,128)}, f32[64,4096]{0,1:T(8,128)S(1)}, u32[]{:S(2)}) copy-start(f32[64,4096]{0,1:T(8,128)S(1)} %scatter_custom_fusion) | copy-start | bytes 3145732
  193.8 32.9 %collective-permute-start.7 = (f32[64,512]{0,1:T(8,128)}, f32[64,512]{0,1:T(8,128)S(1)}, u32[]{:S(2)}, u32[]{:S(2)}) collective-permute-start(f32[64,512]{0,1:T(8,128)} %get-tuple-element.20), channel_id=1, source_target_pairs={{0,8},{4,12},{8,16},{12,20},{16,24},{20,28},{24,32},{28,36},{32,40... | collective-permute-start | bytes 393224 | tf_op jit(solution)/shard_map/ppermute | solution.py:17
  195.7 26.6 %collective-permute-start.6 = (f32[64,512]{0,1:T(8,128)}, f32[64,512]{0,1:T(8,128)}, u32[]{:S(2)}, u32[]{:S(2)}) collective-permute-start(f32[64,512]{0,1:T(8,128)} %get-tuple-element.21), channel_id=1, source_target_pairs={{0,4},{4,8},{8,12},{12,16},{16,20},{20,24},{24,28},{28,32},{32,36}... | collective-permute-start | bytes 393224 | tf_op jit(solution)/shard_map/ppermute | solution.py:17
  197.6 20.6 %collective-permute-start.5 = (f32[64,512]{0,1:T(8,128)}, f32[64,512]{0,1:T(8,128)}, u32[]{:S(2)}, u32[]{:S(2)}) collective-permute-start(f32[64,512]{0,1:T(8,128)} %get-tuple-element.22), channel_id=1, source_target_pairs={{0,508},{4,0},{8,4},{12,8},{16,12},{20,16},{24,20},{28,24},{32,28}... | collective-permute-start | bytes 393224 | tf_op jit(solution)/shard_map/ppermute | solution.py:17
  200.1 14.0 %collective-permute-start.4 = (f32[64,512]{0,1:T(8,128)S(1)}, f32[64,512]{0,1:T(8,128)}, u32[]{:S(2)}, u32[]{:S(2)}) collective-permute-start(f32[64,512]{0,1:T(8,128)S(1)} %get-tuple-element.23), channel_id=1, source_target_pairs={{0,504},{4,508},{8,0},{12,4},{16,8},{20,12},{24,16},{28,20},{32,24... | collective-permute-start | bytes 393224 | tf_op jit(solution)/shard_map/ppermute | solution.py:17
  218.2 12.2 %copy-start.4 = (f32[2048]{0:T(1024)S(1)}, f32[2048]{0:T(1024)}, u32[]{:S(2)}) copy-start(f32[2048]{0:T(1024)} %param.17) | copy-start | bytes 24580
  232.2 16.2 %collective-permute-start.8 = (bf16[64,512]{0,1:T(8,128)(2,1)S(1)}, bf16[64,512]{0,1:T(8,128)(2,1)S(1)}, u32[]{:S(2)}, u32[]{:S(2)}) collective-permute-start(bf16[64,512]{0,1:T(8,128)(2,1)S(1)} %select_bitcast_fusion), channel_id=1, source_target_pairs={{0,8},{4,12},{8,16},{12,20},{16,24},{20,28},{24,32},{28,36},{32,40... | collective-permute-start | bytes 196616 | tf_op jit(solution)/shard_map/ppermute | solution.py:17
  234.1 16.2 %collective-permute-start.11 = (bf16[64,512]{0,1:T(8,128)(2,1)S(1)}, bf16[64,512]{0,1:T(8,128)(2,1)S(1)}, u32[]{:S(2)}, u32[]{:S(2)}) collective-permute-start(bf16[64,512]{0,1:T(8,128)(2,1)S(1)} %select_bitcast_fusion), channel_id=1, source_target_pairs={{0,504},{4,508},{8,0},{12,4},{16,8},{20,12},{24,16},{28,20},{32,24... | collective-permute-start | bytes 196616 | tf_op jit(solution)/shard_map/ppermute | solution.py:17
  242.6 7.7 %collective-permute-start.10 = (bf16[64,512]{0,1:T(8,128)(2,1)S(1)}, bf16[64,512]{0,1:T(8,128)(2,1)S(1)}, u32[]{:S(2)}, u32[]{:S(2)}) collective-permute-start(bf16[64,512]{0,1:T(8,128)(2,1)S(1)} %select_bitcast_fusion), channel_id=1, source_target_pairs={{0,508},{4,0},{8,4},{12,8},{16,12},{20,16},{24,20},{28,24},{32,28}... | collective-permute-start | bytes 196616 | tf_op jit(solution)/shard_map/ppermute | solution.py:17
  246.4 3.9 collective-permute-start.9
  413.7 22.7 %copy-start.1 = (f32[64,4096]{0,1:T(8,128)S(1)}, f32[64,4096]{0,1:T(8,128)}, u32[]{:S(2)}) copy-start(f32[64,4096]{0,1:T(8,128)} %scatter_custom_fusion.5) | copy-start | bytes 3145732
  416.0 42.1 %collective-permute-start.15 = (f32[64,512]{0,1:T(8,128)S(1)}, f32[64,512]{0,1:T(8,128)S(1)}, u32[]{:S(2)}, u32[]{:S(2)}) collective-permute-start(f32[64,512]{0,1:T(8,128)S(1)} %get-tuple-element.16), channel_id=1, source_target_pairs={{0,8},{4,12},{8,16},{12,20},{16,24},{20,28},{24,32},{28,36},{32,40... | collective-permute-start | bytes 393224 | tf_op jit(solution)/shard_map/ppermute | solution.py:17
  417.9 34.9 %collective-permute-start.14 = (f32[64,512]{0,1:T(8,128)}, f32[64,512]{0,1:T(8,128)S(1)}, u32[]{:S(2)}, u32[]{:S(2)}) collective-permute-start(f32[64,512]{0,1:T(8,128)} %get-tuple-element.17), channel_id=1, source_target_pairs={{0,4},{4,8},{8,12},{12,16},{16,20},{20,24},{24,28},{28,32},{32,36}... | collective-permute-start | bytes 393224 | tf_op jit(solution)/shard_map/ppermute | solution.py:17
  422.2 25.3 %collective-permute-start.13 = (f32[64,512]{0,1:T(8,128)}, f32[64,512]{0,1:T(8,128)S(1)}, u32[]{:S(2)}, u32[]{:S(2)}) collective-permute-start(f32[64,512]{0,1:T(8,128)} %get-tuple-element.18), channel_id=1, source_target_pairs={{0,508},{4,0},{8,4},{12,8},{16,12},{20,16},{24,20},{28,24},{32,28}... | collective-permute-start | bytes 393224 | tf_op jit(solution)/shard_map/ppermute | solution.py:17
  428.4 14.0 %collective-permute-start.12 = (f32[64,512]{0,1:T(8,128)S(1)}, f32[64,512]{0,1:T(8,128)S(1)}, u32[]{:S(2)}, u32[]{:S(2)}) collective-permute-start(f32[64,512]{0,1:T(8,128)S(1)} %get-tuple-element.19), channel_id=1, source_target_pairs={{0,504},{4,508},{8,0},{12,4},{16,8},{20,12},{24,16},{28,20},{32,24... | collective-permute-start | bytes 393224 | tf_op jit(solution)/shard_map/ppermute | solution.py:17
  518.8 13.8 %all-to-all-start.4 = ((f32[64,1,128]{2,1,0:T(1,128)}), f32[64,1,128]{2,1,0:T(1,128)S(1)}, u32[]{:S(2)}, u32[]{:S(2)}) async-start(f32[64,1,128]{2,1,0:T(1,128)} %broadcast_in_dim.27), calls=%async_computation.4 | async-start | bytes 65536 | tf_op jit(solution)/shard_map/all_to_all | solution.py:53
where the time goes:
time: 541 us; the launch traced here: 540 us
  other arithmetic  223 us (41%)
  local copies, waits for them, and re-layouts  148 us (27%)
  starting transfers between devices  72.8 us (13%)
  blocking collectives  59 us (11%)
  waiting for transfers between devices  27.9 us (5%)
  matrix products  7.21 us (1%)
    scatter-add x2, other arithmetic, apply_operator(): totals.at[:, cell_nodes.reshape(-1)].add(cell_terms.reshape(state_rows, -1))  177 us
    gather x4, local copies, waits for them, and re-layouts, apply_operator(): gathered = jnp.take(extended, cell_nodes, axis=1)  125 us
    ppermute x16, starting transfers between devices, from_behind(): return lax.ppermute(x, axis, [(i, (i + by) % count) for i in range(count)])  68.2 us
    scatter-add x8, other arithmetic, apply_operator(): result = result.at[:, boundary].add(arrived)  37 us
    ppermute x16, waiting for transfers between devices, from_behind(): return lax.ppermute(x, axis, [(i, (i + by) % count) for i in range(count)])  19.6 us
    all_to_all x1, blocking collectives, summed_rows(): lax.all_to_all(nearer, far, split_axis=0, concat_axis=0, tiled=True)  17.7 us
    all_to_all x1, blocking collectives, body(): lax.all_to_all(second.astype(jnp.bfloat16), 'band', split_axis=1, concat_...  17.3 us
    reshape x2, local copies, waits for them, and re-layouts, apply_operator(): cell_terms.reshape(state_rows, -1)  13.9 us
  transfers between devices with their start and end apart: 17, of which 5 were waited for; matrix products, arithmetic and copies ran while one was open for 6% of the time, Pallas kernels for 0%

commit v1 on v0

v1 whole, which is shorter than its diff:
```python
import jax
import jax.numpy as jnp
from jax import lax
from jax.experimental import pallas as pl
from jax.experimental.pallas import tpu as pltpu
from jax.sharding import Mesh
from jax.sharding import PartitionSpec as P

SPACE = ("space_0", "space_1", "space_2", "space_3")
OFFSETS = (-2, -1, 1, 2)
CENTER = 0.5
HALF = 6.0
TILE = 256
STEP = 1024
BF = jnp.bfloat16
F32 = jnp.float32


def from_behind(x, axis, by):
    count = lax.axis_size(axis)
    return lax.ppermute(x, axis, [(i, (i + by) % count) for i in range(count)])


def selection(index, base, count):
    width = index.shape[1]
    high = index // TILE
    low = (index % TILE).astype(F32)
    lines = lax.broadcasted_iota(jnp.int32, (TILE, width), 0).astype(F32).astype(BF)
    tiles = []
    for tile in range(count // TILE):
        here = jnp.where(high == base // TILE + tile, low, -1.0).astype(BF)
        tiles.append(jnp.where(lines == here, jnp.ones((), BF), jnp.zeros((), BF)))
    return jnp.concatenate(tiles, axis=0)


def picked(values, chosen):
    return jnp.dot(values, chosen, preferred_element_type=F32)


def put_back(values, chosen):
    return lax.dot_general(values, chosen, (((1,), (1,)), ((), ())), preferred_element_type=F32)


def prepare_kernel(values, inv_root, boundary, scaled_ref, rim_ref):
    scaled = (inv_root[...] * values[...].astype(F32)).astype(BF)
    scaled_ref[...] = scaled
    chosen = selection(boundary[...], 0, scaled.shape[1])
    rim_ref[...] = picked(scaled, chosen).astype(BF)


def prepare(values, inv_root, boundary):
    rows, owned = values.shape
    return pl.pallas_call(
        prepare_kernel,
        out_shape=(
            jax.ShapeDtypeStruct((rows, owned), BF),
            jax.ShapeDtypeStruct((rows, boundary.shape[1]), BF),
        ),
        name="prepare",
    )(values, inv_root, boundary)


def cells_kernel(owned, index, scale, kinetic, table, out_ref, rim_ref, acc):
    step = pl.program_id(0)
    chosen = selection(index[...], 0, table.shape[1])
    gathered = picked(table[...], chosen).astype(BF)
    terms = jnp.concatenate(
        [
            jnp.dot(gathered[:, i : i + TILE], kinetic[...], preferred_element_type=F32)
            for i in range(0, gathered.shape[1], TILE)
        ],
        axis=1,
    )
    terms = (terms * scale[...]).astype(BF)
    part = put_back(terms, chosen)

    @pl.when(step == 0)
    def _():
        acc[...] = part

    @pl.when(step > 0)
    def _():
        acc[...] += part

    @pl.when(step == pl.num_programs(0) - 1)
    def _():
        out_ref[...] = acc[:, :owned]
        rim_ref[...] = acc[:, owned:].astype(BF)


def cells(table, owned, index, scale, kinetic):
    rows, nodes = table.shape
    places = index.shape[1]
    line = pl.BlockSpec((1, STEP), lambda i: (0, i))

    def kernel(*refs):
        cells_kernel(owned, *refs)

    return pl.pallas_call(
        kernel,
        grid=(places // STEP,),
        in_specs=[
            line,
            line,
            pl.BlockSpec(kinetic.shape, lambda i: (0, 0)),
            pl.BlockSpec((rows, nodes), lambda i: (0, 0)),
        ],
        out_specs=(
            pl.BlockSpec((rows, owned), lambda i: (0, 0)),
            pl.BlockSpec((rows, nodes - owned), lambda i: (0, 0)),
        ),
        out_shape=(
            jax.ShapeDtypeStruct((rows, owned), F32),
            jax.ShapeDtypeStruct((rows, nodes - owned), BF),
        ),
        scratch_shapes=[pltpu.VMEM((rows, nodes), F32)],
        name="cells",
    )(index, scale, kinetic, table)


def image_of(own, arrived, scaled, inv_root, potential, chosen):
    back = arrived[0][...].astype(F32)
    for part in arrived[1:]:
        back = back + part[...].astype(F32)
    upper = back.astype(BF)
    lower = (back - upper.astype(F32)).astype(BF)
    both = put_back(jnp.concatenate([upper, lower], axis=0), chosen)
    rows = back.shape[0]
    total = own[...] + both[:rows] + both[rows:]
    return inv_root[...] * (total + potential[...] * scaled[...].astype(F32))


def first_kernel(own, a0, a1, a2, a3, scaled, start, inv_root, potential, boundary, first_ref, scaled_ref, rim_ref):
    chosen = selection(boundary[...], 0, own.shape[1])
    image = image_of(own, (a0, a1, a2, a3), scaled, inv_root, potential, chosen)
    first = ((image - CENTER * start[...].astype(F32)) / HALF).astype(BF)
    first_ref[...] = first
    scaled_new = (inv_root[...] * first.astype(F32)).astype(BF)
    scaled_ref[...] = scaled_new
    rim_ref[...] = picked(scaled_new, chosen).astype(BF)


def second_kernel(own, a0, a1, a2, a3, scaled, start, first, inv_root, potential, boundary, out_ref):
    chosen = selection(boundary[...], 0, own.shape[1])
    image = image_of(own, (a0, a1, a2, a3), scaled, inv_root, potential, chosen)
    second = 2.0 * (image - CENTER * first[...].astype(F32)) / HALF - start[...].astype(F32)
    out_ref[...] = second.astype(BF)


def exchange_out(rim):
    return [from_behind(rim, SPACE, -offset) for offset in OFFSETS]


def exchange_back(ghost, width):
    return [
        from_behind(ghost[:, i * width : (i + 1) * width], SPACE, offset)
        for i, offset in enumerate(OFFSETS)
    ]


def in_blocks(x, dim, count):
    dims = x.shape
    blocks = x.reshape(*dims[:dim], count, dims[dim] // count, *dims[dim + 1 :])
    return jnp.moveaxis(blocks, dim, 0)


def body(states_in, kinetic, cell_scale, cell_nodes, boundary, potential, inv_mass_root):
    nodes_per_cell = kinetic.shape[0]
    rows, owned = states_in.shape
    width = boundary.shape[0]
    index = cell_nodes.T.reshape(1, -1)
    scale = jnp.repeat(cell_scale, nodes_per_cell).reshape(1, -1)
    stacked = jnp.kron(jnp.eye(TILE // nodes_per_cell, dtype=BF), kinetic.T)
    inv_root = inv_mass_root[None]
    potential = potential[None]
    boundary = boundary[None]

    scaled, rim = prepare(states_in, inv_root, boundary)
    table = jnp.concatenate([scaled, *exchange_out(rim)], axis=1)
    own, ghost = cells(table, owned, index, scale, stacked)
    arrived = exchange_back(ghost, width)
    first, scaled, rim = pl.pallas_call(
        first_kernel,
        out_shape=(
            jax.ShapeDtypeStruct((rows, owned), BF),
            jax.ShapeDtypeStruct((rows, owned), BF),
            jax.ShapeDtypeStruct((rows, width), BF),
        ),
        name="first",
    )(own, *arrived, scaled, states_in, inv_root, potential, boundary)
    table = jnp.concatenate([scaled, *exchange_out(rim)], axis=1)
    own, ghost = cells(table, owned, index, scale, stacked)
    arrived = exchange_back(ghost, width)
    filtered = pl.pallas_call(
        second_kernel,
        out_shape=jax.ShapeDtypeStruct((rows, owned), BF),
        name="second",
    )(own, *arrived, scaled, states_in, first, inv_root, potential, boundary)

    node_total = owned * lax.axis_size(SPACE)
    regrouped = lax.all_to_all(filtered, "band", split_axis=1, concat_axis=0, tiled=True)
    partial_sum = lax.dot_general(regrouped, regrouped, (((1,), (1,)), ((), ())), preferred_element_type=F32)
    blocks = in_blocks(partial_sum.astype(BF), 0, lax.axis_size("band"))
    reduced = jnp.sum(lax.all_to_all(blocks, "band", 0, 0, tiled=True).astype(F32), axis=0)
    margin = lax.psum(reduced, SPACE) / node_total
    return filtered, margin


def solution(mesh):
    split = Mesh(
        mesh.devices.reshape(4, 8, 2, 2, mesh.shape["band"]),
        ("space_0", "space_1", "space_2", "space_3", "band"),
    )
    in_specs = (P("band", SPACE), P(), P(SPACE), P(None, SPACE), P(SPACE), P(SPACE), P(SPACE))
    out_specs = (P("band", SPACE), P("band", None))
    return jax.shard_map(body, mesh=split, in_specs=in_specs, out_specs=out_specs, check_vma=False)
```

time: 541 us -> 1220 us (2.26)
  waiting for transfers between devices: 27.9 us -> 952 us
  other arithmetic: 223 us -> 2.3 us
  Pallas kernels: 0 us -> 152 us
  local copies, waits for them, and re-layouts: 148 us -> 10.2 us
  blocking collectives: 59 us -> 26.9 us
  between operations: 1.17 us -> 14.5 us
    psum x0 -> x1, waiting for transfers between devices: none -> 938 us  [body(): margin = lax.psum(reduced, SPACE) / node_total]
    scatter-add x10 -> x0, other arithmetic: 214 us -> none  [the longest x2 177 us: apply_operator(): totals.at[:, cell_nodes.reshape(-1)].add(cell_terms.reshape(state_rows, -1))]
    pallas_call x0 -> x5, Pallas kernels: none -> 152 us  [the longest x2 144 us: cells(): pl.pallas_call(kernel, grid=(places // STEP,), in_specs=[line, line, pl.B...]
    gather x6 -> x0, local copies, waits for them, and re-layouts: 128 us -> none  [the longest x4 125 us: apply_operator(): gathered = jnp.take(extended, cell_nodes, axis=1)]
    all_to_all x5 -> x2, blocking collectives: 59 us -> 26.9 us  [the longest x1 17.1 us: body(): lax.all_to_all(filtered, 'band', split_axis=1, concat_axis=0, tiled=True)]
    reshape x2 -> x1, local copies, waits for them, and re-layouts: 13.9 us -> 0.76 us  [body(): index = cell_nodes.T.reshape(1, -1)]
  transfers between devices with their start and end apart: 17 -> 17, of which waited for: 5 -> 5; matrix products, arithmetic and copies ran while one was open for 6% -> 0% of each run, Pallas kernels for 0% -> 0%
where the time goes in v1:
time: 1220 us
  waiting for transfers between devices  952 us (78%)
  Pallas kernels  152 us (12%)
  starting transfers between devices  63.8 us (5%)
  blocking collectives  26.9 us (2%)
  between operations  14.5 us (1%)
    psum x1, waiting for transfers between devices, body(): margin = lax.psum(reduced, SPACE) / node_total  938 us
    pallas_call x2, Pallas kernels, cells(): pl.pallas_call(kernel, grid=(places // STEP,), in_specs=[line, line, pl.B...  144 us
    ppermute x16, starting transfers between devices, from_behind(): return lax.ppermute(x, axis, [(i, (i + by) % count) for i in range(count)])  63.8 us
  transfers between devices with their start and end apart: 17, of which 5 were waited for; matrix products, arithmetic and copies ran while one was open for 0% of the time, Pallas kernels for 0%

profile of v1, /device:TPU:1, one launch (start us, length us, event | category | flops | bytes accessed | tf_op | source)
XLA Modules:
  0.0 1222.1 jit_solution(9216194950449654440)
XLA Ops:
  7.2 0.0 all-reduce.2.cloned.1.call-start
  7.2 2.1 prepare.1
  9.3 10.0 collective-permute-start.3
  19.4 2.9 collective-permute-start.2
  22.2 2.7 collective-permute-start.1
  24.9 1.9 collective-permute-start
  26.9 0.1 copy.12
  27.0 0.2 broadcast_multiply_fusion
  27.2 0.0 copy-start.13
  27.2 0.6 copy-done.13
  27.8 0.1 broadcast_in_dim.16
  27.9 0.0 copy-start.3
  28.0 0.8 reshape_reshape.3.refs_1_
  28.7 0.1 copy-done.3
  28.8 0.1 copy.11
  28.9 0.8 reshape.27.refs_0_
  29.6 0.9 mul.27.refs_2_
  30.5 4.7 collective-permute-done
  35.2 0.0 collective-permute-done.1
  35.2 0.0 collective-permute-done.2
  35.2 0.0 collective-permute-done.3
  35.3 0.8 copy-done
  36.1 71.9 %cells.2 = (f32[64,2048]{1,0:T(8,128)}, bf16[64,2048]{1,0:T(8,128)(2,1)}) custom-call(s32[1,16384]{1,0:T(1,128)} %reshape.27.refs_0_, f32[1,16384]{1,0:T(1,128)} %reshape_reshape.3.refs_1_, bf16[256,256]{1,0:T(8,128)(2,1)} %mul.27.refs_2_, bf16[64,4096]{1,0:T(8,128)(2,1)} %copy-done), custom_call_target="tpu_custom_call" | custom-call | tf_op jit(solution)/shard_map/cells/pallas_call | solution.py:99
  108.0 1.0 fusion.2
  108.9 1.9 collective-permute-start.7
  110.9 1.9 collective-permute-start.6
  112.8 2.5 collective-permute-start.5
  115.3 7.9 collective-permute-start.4
  123.1 0.0 collective-permute-done.7.a3
  123.2 0.0 collective-permute-done.6.a2
  123.2 0.0 collective-permute-done.5.a1
  123.2 1.2 collective-permute-done.4.a0
  124.5 0.6 copy-done.11
  125.1 3.1 first.1
  128.2 7.9 collective-permute-start.11
  136.1 5.1 collective-permute-start.10
  141.2 1.9 collective-permute-start.9
  143.1 1.9 collective-permute-start.8
  145.1 1.0 constant_dynamic-update-slice_fusion.9
  146.0 6.5 collective-permute-done.8
  152.6 0.0 collective-permute-done.9
  152.6 0.0 collective-permute-done.10
  152.6 0.0 collective-permute-done.11
  152.7 0.8 copy-done.1
  153.5 71.9 %cells.3 = (f32[64,2048]{1,0:T(8,128)}, bf16[64,2048]{1,0:T(8,128)(2,1)}) custom-call(s32[1,16384]{1,0:T(1,128)} %reshape.27.refs_0_, f32[1,16384]{1,0:T(1,128)} %reshape_reshape.3.refs_1_, bf16[256,256]{1,0:T(8,128)(2,1)} %mul.27.refs_2_, bf16[64,4096]{1,0:T(8,128)(2,1)} %copy-done.1), custom_call_target="tpu_custom_call" | custom-call | tf_op jit(solution)/shard_map/cells/pallas_call | solution.py:99
  225.3 1.0 fusion.1
  226.3 1.9 collective-permute-start.15
  228.2 1.9 collective-permute-start.14
  230.2 3.6 collective-permute-start.13
  233.7 7.9 collective-permute-start.12
  241.6 0.0 collective-permute-done.15.a3
  241.6 0.0 collective-permute-done.14.a2
  241.6 0.0 collective-permute-done.13.a1
  241.6 1.2 collective-permute-done.12.a0
  242.9 0.6 copy-done.7
  243.5 3.0 second.1
  246.5 1.0 copy.16
  247.5 17.1 %all_to_all.24 = bf16[64,4,512]{2,0,1:T(8,128)(2,1)S(1)} all-to-all(bf16[64,4,512]{2,0,1:T(8,128)(2,1)S(1)} %bitcast.16), channel_id=1, replica_groups=mesh['space_0'=4,'space_1'=8,'space_2'=2,'space_3'=2,'band'=4] {'band'}, dimensions={1} | all-to-all | bytes 524288 | tf_op jit(solution)/shard_map/all_to_all | solution.py:201
  264.6 0.3 convolution_convert_fusion
  264.9 9.8 all_to_all.25
  274.7 0.6 convert_reduce_fusion
  275.3 0.0 all-reduce.2.cloned.1.call-update
  275.3 938.5 %all-reduce.2.cloned.1.call-done = f32[64,256]{1,0:T(8,128)} async-done(((f32[64,256]{1,0:T(8,128)}), f32[64,256]{1,0:T(8,128)}) %all-reduce.2.cloned.1.call-update) | async-done | bytes 65552 | tf_op jit(solution)/shard_map/psum | solution.py:205
  1213.8 1.5 broadcast_multiply_fusion.1
  (30 shorter events, 0.1 us)
Async XLA Ops:
  7.2 1206.6 %all-reduce.2.cloned.1.call-start = ((), (), s32[]{:S(2)}) async-start(), calls=%async_computation.2 | async-start | bytes 131072 | tf_op jit(solution)/shard_map/psum | solution.py:205
  7.2 19.7 %copy-start.12 = (bf16[64,64]{1,0:T(8,128)(2,1)S(1)}, bf16[64,64]{1,0:T(8,128)(2,1)}, u32[]{:S(2)}) copy-start(bf16[64,64]{1,0:T(8,128)(2,1)} %param.8) | copy-start | bytes 24580
  9.3 17.8 %copy-start.2 = (bf16[64,2048]{1,0:T(8,128)(2,1)S(1)}, bf16[64,2048]{1,0:T(8,128)(2,1)}, u32[]{:S(2)}) copy-start(bf16[64,2048]{1,0:T(8,128)(2,1)} %get-tuple-element.11.scaled) | copy-start | bytes 786436
  9.3 25.9 %collective-permute-start.3 = (bf16[64,512]{1,0:T(8,128)(2,1)}, bf16[64,512]{1,0:T(8,128)(2,1)S(1)}, u32[]{:S(2)}, u32[]{:S(2)}) collective-permute-start(bf16[64,512]{1,0:T(8,128)(2,1)} %get-tuple-element.12), channel_id=1, source_target_pairs={{0,504},{4,508},{8,0},{12,4},{16,8},{20,12},{24,16},{28,20},{32,24... | collective-permute-start | bytes 196616 | tf_op jit(solution)/shard_map/ppermute | solution.py:21
  19.4 15.9 %collective-permute-start.2 = (bf16[64,512]{1,0:T(8,128)(2,1)}, bf16[64,512]{1,0:T(8,128)(2,1)S(1)}, u32[]{:S(2)}, u32[]{:S(2)}) collective-permute-start(bf16[64,512]{1,0:T(8,128)(2,1)} %get-tuple-element.12), channel_id=1, source_target_pairs={{0,508},{4,0},{8,4},{12,8},{16,12},{20,16},{24,20},{28,24},{32,28}... | collective-permute-start | bytes 196616 | tf_op jit(solution)/shard_map/ppermute | solution.py:21
  22.2 13.0 %collective-permute-start.1 = (bf16[64,512]{1,0:T(8,128)(2,1)}, bf16[64,512]{1,0:T(8,128)(2,1)S(1)}, u32[]{:S(2)}, u32[]{:S(2)}) collective-permute-start(bf16[64,512]{1,0:T(8,128)(2,1)} %get-tuple-element.12), channel_id=1, source_target_pairs={{0,4},{4,8},{8,12},{12,16},{16,20},{20,24},{24,28},{28,32},{32,36}... | collective-permute-start | bytes 196616 | tf_op jit(solution)/shard_map/ppermute | solution.py:21
  24.9 10.3 collective-permute-start
  27.2 0.7 copy-start.13
  27.9 0.8 copy-start.3
  35.3 0.8 copy-start
  108.9 14.2 %collective-permute-start.7 = (bf16[64,512]{1,0:T(8,128)(2,1)S(1)}, bf16[64,512]{1,0:T(8,128)(2,1)S(1)}, u32[]{:S(2)}, u32[]{:S(2)}) collective-permute-start(bf16[64,512]{1,0:T(8,128)(2,1)S(1)} %get-tuple-element.24), channel_id=1, source_target_pairs={{0,8},{4,12},{8,16},{12,20},{16,24},{20,28},{24,32},{28,36},{32,40... | collective-permute-start | bytes 196616 | tf_op jit(solution)/shard_map/ppermute | solution.py:21
  110.9 12.3 %collective-permute-start.6 = (bf16[64,512]{1,0:T(8,128)(2,1)S(1)}, bf16[64,512]{1,0:T(8,128)(2,1)S(1)}, u32[]{:S(2)}, u32[]{:S(2)}) collective-permute-start(bf16[64,512]{1,0:T(8,128)(2,1)S(1)} %get-tuple-element.25), channel_id=1, source_target_pairs={{0,4},{4,8},{8,12},{12,16},{16,20},{20,24},{24,28},{28,32},{32,36}... | collective-permute-start | bytes 196616 | tf_op jit(solution)/shard_map/ppermute | solution.py:21
  112.8 10.4 collective-permute-start.5
  115.3 9.2 collective-permute-start.4
  123.2 1.3 copy-start.8
  123.2 1.3 copy-start.9
  123.2 1.3 copy-start.10
  124.5 0.6 copy-start.11
  128.2 24.4 %collective-permute-start.11 = (bf16[64,512]{1,0:T(8,128)(2,1)}, bf16[64,512]{1,0:T(8,128)(2,1)S(1)}, u32[]{:S(2)}, u32[]{:S(2)}) collective-permute-start(bf16[64,512]{1,0:T(8,128)(2,1)} %get-tuple-element.16), channel_id=1, source_target_pairs={{0,504},{4,508},{8,0},{12,4},{16,8},{20,12},{24,16},{28,20},{32,24... | collective-permute-start | bytes 196616 | tf_op jit(solution)/shard_map/ppermute | solution.py:21
  136.1 16.5 %collective-permute-start.10 = (bf16[64,512]{1,0:T(8,128)(2,1)}, bf16[64,512]{1,0:T(8,128)(2,1)S(1)}, u32[]{:S(2)}, u32[]{:S(2)}) collective-permute-start(bf16[64,512]{1,0:T(8,128)(2,1)} %get-tuple-element.16), channel_id=1, source_target_pairs={{0,508},{4,0},{8,4},{12,8},{16,12},{20,16},{24,20},{28,24},{32,28}... | collective-permute-start | bytes 196616 | tf_op jit(solution)/shard_map/ppermute | solution.py:21
  141.2 11.4 collective-permute-start.9
  143.1 9.4 collective-permute-start.8
  152.6 0.8 copy-start.1
  226.3 15.3 %collective-permute-start.15 = (bf16[64,512]{1,0:T(8,128)(2,1)S(1)}, bf16[64,512]{1,0:T(8,128)(2,1)S(1)}, u32[]{:S(2)}, u32[]{:S(2)}) collective-permute-start(bf16[64,512]{1,0:T(8,128)(2,1)S(1)} %get-tuple-element.20), channel_id=1, source_target_pairs={{0,8},{4,12},{8,16},{12,20},{16,24},{20,28},{24,32},{28,36},{32,40... | collective-permute-start | bytes 196616 | tf_op jit(solution)/shard_map/ppermute | solution.py:21
  228.2 13.4 %collective-permute-start.14 = (bf16[64,512]{1,0:T(8,128)(2,1)S(1)}, bf16[64,512]{1,0:T(8,128)(2,1)S(1)}, u32[]{:S(2)}, u32[]{:S(2)}) collective-permute-start(bf16[64,512]{1,0:T(8,128)(2,1)S(1)} %get-tuple-element.21), channel_id=1, source_target_pairs={{0,4},{4,8},{8,12},{12,16},{16,20},{20,24},{24,28},{28,32},{32,36}... | collective-permute-start | bytes 196616 | tf_op jit(solution)/shard_map/ppermute | solution.py:21
  230.2 11.5 collective-permute-start.13
  233.7 9.2 collective-permute-start.12
  241.6 1.3 copy-start.4
  241.6 1.3 copy-start.5
  241.6 1.3 copy-start.6
  242.9 0.6 copy-start.7
Sparse Core Ops, SparseCore 0:
  275.5 938.2 all-reduce.1

commit v2 on v1

v2 whole, which is shorter than its diff:
```python
import jax
import jax.numpy as jnp
from jax import lax
from jax.experimental import pallas as pl
from jax.experimental.pallas import tpu as pltpu
from jax.sharding import Mesh
from jax.sharding import PartitionSpec as P

SPACE = ("outer", "quad")
QUAD = 4
OFFSETS = (-2, -1, 1, 2)
CENTER = 0.5
HALF = 6.0
TILE = 256
STEP = 2048
BF = jnp.bfloat16
F32 = jnp.float32


def selection(low, count):
    width = low.shape[1]
    lines = lax.broadcasted_iota(jnp.int32, (TILE, width), 0).astype(F32).astype(BF)
    place = (low % TILE).astype(F32)
    tiles = []
    for tile in range(count // TILE):
        here = jnp.where(low // TILE == tile, place, -1.0).astype(BF)
        tiles.append(jnp.where(lines == here, jnp.ones((), BF), jnp.zeros((), BF)))
    return jnp.concatenate(tiles, axis=0)


def picked(values, chosen):
    return jnp.dot(values, chosen, preferred_element_type=F32)


def put_back(values, chosen):
    return lax.dot_general(values, chosen, (((1,), (1,)), ((), ())), preferred_element_type=F32)


def from_pieces(values, piece, count):
    return jnp.concatenate([values[:, i * piece : (i + 1) * piece] for i in range(count)], axis=0)


def take_columns(values, index, piece):
    rows, count = values.shape[0], values.shape[1] // piece
    both = picked(from_pieces(values, piece, count), selection(index % piece, piece))
    part = index // piece
    result = both[:rows]
    for i in range(1, count):
        result = jnp.where(part == i, both[i * rows : (i + 1) * rows], result)
    return result


def add_columns(values, index, piece, count):
    rows = values.shape[0]
    part = index // piece
    none = jnp.zeros((), values.dtype)
    spread = jnp.concatenate([jnp.where(part == i, values, none) for i in range(count)], axis=0)
    sums = put_back(spread, selection(index % piece, piece))
    return [sums[i * rows : (i + 1) * rows] for i in range(count)]


def prepare_kernel(values, inv_root, boundary, scaled_ref, rim_ref):
    scaled = (inv_root[...] * values[...].astype(F32)).astype(BF)
    scaled_ref[...] = scaled
    rim_ref[...] = take_columns(scaled, boundary[...], boundary.shape[1]).astype(BF)


def cells_kernel(index, scale, kinetic, scaled, ghosts, own_ref, ghost_ref, table, acc):
    step = pl.program_id(0)
    count, rows, piece = ghosts.shape
    own_count = scaled.shape[1] // piece

    @pl.when(step == 0)
    def _():
        for i in range(own_count):
            table[i * rows : (i + 1) * rows] = scaled[:, i * piece : (i + 1) * piece]
        for i in range(count):
            table[(own_count + i) * rows : (own_count + i + 1) * rows] = ghosts[i]

    places = index[...]
    chosen = selection(places % piece, piece)
    part = places // piece
    both = picked(table[...], chosen)
    gathered = both[:rows]
    for i in range(1, own_count + count):
        gathered = jnp.where(part == i, both[i * rows : (i + 1) * rows], gathered)
    gathered = gathered.astype(BF)
    terms = jnp.concatenate(
        [
            jnp.dot(gathered[:, i : i + TILE], kinetic[...], preferred_element_type=F32)
            for i in range(0, gathered.shape[1], TILE)
        ],
        axis=1,
    )
    terms = terms * scale[...]
    spread = jnp.concatenate(
        [jnp.where(part == i, terms, 0.0).astype(BF) for i in range(own_count + count)], axis=0
    )
    sums = put_back(spread, chosen)

    @pl.when(step == 0)
    def _():
        acc[...] = sums

    @pl.when(step > 0)
    def _():
        acc[...] += sums

    @pl.when(step == pl.num_programs(0) - 1)
    def _():
        for i in range(own_count):
            own_ref[:, i * piece : (i + 1) * piece] = acc[i * rows : (i + 1) * rows]
        for i in range(count):
            ghost_ref[i] = acc[(own_count + i) * rows : (own_count + i + 1) * rows].astype(BF)


def cells(scaled, ghosts, index, scale, kinetic):
    rows, owned = scaled.shape
    count, _, piece = ghosts.shape
    places = index.shape[1]
    line = pl.BlockSpec((1, STEP), lambda i: (0, i))
    stack = (owned // piece + count) * rows
    return pl.pallas_call(
        cells_kernel,
        grid=(places // STEP,),
        in_specs=[
            line,
            line,
            pl.BlockSpec(kinetic.shape, lambda i: (0, 0)),
            pl.BlockSpec(scaled.shape, lambda i: (0, 0)),
            pl.BlockSpec(ghosts.shape, lambda i: (0, 0, 0)),
        ],
        out_specs=(
            pl.BlockSpec((rows, owned), lambda i: (0, 0)),
            pl.BlockSpec(ghosts.shape, lambda i: (0, 0, 0)),
        ),
        out_shape=(
            jax.ShapeDtypeStruct((rows, owned), F32),
            jax.ShapeDtypeStruct(ghosts.shape, BF),
        ),
        scratch_shapes=[pltpu.VMEM((stack, piece), BF), pltpu.VMEM((stack, piece), F32)],
        name="cells",
    )(index, scale, kinetic, scaled, ghosts)


def image_of(own, arrived, scaled, inv_root, potential, boundary):
    back = arrived[0].astype(F32)
    for i in range(1, arrived.shape[0]):
        back = back + arrived[i].astype(F32)
    upper = back.astype(BF)
    lower = (back - upper.astype(F32)).astype(BF)
    rows, piece = back.shape
    sums = add_columns(jnp.concatenate([upper, lower], axis=0), boundary[...], piece, own.shape[1] // piece)
    total = own[...] + jnp.concatenate([part[:rows] + part[rows:] for part in sums], axis=1)
    return inv_root[...] * (total + potential[...] * scaled[...].astype(F32))


def first_kernel(own, arrived, scaled, start, inv_root, potential, boundary, first_ref, scaled_ref, rim_ref):
    image = image_of(own, arrived, scaled, inv_root, potential, boundary)
    first = ((image - CENTER * start[...].astype(F32)) / HALF).astype(BF)
    first_ref[...] = first
    scaled_new = (inv_root[...] * first.astype(F32)).astype(BF)
    scaled_ref[...] = scaled_new
    rim_ref[...] = take_columns(scaled_new, boundary[...], boundary.shape[1]).astype(BF)


def second_kernel(own, arrived, scaled, start, first, inv_root, potential, boundary, out_ref):
    image = image_of(own, arrived, scaled, inv_root, potential, boundary)
    second = 2.0 * (image - CENTER * first[...].astype(F32)) / HALF - start[...].astype(F32)
    out_ref[...] = second.astype(BF)


def across(x):
    quads = lax.axis_size(SPACE[0])
    pairs = []
    for m in range(quads):
        for r in range(QUAD):
            other = (m + 1) % quads if r >= 2 else (m - 1) % quads
            pairs.append((m * QUAD + r, other * QUAD + (r + 2) % QUAD))
    return lax.ppermute(x, SPACE, pairs)


def exchange_out(rim):
    mine = lax.axis_index(SPACE[1])
    near = lax.all_gather(rim, SPACE[1], axis=0)
    edge = lax.dynamic_slice_in_dim(near, jnp.where(mine >= 2, 2, 0), 2, axis=0)
    far = across(edge)
    low = mine < 2
    line = jnp.concatenate([far, near, far], axis=0)
    parts = [lax.dynamic_index_in_dim(line, mine + 2 + offset, 0, keepdims=False) for offset in OFFSETS]
    return jnp.stack(parts)


def exchange_back(ghost):
    mine = lax.axis_index(SPACE[1])
    low = mine < 2
    direct = jnp.where(low, ghost[0], ghost[3])
    handed = jnp.where(mine == 0, ghost[1], jnp.where(mine == 3, ghost[2], jnp.zeros_like(direct)))
    arrived = across(jnp.stack([direct, handed]))
    zero = jnp.zeros_like(direct)
    blocks = []
    for member in range(QUAD):
        block = zero
        for i, offset in enumerate(OFFSETS):
            block = jnp.where(mine + offset == member, ghost[i], block)
        blocks.append(block)
    blocks = jnp.stack(blocks)
    extra = jnp.where(jnp.arange(QUAD)[:, None, None] == jnp.where(mine == 1, 0, jnp.where(mine == 2, 3, -1)), arrived[1][None], 0)
    blocks = (blocks.astype(F32) + extra.astype(F32)).astype(BF)
    near = lax.all_to_all(blocks, SPACE[1], 0, 0, tiled=True)
    return jnp.concatenate([near, arrived[:1]], axis=0)


def body(states_in, kinetic, cell_scale, cell_nodes, boundary, potential, inv_mass_root):
    nodes_per_cell = kinetic.shape[0]
    rows, owned = states_in.shape
    index = cell_nodes.T.reshape(1, -1)
    scale = jnp.repeat(cell_scale, nodes_per_cell).reshape(1, -1)
    stacked = jnp.kron(jnp.eye(TILE // nodes_per_cell, dtype=BF), kinetic.T)
    inv_root = inv_mass_root[None]
    potential = potential[None]
    boundary = boundary[None]
    width = boundary.shape[1]

    scaled, rim = pl.pallas_call(
        prepare_kernel,
        out_shape=(
            jax.ShapeDtypeStruct((rows, owned), BF),
            jax.ShapeDtypeStruct((rows, width), BF),
        ),
        name="prepare",
    )(states_in, inv_root, boundary)
    own, ghost = cells(scaled, exchange_out(rim), index, scale, stacked)
    first, scaled, rim = pl.pallas_call(
        first_kernel,
        out_shape=(
            jax.ShapeDtypeStruct((rows, owned), BF),
            jax.ShapeDtypeStruct((rows, owned), BF),
            jax.ShapeDtypeStruct((rows, width), BF),
        ),
        name="first",
    )(own, exchange_back(ghost), scaled, states_in, inv_root, potential, boundary)
    own, ghost = cells(scaled, exchange_out(rim), index, scale, stacked)
    filtered = pl.pallas_call(
        second_kernel,
        out_shape=jax.ShapeDtypeStruct((rows, owned), BF),
        name="second",
    )(own, exchange_back(ghost), scaled, states_in, first, inv_root, potential, boundary)

    bands = lax.axis_size("band")
    outer = lax.axis_size(SPACE[0])
    node_total = owned * outer * QUAD
    regrouped = lax.all_to_all(filtered, "band", split_axis=1, concat_axis=0, tiled=True)
    partial_sum = lax.dot_general(regrouped, regrouped, (((1,), (1,)), ((), ())), preferred_element_type=F32)
    states = partial_sum.shape[0]
    blocks = partial_sum.astype(BF).reshape(bands * QUAD, states // (bands * QUAD), states)
    sums = lax.all_to_all(blocks, ("band", SPACE[1]), 0, 0, tiled=True).astype(F32).sum(axis=0)
    spread = jnp.broadcast_to(sums.astype(BF)[None], (outer, *sums.shape))
    total = lax.all_to_all(spread, SPACE[0], 0, 0, tiled=True).astype(F32).sum(axis=0)
    margin = lax.all_gather(total / node_total, SPACE[1], axis=0, tiled=True)
    return filtered, margin


def solution(mesh):
    bands = mesh.shape["band"]
    split = Mesh(mesh.devices.reshape(-1, QUAD, bands), (*SPACE, "band"))
    in_specs = (P("band", SPACE), P(), P(SPACE), P(None, SPACE), P(SPACE), P(SPACE), P(SPACE))
    out_specs = (P("band", SPACE), P("band", None))
    return jax.shard_map(body, mesh=split, in_specs=in_specs, out_specs=out_specs, check_vma=False)
```

time: 1220 us -> 196 us (0.16)
  waiting for transfers between devices: 952 us -> 24.7 us
  Pallas kernels: 152 us -> 54.8 us
  blocking collectives: 26.9 us -> 90.2 us
  starting transfers between devices: 63.8 us -> 13.4 us
  between operations: 14.5 us -> 0.9 us
    psum x1 -> x0, waiting for transfers between devices: 938 us -> none  [body(): margin = lax.psum(reduced, SPACE) / node_total]
    pallas_call x3, Pallas kernels: 146 us -> 49.4 us  [the longest x2 47.5 us: cells(): pl.pallas_call(cells_kernel, grid=(places // STEP,), in_specs=[line, line...]
    ppermute x16 -> x4, starting transfers between devices: 63.8 us -> 13.4 us  [across(): return lax.ppermute(x, SPACE, pairs)]
    all_to_all x1 -> x4, blocking collectives: 9.82 us -> 49.8 us  [the longest x2 19.1 us: exchange_back(): near = lax.all_to_all(blocks, SPACE[1], 0, 0, tiled=True)]
    all_gather x0 -> x3, blocking collectives: none -> 26.6 us  [the longest x2 19.5 us: exchange_out(): near = lax.all_gather(rim, SPACE[1], axis=0)]
    ppermute x16 -> x4, waiting for transfers between devices: 13.7 us -> 24.7 us  [across(): return lax.ppermute(x, SPACE, pairs)]
  transfers between devices with their start and end apart: 17 -> 4, of which waited for: 5 -> 4; matrix products, arithmetic and copies ran while one was open for 0% -> 1% of each run, Pallas kernels for 0% -> 0%
where the time goes in v2:
time: 196 us; the launch traced here: 195 us
  blocking collectives  90.2 us (46%)
  Pallas kernels  54.8 us (28%)
  waiting for transfers between devices  24.7 us (13%)
  starting transfers between devices  13.4 us (7%)
  other arithmetic  5.75 us (3%)
  local copies, waits for them, and re-layouts  5.27 us (3%)
    pallas_call x2, Pallas kernels, cells(): pl.pallas_call(cells_kernel, grid=(places // STEP,), in_specs=[line, line...  47.5 us
    ppermute x4, waiting for transfers between devices, across(): return lax.ppermute(x, SPACE, pairs)  24.7 us
    all_gather x2, blocking collectives, exchange_out(): near = lax.all_gather(rim, SPACE[1], axis=0)  19.5 us
    all_to_all x2, blocking collectives, exchange_back(): near = lax.all_to_all(blocks, SPACE[1], 0, 0, tiled=True)  19.1 us
    all_to_all x1, blocking collectives, body(): lax.all_to_all(spread, SPACE[0], 0, 0, tiled=True).astype(F32).sum(axis=0)  15.8 us
    all_to_all x1, blocking collectives, body(): lax.all_to_all(blocks, ('band', SPACE[1]), 0, 0, tiled=True).astype(F32)  14.9 us
    all_to_all x1, blocking collectives, body(): lax.all_to_all(filtered, 'band', split_axis=1, concat_axis=0, tiled=True)  13.7 us
    ppermute x4, starting transfers between devices, across(): return lax.ppermute(x, SPACE, pairs)  13.4 us
  transfers between devices with their start and end apart: 4, of which 4 were waited for; matrix products, arithmetic and copies ran while one was open for 1% of the time, Pallas kernels for 0%

profile of v2, /device:TPU:1, one launch (start us, length us, event | category | flops | bytes accessed | tf_op | source)
XLA Modules:
  0.0 195.2 jit_solution(8071250510047173983)
XLA Ops:
  0.6 1.9 prepare.1
  2.6 12.6 %all-gather = bf16[256,512]{1,0:T(8,128)(2,1)S(1)} all-gather(bf16[64,512]{1,0:T(8,128)(2,1)} %get-tuple-element.12), channel_id=2, replica_groups=mesh['outer'=32,'quad'=4,'band'=4] {'quad'}, dimensions={0}, use_global_device_ids=true | all-gather | bytes 327680 | tf_op jit(solution)/shard_map/all_gather | solution.py:185
  15.2 0.0 copy-start.3
  15.2 3.8 %collective-permute-start = (bf16[2,64,512]{2,1,0:T(8,128)(2,1)S(1)}, bf16[2,64,512]{2,1,0:T(8,128)(2,1)S(1)}, u32[]{:S(2)}, u32[]{:S(2)}) collective-permute-start(bf16[2,64,512]{2,1,0:T(8,128)(2,1)S(1)} %constant_dynamic-slice_fusion.9), channel_id=1, source_target_pairs={{0,504},{4,508},{8,16},{12,20},{16,8},{20,12},{24,32},{28,36},{32,... | collective-permute-start | bytes 393224 | tf_op jit(solution)/shard_map/ppermute | solution.py:180
  19.0 0.0 copy-done.3
  19.0 0.1 copy.15
  19.1 0.2 broadcast_multiply_fusion
  19.3 0.0 copy-start.4
  19.4 0.7 copy-done.4
  20.0 0.1 broadcast_in_dim.57
  20.1 0.0 copy-start.2
  20.1 0.7 reshape_reshape.3.scale
  20.9 0.1 copy-done.2
  21.0 0.1 copy.14
  21.1 0.8 reshape.33.index
  21.8 0.9 mul.27.kinetic
  22.7 3.5 %collective-permute-done = bf16[2,64,512]{2,1,0:T(8,128)(2,1)S(1)} collective-permute-done((bf16[2,64,512]{2,1,0:T(8,128)(2,1)S(1)}, bf16[2,64,512]{2,1,0:T(8,128)(2,1)S(1)}, u32[]{:S(2)}, u32[]{:S(2)}) %collective-permute-start) | collective-permute-done | bytes 131104 | tf_op jit(solution)/shard_map/ppermute | solution.py:180
  26.2 0.1 pad_maximum_fusion
  26.3 0.7 pad_maximum_fusion.4.ghosts
  27.1 23.8 %cells.2 = (f32[64,2048]{1,0:T(8,128)}, bf16[4,64,512]{2,1,0:T(8,128)(2,1)}) custom-call(s32[1,16384]{1,0:T(1,128)} %reshape.33.index, f32[1,16384]{1,0:T(1,128)} %reshape_reshape.3.scale, bf16[256,256]{1,0:T(8,128)(2,1)} %mul.27.kinetic, bf16[64,2048]{1,0:T(8,128)(2,1)} %get-tuple-element.11.scaled, bf16[4,64,512]{2,1,0:T(8,128)(2,1)} %pad_maximum_fusion.4.ghosts), custom_call_target="tpu_custom_call" | custom-call | tf_op jit(solution)/shard_map/cells/pallas_call | solution.py:123
  50.8 0.0 copy-start.1
  50.9 1.0 select_select_fusion.8
  51.9 0.1 copy-done.1
  52.0 3.7 %collective-permute-start.1 = (bf16[2,64,512]{2,1,0:T(8,128)(2,1)S(1)}, bf16[2,64,512]{2,1,0:T(8,128)(2,1)S(1)}, u32[]{:S(2)}, u32[]{:S(2)}) collective-permute-start(bf16[2,64,512]{2,1,0:T(8,128)(2,1)S(1)} %pad_maximum_fusion.6), channel_id=1, source_target_pairs={{0,504},{4,508},{8,16},{12,20},{16,8},{20,12},{24,32},{28,36},{32,... | collective-permute-start | bytes 393224 | tf_op jit(solution)/shard_map/ppermute | solution.py:180
  55.8 6.2 %collective-permute-done.1 = bf16[2,64,512]{2,1,0:T(8,128)(2,1)S(1)} collective-permute-done((bf16[2,64,512]{2,1,0:T(8,128)(2,1)S(1)}, bf16[2,64,512]{2,1,0:T(8,128)(2,1)S(1)}, u32[]{:S(2)}, u32[]{:S(2)}) %collective-permute-start.1) | collective-permute-done | bytes 131104 | tf_op jit(solution)/shard_map/ppermute | solution.py:180
  61.9 0.1 add_convert_fusion.1
  62.1 9.5 %all_to_all.39 = bf16[4,64,512]{2,1,0:T(8,128)(2,1)S(1)} all-to-all(bf16[4,64,512]{2,1,0:T(8,128)(2,1)S(1)} %add_convert_fusion.1), channel_id=1, replica_groups=mesh['outer'=32,'quad'=4,'band'=4] {'quad'}, dimensions={0} | all-to-all | bytes 524288 | tf_op jit(solution)/shard_map/all_to_all | solution.py:210
  71.6 0.7 pad_maximum_fusion.2.arrived
  72.3 2.7 %first.1 = (bf16[64,2048]{1,0:T(8,128)(2,1)}, bf16[64,2048]{1,0:T(8,128)(2,1)}, bf16[64,512]{1,0:T(8,128)(2,1)}) custom-call(f32[64,2048]{1,0:T(8,128)} %get-tuple-element.13.own, bf16[5,64,512]{2,1,0:T(8,128)(2,1)} %pad_maximum_fusion.2.arrived, bf16[64,2048]{1,0:T(8,128)(2,1)} %get-tuple-element.11.scaled, bf16[64,2048]{1,0:T(8,128)(2,1)} %start.3, ...), custom_call_target="tpu_custom_call" | custom-call | tf_op jit(solution)/shard_map/first/pallas_call | solution.py:234
  75.1 6.8 %all-gather.1 = bf16[256,512]{1,0:T(8,128)(2,1)S(1)} all-gather(bf16[64,512]{1,0:T(8,128)(2,1)} %get-tuple-element.16), channel_id=3, replica_groups=mesh['outer'=32,'quad'=4,'band'=4] {'quad'}, dimensions={0}, use_global_device_ids=true | all-gather | bytes 327680 | tf_op jit(solution)/shard_map/all_gather | solution.py:185
  81.9 2.9 %collective-permute-start.2 = (bf16[2,64,512]{2,1,0:T(8,128)(2,1)S(1)}, bf16[2,64,512]{2,1,0:T(8,128)(2,1)S(1)}, u32[]{:S(2)}, u32[]{:S(2)}) collective-permute-start(bf16[2,64,512]{2,1,0:T(8,128)(2,1)S(1)} %constant_dynamic-slice_fusion.4), channel_id=1, source_target_pairs={{0,504},{4,508},{8,16},{12,20},{16,8},{20,12},{24,32},{28,36},{32,... | collective-permute-start | bytes 393224 | tf_op jit(solution)/shard_map/ppermute | solution.py:180
  84.9 8.1 %collective-permute-done.2 = bf16[2,64,512]{2,1,0:T(8,128)(2,1)S(1)} collective-permute-done((bf16[2,64,512]{2,1,0:T(8,128)(2,1)S(1)}, bf16[2,64,512]{2,1,0:T(8,128)(2,1)S(1)}, u32[]{:S(2)}, u32[]{:S(2)}) %collective-permute-start.2) | collective-permute-done | bytes 131104 | tf_op jit(solution)/shard_map/ppermute | solution.py:180
  92.9 0.1 pad_maximum_fusion.1
  93.0 0.7 pad_maximum_fusion.5.ghosts
  93.8 23.7 %cells.3 = (f32[64,2048]{1,0:T(8,128)}, bf16[4,64,512]{2,1,0:T(8,128)(2,1)}) custom-call(s32[1,16384]{1,0:T(1,128)} %reshape.33.index, f32[1,16384]{1,0:T(1,128)} %reshape_reshape.3.scale, bf16[256,256]{1,0:T(8,128)(2,1)} %mul.27.kinetic, bf16[64,2048]{1,0:T(8,128)(2,1)} %get-tuple-element.15.scaled, bf16[4,64,512]{2,1,0:T(8,128)(2,1)} %pad_maximum_fusion.5.ghosts), custom_call_target="tpu_custom_call" | custom-call | tf_op jit(solution)/shard_map/cells/pallas_call | solution.py:123
  117.5 0.0 copy-start
  117.5 1.0 select_select_fusion.3
  118.5 0.1 copy-done
  118.6 2.9 %collective-permute-start.3 = (bf16[2,64,512]{2,1,0:T(8,128)(2,1)S(1)}, bf16[2,64,512]{2,1,0:T(8,128)(2,1)S(1)}, u32[]{:S(2)}, u32[]{:S(2)}) collective-permute-start(bf16[2,64,512]{2,1,0:T(8,128)(2,1)S(1)} %pad_maximum_fusion.7), channel_id=1, source_target_pairs={{0,504},{4,508},{8,16},{12,20},{16,8},{20,12},{24,32},{28,36},{32,... | collective-permute-start | bytes 393224 | tf_op jit(solution)/shard_map/ppermute | solution.py:180
  121.6 7.0 %collective-permute-done.3 = bf16[2,64,512]{2,1,0:T(8,128)(2,1)S(1)} collective-permute-done((bf16[2,64,512]{2,1,0:T(8,128)(2,1)S(1)}, bf16[2,64,512]{2,1,0:T(8,128)(2,1)S(1)}, u32[]{:S(2)}, u32[]{:S(2)}) %collective-permute-start.3) | collective-permute-done | bytes 131104 | tf_op jit(solution)/shard_map/ppermute | solution.py:180
  128.6 0.1 add_convert_fusion
  128.7 9.6 %all_to_all.40 = bf16[4,64,512]{2,1,0:T(8,128)(2,1)S(1)} all-to-all(bf16[4,64,512]{2,1,0:T(8,128)(2,1)S(1)} %add_convert_fusion), channel_id=1, replica_groups=mesh['outer'=32,'quad'=4,'band'=4] {'quad'}, dimensions={0} | all-to-all | bytes 524288 | tf_op jit(solution)/shard_map/all_to_all | solution.py:210
  138.3 0.7 pad_maximum_fusion.3.arrived
  139.1 2.6 %second.1 = bf16[64,2048]{1,0:T(8,128)(2,1)} custom-call(f32[64,2048]{1,0:T(8,128)} %get-tuple-element.17.own, bf16[5,64,512]{2,1,0:T(8,128)(2,1)} %pad_maximum_fusion.3.arrived, bf16[64,2048]{1,0:T(8,128)(2,1)} %get-tuple-element.15.scaled, bf16[64,2048]{1,0:T(8,128)(2,1)} %start.3, bf16[64,2048]{1,0:T(8,128)(2,1)} %get-tuple-element.19.first, ...), custom_call_target="tpu_custom_call" | custom-call | tf_op jit(solution)/shard_map/second/pallas_call | solution.py:244
  141.7 1.0 copy.19
  142.7 13.7 %all_to_all.41 = bf16[64,4,512]{2,0,1:T(8,128)(2,1)S(1)} all-to-all(bf16[64,4,512]{2,0,1:T(8,128)(2,1)S(1)} %bitcast.26), channel_id=1, replica_groups=mesh['outer'=32,'quad'=4,'band'=4] {'band'}, dimensions={1} | all-to-all | bytes 524288 | tf_op jit(solution)/shard_map/all_to_all | solution.py:253
  156.4 0.3 convolution_convert_fusion
  156.7 14.9 %all_to_all.42 = bf16[16,16,256]{2,1,0:T(8,128)(2,1)S(1)} all-to-all(bf16[16,16,256]{2,1,0:T(8,128)(2,1)S(1)} %bitcast.28), channel_id=1, replica_groups=mesh['outer'=32,'quad'=4,'band'=4] {'band','quad'}, dimensions={0} | all-to-all | bytes 262144 | tf_op jit(solution)/shard_map/all_to_all | solution.py:257
  171.6 15.8 %all_to_all.43 = bf16[32,16,256]{2,1,0:T(8,128)(2,1)S(1)} all-to-all(bf16[32,16,256]{2,1,0:T(8,128)(2,1)S(1)} %broadcast_in_dim.67), channel_id=1, replica_groups=mesh['outer'=32,'quad'=4,'band'=4] {'outer'}, dimensions={0} | all-to-all | bytes 524288 | tf_op jit(solution)/shard_map/all_to_all | solution.py:259
  187.5 7.1 %all_gather.19 = f32[64,256]{1,0:T(8,128)S(1)} all-gather(f32[16,256]{1,0:T(8,128)S(1)} %broadcast_multiply_fusion.1), channel_id=1, replica_groups=mesh['outer'=32,'quad'=4,'band'=4] {'quad'}, dimensions={0}, use_global_device_ids=true | all-gather | bytes 81920 | tf_op jit(solution)/shard_map/all_gather | solution.py:260
  194.6 0.6 copy.21
  (18 shorter events, 0.3 us)
Async XLA Ops:
  15.2 3.8 %copy-start.3 = (bf16[64,64]{1,0:T(8,128)(2,1)S(1)}, bf16[64,64]{1,0:T(8,128)(2,1)}, u32[]{:S(2)}) copy-start(bf16[64,64]{1,0:T(8,128)(2,1)} %param.8) | copy-start | bytes 24580
  15.2 11.0 %collective-permute-start = (bf16[2,64,512]{2,1,0:T(8,128)(2,1)S(1)}, bf16[2,64,512]{2,1,0:T(8,128)(2,1)S(1)}, u32[]{:S(2)}, u32[]{:S(2)}) collective-permute-start(bf16[2,64,512]{2,1,0:T(8,128)(2,1)S(1)} %constant_dynamic-slice_fusion.9), channel_id=1, source_target_pairs={{0,504},{4,508},{8,16},{12,20},{16,8},{20,12},{24,32},{28,36},{32,... | collective-permute-start | bytes 393224 | tf_op jit(solution)/shard_map/ppermute | solution.py:180
  19.3 0.7 copy-start.4
  20.1 0.8 copy-start.2
  50.8 1.1 copy-start.1
  52.0 9.9 %collective-permute-start.1 = (bf16[2,64,512]{2,1,0:T(8,128)(2,1)S(1)}, bf16[2,64,512]{2,1,0:T(8,128)(2,1)S(1)}, u32[]{:S(2)}, u32[]{:S(2)}) collective-permute-start(bf16[2,64,512]{2,1,0:T(8,128)(2,1)S(1)} %pad_maximum_fusion.6), channel_id=1, source_target_pairs={{0,504},{4,508},{8,16},{12,20},{16,8},{20,12},{24,32},{28,36},{32,... | collective-permute-start | bytes 393224 | tf_op jit(solution)/shard_map/ppermute | solution.py:180
  81.9 11.0 %collective-permute-start.2 = (bf16[2,64,512]{2,1,0:T(8,128)(2,1)S(1)}, bf16[2,64,512]{2,1,0:T(8,128)(2,1)S(1)}, u32[]{:S(2)}, u32[]{:S(2)}) collective-permute-start(bf16[2,64,512]{2,1,0:T(8,128)(2,1)S(1)} %constant_dynamic-slice_fusion.4), channel_id=1, source_target_pairs={{0,504},{4,508},{8,16},{12,20},{16,8},{20,12},{24,32},{28,36},{32,... | collective-permute-start | bytes 393224 | tf_op jit(solution)/shard_map/ppermute | solution.py:180
  117.5 1.1 copy-start
  118.6 9.9 %collective-permute-start.3 = (bf16[2,64,512]{2,1,0:T(8,128)(2,1)S(1)}, bf16[2,64,512]{2,1,0:T(8,128)(2,1)S(1)}, u32[]{:S(2)}, u32[]{:S(2)}) collective-permute-start(bf16[2,64,512]{2,1,0:T(8,128)(2,1)S(1)} %pad_maximum_fusion.7), channel_id=1, source_target_pairs={{0,504},{4,508},{8,16},{12,20},{16,8},{20,12},{24,32},{28,36},{32,... | collective-permute-start | bytes 393224 | tf_op jit(solution)/shard_map/ppermute | solution.py:180

commit v3 on v2

v3 whole, which is shorter than its diff:
```python
import jax
import jax.numpy as jnp
from jax import lax
from jax.experimental import pallas as pl
from jax.experimental.pallas import tpu as pltpu
from jax.sharding import Mesh
from jax.sharding import PartitionSpec as P

SPACE = ("outer", "quad")
QUAD = 4
OFFSETS = (-2, -1, 1, 2)
CENTER = 0.5
HALF = 6.0
TILE = 256
STEP = 2048
BF = jnp.bfloat16
F32 = jnp.float32


def selection(low, count):
    width = low.shape[1]
    lines = lax.broadcasted_iota(jnp.int32, (TILE, width), 0).astype(F32).astype(BF)
    place = (low % TILE).astype(F32)
    tiles = []
    for tile in range(count // TILE):
        here = jnp.where(low // TILE == tile, place, -1.0).astype(BF)
        tiles.append(jnp.where(lines == here, jnp.ones((), BF), jnp.zeros((), BF)))
    return jnp.concatenate(tiles, axis=0)


def picked(values, chosen):
    return jnp.dot(values, chosen, preferred_element_type=F32)


def put_back(values, chosen):
    return lax.dot_general(values, chosen, (((1,), (1,)), ((), ())), preferred_element_type=F32)


def from_pieces(values, piece, count):
    return jnp.concatenate([values[:, i * piece : (i + 1) * piece] for i in range(count)], axis=0)


def take_columns(values, index, piece):
    rows, count = values.shape[0], values.shape[1] // piece
    both = picked(from_pieces(values, piece, count), selection(index % piece, piece))
    part = index // piece
    result = both[:rows]
    for i in range(1, count):
        result = jnp.where(part == i, both[i * rows : (i + 1) * rows], result)
    return result


def add_columns(values, index, piece, count):
    rows = values.shape[0]
    part = index // piece
    none = jnp.zeros((), values.dtype)
    spread = jnp.concatenate([jnp.where(part == i, values, none) for i in range(count)], axis=0)
    sums = put_back(spread, selection(index % piece, piece))
    return [sums[i * rows : (i + 1) * rows] for i in range(count)]


def prepare_kernel(values, inv_root, boundary, scaled_ref, rim_ref):
    scaled = (inv_root[...] * values[...].astype(F32)).astype(BF)
    scaled_ref[...] = scaled
    rim_ref[...] = take_columns(scaled, boundary[...], boundary.shape[1]).astype(BF)


def cells_kernel(mine, index, scale, kinetic, scaled, near, far, farther, own_ref, near_ref, far_ref, farther_ref, table, acc):
    step = pl.program_id(0)
    place = mine[0]
    rows, piece = far.shape
    own_count = scaled.shape[1] // piece
    count = own_count + len(OFFSETS)

    @pl.when(step == 0)
    def _():
        for i in range(own_count):
            table[i * rows : (i + 1) * rows] = scaled[:, i * piece : (i + 1) * piece]
        for i, offset in enumerate(OFFSETS):
            low = (own_count + i) * rows
            member = place + offset
            inside = jnp.logical_and(member >= 0, member < QUAD)

            @pl.when(inside)
            def _():
                table[low : low + rows] = near[jnp.clip(member, 0, QUAD - 1)]

            @pl.when(jnp.logical_not(inside))
            def _():
                table[low : low + rows] = (far if abs(offset) == 2 else farther)[...]

    places = index[...]
    chosen = selection(places % piece, piece)
    part = places // piece
    both = picked(table[...], chosen)
    gathered = both[:rows]
    for i in range(1, count):
        gathered = jnp.where(part == i, both[i * rows : (i + 1) * rows], gathered)
    gathered = gathered.astype(BF)
    terms = jnp.concatenate(
        [picked(gathered[:, i : i + TILE], kinetic[...]) for i in range(0, STEP, TILE)], axis=1
    )
    terms = terms * scale[...]
    spread = jnp.concatenate([jnp.where(part == i, terms, 0.0).astype(BF) for i in range(count)], axis=0)
    sums = put_back(spread, chosen)

    @pl.when(step == 0)
    def _():
        acc[...] = sums

    @pl.when(step > 0)
    def _():
        acc[...] += sums

    @pl.when(step == pl.num_programs(0) - 1)
    def _():
        def slot(i):
            return acc[(own_count + i) * rows : (own_count + i + 1) * rows].astype(BF)

        for i in range(own_count):
            own_ref[:, i * piece : (i + 1) * piece] = acc[i * rows : (i + 1) * rows]
        near_ref[...] = jnp.zeros_like(near_ref)
        for i, offset in enumerate(OFFSETS):
            member = place + offset

            @pl.when(jnp.logical_and(member >= 0, member < QUAD))
            def _():
                near_ref[jnp.clip(member, 0, QUAD - 1)] = slot(i)

        @pl.when(place < 2)
        def _():
            far_ref[...] = slot(0)
            farther_ref[...] = slot(1)

        @pl.when(place >= 2)
        def _():
            far_ref[...] = slot(3)
            farther_ref[...] = slot(2)


def cells(mine, scaled, ghosts, index, scale, kinetic):
    rows, owned = scaled.shape
    near, far, _ = ghosts
    piece = far.shape[1]
    places = index.shape[1]
    line = pl.BlockSpec((1, STEP), lambda i, mine: (0, i))

    def whole(shape):
        return pl.BlockSpec(shape, lambda i, mine: (0,) * len(shape))

    stack = (owned // piece + len(OFFSETS)) * rows
    blocks = [whole(near.shape), whole(far.shape), whole(far.shape)]
    own, *ghosts = pl.pallas_call(
        cells_kernel,
        grid_spec=pltpu.PrefetchScalarGridSpec(
            num_scalar_prefetch=1,
            grid=(places // STEP,),
            in_specs=[line, line, whole(kinetic.shape), whole(scaled.shape), *blocks],
            out_specs=[whole(scaled.shape), *blocks],
            scratch_shapes=[pltpu.VMEM((stack, piece), BF), pltpu.VMEM((stack, piece), F32)],
        ),
        out_shape=(
            jax.ShapeDtypeStruct((rows, owned), F32),
            jax.ShapeDtypeStruct(near.shape, BF),
            jax.ShapeDtypeStruct(far.shape, BF),
            jax.ShapeDtypeStruct(far.shape, BF),
        ),
        name="cells",
    )(mine, index, scale, kinetic, scaled, *ghosts)
    return own, ghosts


def image_of(own, near, far, farther, scaled, inv_root, potential, boundary):
    back = far[...].astype(F32) + farther[...].astype(F32)
    for i in range(QUAD):
        back = back + near[i].astype(F32)
    upper = back.astype(BF)
    lower = (back - upper.astype(F32)).astype(BF)
    rows, piece = back.shape
    sums = add_columns(jnp.concatenate([upper, lower], axis=0), boundary[...], piece, own.shape[1] // piece)
    total = own[...] + jnp.concatenate([part[:rows] + part[rows:] for part in sums], axis=1)
    return inv_root[...] * (total + potential[...] * scaled[...].astype(F32))


def first_kernel(own, near, far, farther, scaled, start, inv_root, potential, boundary, first_ref, scaled_ref, rim_ref):
    image = image_of(own, near, far, farther, scaled, inv_root, potential, boundary)
    first = ((image - CENTER * start[...].astype(F32)) / HALF).astype(BF)
    first_ref[...] = first
    scaled_new = (inv_root[...] * first.astype(F32)).astype(BF)
    scaled_ref[...] = scaled_new
    rim_ref[...] = take_columns(scaled_new, boundary[...], boundary.shape[1]).astype(BF)


def second_kernel(own, near, far, farther, scaled, start, first, inv_root, potential, boundary, out_ref, block_ref):
    image = image_of(own, near, far, farther, scaled, inv_root, potential, boundary)
    second = 2.0 * (image - CENTER * first[...].astype(F32)) / HALF - start[...].astype(F32)
    second = second.astype(BF)
    out_ref[...] = second
    width = block_ref.shape[2]
    for i in range(block_ref.shape[0]):
        block_ref[i] = second[:, i * width : (i + 1) * width]


def swapped(x, pairs):
    quads = lax.axis_size(SPACE[0])
    sends = []
    for m in range(quads):
        for here, there in pairs.items():
            ends = (m * QUAD + here, (m + 1) % quads * QUAD + there)
            sends += [ends, ends[::-1]]
    return lax.ppermute(x, SPACE, sends)


def both_across(far, farther):
    return swapped(far, {2: 0, 3: 1}), swapped(farther, {3: 0})


def exchange_out(rim):
    far, farther = both_across(rim, rim)
    return lax.all_gather(rim, SPACE[1], axis=0), far, farther


def exchange_back(near, far, farther):
    far, farther = both_across(far, farther)
    return lax.all_to_all(near, SPACE[1], 0, 0, tiled=True), far, farther


def body(states_in, kinetic, cell_scale, cell_nodes, boundary, potential, inv_mass_root):
    nodes_per_cell = kinetic.shape[0]
    rows, owned = states_in.shape
    index = cell_nodes.T.reshape(1, -1)
    scale = jnp.repeat(cell_scale, nodes_per_cell).reshape(1, -1)
    stacked = jnp.kron(jnp.eye(TILE // nodes_per_cell, dtype=BF), kinetic.T)
    inv_root = inv_mass_root[None]
    potential = potential[None]
    boundary = boundary[None]
    width = boundary.shape[1]
    bands = lax.axis_size("band")
    mine = lax.axis_index(SPACE[1])[None]

    scaled, rim = pl.pallas_call(
        prepare_kernel,
        out_shape=(
            jax.ShapeDtypeStruct((rows, owned), BF),
            jax.ShapeDtypeStruct((rows, width), BF),
        ),
        name="prepare",
    )(states_in, inv_root, boundary)
    own, ghost = cells(mine, scaled, exchange_out(rim), index, scale, stacked)
    first, scaled, rim = pl.pallas_call(
        first_kernel,
        out_shape=(
            jax.ShapeDtypeStruct((rows, owned), BF),
            jax.ShapeDtypeStruct((rows, owned), BF),
            jax.ShapeDtypeStruct((rows, width), BF),
        ),
        name="first",
    )(own, *exchange_back(*ghost), scaled, states_in, inv_root, potential, boundary)
    own, ghost = cells(mine, scaled, exchange_out(rim), index, scale, stacked)
    filtered, blocks = pl.pallas_call(
        second_kernel,
        out_shape=(
            jax.ShapeDtypeStruct((rows, owned), BF),
            jax.ShapeDtypeStruct((bands, rows, owned // bands), BF),
        ),
        name="second",
    )(own, *exchange_back(*ghost), scaled, states_in, first, inv_root, potential, boundary)

    outer = lax.axis_size(SPACE[0])
    node_total = owned * outer * QUAD
    regrouped = lax.all_to_all(blocks, "band", 0, 0, tiled=True).reshape(bands * rows, -1)
    partial_sum = lax.dot_general(regrouped, regrouped, (((1,), (1,)), ((), ())), preferred_element_type=F32)
    states = partial_sum.shape[0]
    blocks = partial_sum.astype(BF).reshape(bands * QUAD, states // (bands * QUAD), states)
    sums = lax.all_to_all(blocks, ("band", SPACE[1]), 0, 0, tiled=True).astype(F32).sum(axis=0)
    spread = jnp.broadcast_to(sums.astype(BF)[None], (outer, *sums.shape))
    total = lax.all_to_all(spread, SPACE[0], 0, 0, tiled=True).astype(F32).sum(axis=0)
    margin = lax.all_gather(total / node_total, SPACE[1], axis=0, tiled=True)
    return filtered, margin


def solution(mesh):
    bands = mesh.shape["band"]
    split = Mesh(mesh.devices.reshape(-1, QUAD, bands), (*SPACE, "band"))
    in_specs = (P("band", SPACE), P(), P(SPACE), P(None, SPACE), P(SPACE), P(SPACE), P(SPACE))
    out_specs = (P("band", SPACE), P("band", None))
    return jax.shard_map(body, mesh=split, in_specs=in_specs, out_specs=out_specs, check_vma=False)
```

time: 196 us -> 189 us (0.964)
  starting transfers between devices: 13.4 us -> 51.4 us
  blocking collectives: 90.2 us -> 66.6 us
  waiting for transfers between devices: 24.7 us -> 6.75 us
  other arithmetic: 5.75 us -> 0.25 us
    ppermute x4 -> x8, starting transfers between devices: 13.4 us -> 43.7 us  [swapped(): return lax.ppermute(x, SPACE, sends)]
    ppermute x4 -> x8, waiting for transfers between devices: 24.7 us -> 6.75 us  [swapped(): return lax.ppermute(x, SPACE, sends)]
    all_to_all x3 -> x1, blocking collectives: 32.8 us -> 17.4 us  [body(): lax.all_to_all(blocks, 'band', 0, 0, tiled=True).reshape(bands * rows, -1)]
    all_gather x2, blocking collectives: 19.5 us -> 10.5 us  [exchange_out(): return (lax.all_gather(rim, SPACE[1], axis=0), far, farther)]
    all_to_all x0 -> x2, starting transfers between devices: none -> 7.69 us  [exchange_back(): return (lax.all_to_all(near, SPACE[1], 0, 0, tiled=True), far, farther)]
    all_to_all x1, blocking collectives: 14.9 us -> 18.3 us  [body(): lax.all_to_all(blocks, ('band', SPACE[1]), 0, 0, tiled=True).astype(F32)]
    unnamed x11 -> x37, local copies, waits for them, and re-layouts: 1.55 us -> 4.03 us
    select_n x6 -> x0, other arithmetic: 2.08 us -> none  [exchange_back(): block = jnp.where(mine + offset == member, ghost[i], block)]
  transfers between devices with their start and end apart: 4 -> 10, of which waited for: 4 -> 2; matrix products, arithmetic and copies ran while one was open for 1% -> 1% of each run, Pallas kernels for 0% -> 0%
where the time goes in v3:
time: 189 us; the launch traced here: 188 us
  blocking collectives  66.6 us (35%)
  Pallas kernels  55.4 us (29%)
  starting transfers between devices  51.4 us (27%)
  waiting for transfers between devices  6.75 us (4%)
  local copies, waits for them, and re-layouts  6.69 us (4%)
    pallas_call x2, Pallas kernels, cells(): pl.pallas_call(cells_kernel, grid_spec=pltpu.PrefetchScalarGridSpec(num_s...  48 us
    ppermute x8, starting transfers between devices, swapped(): return lax.ppermute(x, SPACE, sends)  43.7 us
    all_to_all x1, blocking collectives, body(): lax.all_to_all(blocks, ('band', SPACE[1]), 0, 0, tiled=True).astype(F32)  18.3 us
    all_to_all x1, blocking collectives, body(): lax.all_to_all(blocks, 'band', 0, 0, tiled=True).reshape(bands * rows, -1)  17.4 us
    all_to_all x1, blocking collectives, body(): lax.all_to_all(spread, SPACE[0], 0, 0, tiled=True).astype(F32).sum(axis=0)  14.4 us
    all_gather x2, blocking collectives, exchange_out(): return (lax.all_gather(rim, SPACE[1], axis=0), far, farther)  10.5 us
    all_to_all x2, starting transfers between devices, exchange_back(): return (lax.all_to_all(near, SPACE[1], 0, 0, tiled=True), far, farther)  7.69 us
    ppermute x8, waiting for transfers between devices, swapped(): return lax.ppermute(x, SPACE, sends)  6.75 us
  transfers between devices with their start and end apart: 10, of which 2 were waited for; matrix products, arithmetic and copies ran while one was open for 1% of the time, Pallas kernels for 0%

profile of v3, /device:TPU:1, one launch (start us, length us, event | category | flops | bytes accessed | tf_op | source)
XLA Modules:
  0.0 188.3 jit_solution(8897136144862218053)
XLA Ops:
  0.6 0.0 copy-start.12
  0.6 1.9 %prepare.1 = (bf16[64,2048]{1,0:T(8,128)(2,1)}, bf16[64,512]{1,0:T(8,128)(2,1)}) custom-call(bf16[64,2048]{1,0:T(8,128)(2,1)} %start.3, f32[1,2048]{1,0:T(1,128)} %bitcast.16, s32[1,512]{1,0:T(1,128)} %bitcast.22), custom_call_target="tpu_custom_call" | custom-call | tf_op jit(solution)/shard_map/prepare/pallas_call | solution.py:241
  2.6 0.7 collective-permute-start.1
  3.2 15.6 %collective-permute-start = (bf16[64,512]{1,0:T(8,128)(2,1)}, bf16[64,512]{1,0:T(8,128)(2,1)S(1)}, u32[]{:S(2)}, u32[]{:S(2)}) collective-permute-start(bf16[64,512]{1,0:T(8,128)(2,1)} %get-tuple-element.18), channel_id=1, source_target_pairs={{8,16},{16,8},{12,20},{20,12},{24,32},{32,24},{28,36},{36,28},{40,... | collective-permute-start | bytes 196616 | tf_op jit(solution)/shard_map/ppermute | solution.py:211
  18.8 0.0 copy-done.12
  18.8 0.0 copy-start.13
  18.8 0.1 copy.14
  18.9 0.6 copy-done.13
  19.5 0.1 broadcast_in_dim.26
  19.6 0.0 copy-start.2
  19.6 0.7 reshape_reshape.3.scale
  20.4 0.1 copy-done.2
  20.4 0.1 copy.13
  20.5 0.8 reshape.28.index
  21.3 0.2 broadcast_multiply_fusion
  21.5 0.0 copy-start.5
  21.5 0.9 mul.27.kinetic
  22.3 0.0 copy-done.5
  22.3 5.1 %all-gather = bf16[256,512]{1,0:T(8,128)(2,1)} all-gather(bf16[64,512]{1,0:T(8,128)(2,1)S(1)} %copy-done.5), channel_id=2, replica_groups=mesh['outer'=32,'quad'=4,'band'=4] {'quad'}, dimensions={0}, use_global_device_ids=true | all-gather | bytes 327680 | tf_op jit(solution)/shard_map/all_gather | solution.py:220
  27.4 0.0 collective-permute-done.1.farther
  27.4 0.0 collective-permute-done.far
  27.4 0.0 copy-start.4
  27.4 0.6 copy-done.3
  28.0 0.0 copy-done.4
  28.0 24.0 %cells.2 = (f32[64,2048]{1,0:T(8,128)}, bf16[4,64,512]{2,1,0:T(8,128)(2,1)}, bf16[64,512]{1,0:T(8,128)(2,1)}, bf16[64,512]{1,0:T(8,128)(2,1)}) custom-call(s32[1]{0:T(128)} %bitcast.mine, s32[1,16384]{1,0:T(1,128)} %reshape.28.index, f32[1,16384]{1,0:T(1,128)} %reshape_reshape.3.scale, bf16[256,256]{1,0:T(8,128)(2,1)} %mul.27.kinetic, ...), custom_call_target="tpu_custom_call" | custom-call | tf_op jit(solution)/shard_map/cells/pallas_call | solution.py:153
  52.0 3.8 %all-to-all-start = ((bf16[4,64,512]{2,1,0:T(8,128)(2,1)}), bf16[4,64,512]{2,1,0:T(8,128)(2,1)S(1)}, u32[]{:S(2)}, u32[]{:S(2)}) async-start(bf16[4,64,512]{2,1,0:T(8,128)(2,1)} %get-tuple-element.20), calls=%async_computation | async-start | bytes 524288 | tf_op jit(solution)/shard_map/all_to_all | solution.py:225
  55.9 0.0 copy-done.17
  55.9 4.8 %collective-permute-start.2 = (bf16[64,512]{1,0:T(8,128)(2,1)S(1)}, bf16[64,512]{1,0:T(8,128)(2,1)S(1)}, u32[]{:S(2)}, u32[]{:S(2)}) collective-permute-start(bf16[64,512]{1,0:T(8,128)(2,1)S(1)} %copy-done.17), channel_id=1, source_target_pairs={{8,16},{16,8},{12,20},{20,12},{24,32},{32,24},{28,36},{36,28},{40,... | collective-permute-start | bytes 196616 | tf_op jit(solution)/shard_map/ppermute | solution.py:211
  60.7 0.0 copy-done.16
  60.7 0.7 collective-permute-start.3
  61.4 4.2 %collective-permute-done.2.far = bf16[64,512]{1,0:T(8,128)(2,1)S(1)} collective-permute-done((bf16[64,512]{1,0:T(8,128)(2,1)S(1)}, bf16[64,512]{1,0:T(8,128)(2,1)S(1)}, u32[]{:S(2)}, u32[]{:S(2)}) %collective-permute-start.2) | collective-permute-done | bytes 65568 | tf_op jit(solution)/shard_map/ppermute | solution.py:211
  65.6 0.0 collective-permute-done.3.farther
  65.6 0.0 all-to-all-done.near
  65.6 0.0 copy-start.1
  65.6 0.6 copy-done.6
  66.2 0.0 copy-done.7
  66.2 0.1 copy-done.1
  66.3 2.8 %first.1 = (bf16[64,2048]{1,0:T(8,128)(2,1)}, bf16[64,2048]{1,0:T(8,128)(2,1)}, bf16[64,512]{1,0:T(8,128)(2,1)}) custom-call(f32[64,2048]{1,0:T(8,128)} %get-tuple-element.19.own, bf16[4,64,512]{2,1,0:T(8,128)(2,1)} %copy-done.1, bf16[64,512]{1,0:T(8,128)(2,1)} %copy-done.6, bf16[64,512]{1,0:T(8,128)(2,1)} %copy-done.7, ...), custom_call_target="tpu_custom_call" | custom-call | tf_op jit(solution)/shard_map/first/pallas_call | solution.py:250
  69.1 0.7 collective-permute-start.5
  69.8 14.3 %collective-permute-start.4 = (bf16[64,512]{1,0:T(8,128)(2,1)}, bf16[64,512]{1,0:T(8,128)(2,1)S(1)}, u32[]{:S(2)}, u32[]{:S(2)}) collective-permute-start(bf16[64,512]{1,0:T(8,128)(2,1)} %get-tuple-element.24), channel_id=1, source_target_pairs={{8,16},{16,8},{12,20},{20,12},{24,32},{32,24},{28,36},{36,28},{40,... | collective-permute-start | bytes 196616 | tf_op jit(solution)/shard_map/ppermute | solution.py:211
  84.0 5.5 %all-gather.1 = bf16[256,512]{1,0:T(8,128)(2,1)} all-gather(bf16[64,512]{1,0:T(8,128)(2,1)} %get-tuple-element.24), channel_id=3, replica_groups=mesh['outer'=32,'quad'=4,'band'=4] {'quad'}, dimensions={0}, use_global_device_ids=true | all-gather | bytes 327680 | tf_op jit(solution)/shard_map/all_gather | solution.py:220
  89.5 0.0 collective-permute-done.5.farther
  89.5 0.0 collective-permute-done.4.far
  89.5 0.6 copy-done.8
  90.1 0.0 copy-done.9
  90.1 24.0 %cells.3 = (f32[64,2048]{1,0:T(8,128)}, bf16[4,64,512]{2,1,0:T(8,128)(2,1)}, bf16[64,512]{1,0:T(8,128)(2,1)}, bf16[64,512]{1,0:T(8,128)(2,1)}) custom-call(s32[1]{0:T(128)} %bitcast.mine, s32[1,16384]{1,0:T(1,128)} %reshape.28.index, f32[1,16384]{1,0:T(1,128)} %reshape_reshape.3.scale, bf16[256,256]{1,0:T(8,128)(2,1)} %mul.27.kinetic, ...), custom_call_target="tpu_custom_call" | custom-call | tf_op jit(solution)/shard_map/cells/pallas_call | solution.py:153
  114.1 0.0 copy-start.14
  114.1 3.8 %all-to-all-start.1 = ((bf16[4,64,512]{2,1,0:T(8,128)(2,1)}), bf16[4,64,512]{2,1,0:T(8,128)(2,1)S(1)}, u32[]{:S(2)}, u32[]{:S(2)}) async-start(bf16[4,64,512]{2,1,0:T(8,128)(2,1)} %get-tuple-element.26), calls=%async_computation.1 | async-start | bytes 524288 | tf_op jit(solution)/shard_map/all_to_all | solution.py:225
  118.0 0.0 copy-done.15
  118.0 6.5 %collective-permute-start.6 = (bf16[64,512]{1,0:T(8,128)(2,1)S(1)}, bf16[64,512]{1,0:T(8,128)(2,1)S(1)}, u32[]{:S(2)}, u32[]{:S(2)}) collective-permute-start(bf16[64,512]{1,0:T(8,128)(2,1)S(1)} %copy-done.15), channel_id=1, source_target_pairs={{8,16},{16,8},{12,20},{20,12},{24,32},{32,24},{28,36},{36,28},{40,... | collective-permute-start | bytes 196616 | tf_op jit(solution)/shard_map/ppermute | solution.py:211
  124.5 0.7 collective-permute-start.7
  125.2 2.5 %collective-permute-done.6.far = bf16[64,512]{1,0:T(8,128)(2,1)S(1)} collective-permute-done((bf16[64,512]{1,0:T(8,128)(2,1)S(1)}, bf16[64,512]{1,0:T(8,128)(2,1)S(1)}, u32[]{:S(2)}, u32[]{:S(2)}) %collective-permute-start.6) | collective-permute-done | bytes 65568 | tf_op jit(solution)/shard_map/ppermute | solution.py:211
  127.7 0.0 collective-permute-done.7.farther
  127.7 0.0 all-to-all-done.1.near
  127.7 0.6 copy-done.10
  128.3 0.0 copy-done.11
  128.3 0.1 copy-done
  128.4 2.8 %second.1 = (bf16[64,2048]{1,0:T(8,128)(2,1)}, bf16[4,64,512]{2,1,0:T(8,128)(2,1)}) custom-call(f32[64,2048]{1,0:T(8,128)} %get-tuple-element.25.own, bf16[4,64,512]{2,1,0:T(8,128)(2,1)} %copy-done, bf16[64,512]{1,0:T(8,128)(2,1)} %copy-done.10, bf16[64,512]{1,0:T(8,128)(2,1)} %copy-done.11, bf16[64,2048]{1,0:T(8,128)(2,1)} %get-tuple-element.23.scaled, ...), custom_call_target="tpu_custom_call" | custom-call | tf_op jit(solution)/shard_map/second/pallas_call | solution.py:260
  131.2 17.4 %all_to_all.25 = bf16[4,64,512]{2,1,0:T(8,128)(2,1)S(1)} all-to-all(bf16[4,64,512]{2,1,0:T(8,128)(2,1)} %get-tuple-element.31), channel_id=1, replica_groups=mesh['outer'=32,'quad'=4,'band'=4] {'band'}, dimensions={0} | all-to-all | bytes 524288 | tf_op jit(solution)/shard_map/all_to_all | solution.py:271
  148.5 0.3 convolution_convert_fusion
  148.8 18.3 %all_to_all.26 = bf16[16,16,256]{2,1,0:T(8,128)(2,1)S(1)} all-to-all(bf16[16,16,256]{2,1,0:T(8,128)(2,1)S(1)} %bitcast.15), channel_id=1, replica_groups=mesh['outer'=32,'quad'=4,'band'=4] {'band','quad'}, dimensions={0} | all-to-all | bytes 262144 | tf_op jit(solution)/shard_map/all_to_all | solution.py:275
  167.2 14.4 %all_to_all.27 = bf16[32,16,256]{2,1,0:T(8,128)(2,1)S(1)} all-to-all(bf16[32,16,256]{2,1,0:T(8,128)(2,1)S(1)} %broadcast_in_dim.30), channel_id=1, replica_groups=mesh['outer'=32,'quad'=4,'band'=4] {'outer'}, dimensions={0} | all-to-all | bytes 524288 | tf_op jit(solution)/shard_map/all_to_all | solution.py:277
  181.7 6.0 %all_gather.19 = f32[64,256]{1,0:T(8,128)S(1)} all-gather(f32[16,256]{1,0:T(8,128)S(1)} %broadcast_multiply_fusion.1), channel_id=1, replica_groups=mesh['outer'=32,'quad'=4,'band'=4] {'quad'}, dimensions={0}, use_global_device_ids=true | all-gather | bytes 81920 | tf_op jit(solution)/shard_map/all_gather | solution.py:278
  187.7 0.6 copy.16
  (17 shorter events, 0.1 us)
Async XLA Ops:
  0.6 18.2 %copy-start.12 = (bf16[64,64]{1,0:T(8,128)(2,1)S(1)}, bf16[64,64]{1,0:T(8,128)(2,1)}, u32[]{:S(2)}) copy-start(bf16[64,64]{1,0:T(8,128)(2,1)} %param.8) | copy-start | bytes 24580
  2.6 24.8 %collective-permute-start.1 = (bf16[64,512]{1,0:T(8,128)(2,1)}, bf16[64,512]{1,0:T(8,128)(2,1)S(1)}, u32[]{:S(2)}, u32[]{:S(2)}) collective-permute-start(bf16[64,512]{1,0:T(8,128)(2,1)} %get-tuple-element.18), channel_id=1, source_target_pairs={{12,16},{16,12},{28,32},{32,28},{44,48},{48,44},{60,64},{64,60},{7... | collective-permute-start | bytes 196616 | tf_op jit(solution)/shard_map/ppermute | solution.py:211
  3.2 24.2 %collective-permute-start = (bf16[64,512]{1,0:T(8,128)(2,1)}, bf16[64,512]{1,0:T(8,128)(2,1)S(1)}, u32[]{:S(2)}, u32[]{:S(2)}) collective-permute-start(bf16[64,512]{1,0:T(8,128)(2,1)} %get-tuple-element.18), channel_id=1, source_target_pairs={{8,16},{16,8},{12,20},{20,12},{24,32},{32,24},{28,36},{36,28},{40,... | collective-permute-start | bytes 196616 | tf_op jit(solution)/shard_map/ppermute | solution.py:211
  18.8 0.7 copy-start.13
  19.6 0.8 copy-start.2
  21.5 0.9 copy-start.5
  27.4 0.6 copy-start.3
  27.4 0.6 copy-start.4
  52.0 3.9 %copy-start.17 = (bf16[64,512]{1,0:T(8,128)(2,1)S(1)}, bf16[64,512]{1,0:T(8,128)(2,1)}, u32[]{:S(2)}) copy-start(bf16[64,512]{1,0:T(8,128)(2,1)} %get-tuple-element.21) | copy-start | bytes 196612
  52.0 8.6 %copy-start.16 = (bf16[64,512]{1,0:T(8,128)(2,1)S(1)}, bf16[64,512]{1,0:T(8,128)(2,1)}, u32[]{:S(2)}) copy-start(bf16[64,512]{1,0:T(8,128)(2,1)} %get-tuple-element.22) | copy-start | bytes 196612
  52.0 13.6 %all-to-all-start = ((bf16[4,64,512]{2,1,0:T(8,128)(2,1)}), bf16[4,64,512]{2,1,0:T(8,128)(2,1)S(1)}, u32[]{:S(2)}, u32[]{:S(2)}) async-start(bf16[4,64,512]{2,1,0:T(8,128)(2,1)} %get-tuple-element.20), calls=%async_computation | async-start | bytes 524288 | tf_op jit(solution)/shard_map/all_to_all | solution.py:225
  55.9 9.7 %collective-permute-start.2 = (bf16[64,512]{1,0:T(8,128)(2,1)S(1)}, bf16[64,512]{1,0:T(8,128)(2,1)S(1)}, u32[]{:S(2)}, u32[]{:S(2)}) collective-permute-start(bf16[64,512]{1,0:T(8,128)(2,1)S(1)} %copy-done.17), channel_id=1, source_target_pairs={{8,16},{16,8},{12,20},{20,12},{24,32},{32,24},{28,36},{36,28},{40,... | collective-permute-start | bytes 196616 | tf_op jit(solution)/shard_map/ppermute | solution.py:211
  60.7 4.9 %collective-permute-start.3 = (bf16[64,512]{1,0:T(8,128)(2,1)S(1)}, bf16[64,512]{1,0:T(8,128)(2,1)S(1)}, u32[]{:S(2)}, u32[]{:S(2)}) collective-permute-start(bf16[64,512]{1,0:T(8,128)(2,1)S(1)} %copy-done.16), channel_id=1, source_target_pairs={{12,16},{16,12},{28,32},{32,28},{44,48},{48,44},{60,64},{64,60},{7... | collective-permute-start | bytes 196616 | tf_op jit(solution)/shard_map/ppermute | solution.py:211
  65.6 0.6 copy-start.6
  65.6 0.6 copy-start.7
  65.6 0.7 copy-start.1
  69.1 20.4 %collective-permute-start.5 = (bf16[64,512]{1,0:T(8,128)(2,1)}, bf16[64,512]{1,0:T(8,128)(2,1)S(1)}, u32[]{:S(2)}, u32[]{:S(2)}) collective-permute-start(bf16[64,512]{1,0:T(8,128)(2,1)} %get-tuple-element.24), channel_id=1, source_target_pairs={{12,16},{16,12},{28,32},{32,28},{44,48},{48,44},{60,64},{64,60},{7... | collective-permute-start | bytes 196616 | tf_op jit(solution)/shard_map/ppermute | solution.py:211
  69.8 19.8 %collective-permute-start.4 = (bf16[64,512]{1,0:T(8,128)(2,1)}, bf16[64,512]{1,0:T(8,128)(2,1)S(1)}, u32[]{:S(2)}, u32[]{:S(2)}) collective-permute-start(bf16[64,512]{1,0:T(8,128)(2,1)} %get-tuple-element.24), channel_id=1, source_target_pairs={{8,16},{16,8},{12,20},{20,12},{24,32},{32,24},{28,36},{36,28},{40,... | collective-permute-start | bytes 196616 | tf_op jit(solution)/shard_map/ppermute | solution.py:211
  89.5 0.6 copy-start.8
  89.5 0.6 copy-start.9
  114.1 3.9 %copy-start.15 = (bf16[64,512]{1,0:T(8,128)(2,1)S(1)}, bf16[64,512]{1,0:T(8,128)(2,1)}, u32[]{:S(2)}) copy-start(bf16[64,512]{1,0:T(8,128)(2,1)} %get-tuple-element.27) | copy-start | bytes 196612
  114.1 10.4 %copy-start.14 = (bf16[64,512]{1,0:T(8,128)(2,1)S(1)}, bf16[64,512]{1,0:T(8,128)(2,1)}, u32[]{:S(2)}) copy-start(bf16[64,512]{1,0:T(8,128)(2,1)} %get-tuple-element.28) | copy-start | bytes 196612
  114.1 13.6 %all-to-all-start.1 = ((bf16[4,64,512]{2,1,0:T(8,128)(2,1)}), bf16[4,64,512]{2,1,0:T(8,128)(2,1)S(1)}, u32[]{:S(2)}, u32[]{:S(2)}) async-start(bf16[4,64,512]{2,1,0:T(8,128)(2,1)} %get-tuple-element.26), calls=%async_computation.1 | async-start | bytes 524288 | tf_op jit(solution)/shard_map/all_to_all | solution.py:225
  118.0 9.7 %collective-permute-start.6 = (bf16[64,512]{1,0:T(8,128)(2,1)S(1)}, bf16[64,512]{1,0:T(8,128)(2,1)S(1)}, u32[]{:S(2)}, u32[]{:S(2)}) collective-permute-start(bf16[64,512]{1,0:T(8,128)(2,1)S(1)} %copy-done.15), channel_id=1, source_target_pairs={{8,16},{16,8},{12,20},{20,12},{24,32},{32,24},{28,36},{36,28},{40,... | collective-permute-start | bytes 196616 | tf_op jit(solution)/shard_map/ppermute | solution.py:211
  124.5 3.2 %collective-permute-start.7 = (bf16[64,512]{1,0:T(8,128)(2,1)S(1)}, bf16[64,512]{1,0:T(8,128)(2,1)S(1)}, u32[]{:S(2)}, u32[]{:S(2)}) collective-permute-start(bf16[64,512]{1,0:T(8,128)(2,1)S(1)} %copy-done.14), channel_id=1, source_target_pairs={{12,16},{16,12},{28,32},{32,28},{44,48},{48,44},{60,64},{64,60},{7... | collective-permute-start | bytes 196616 | tf_op jit(solution)/shard_map/ppermute | solution.py:211
  127.7 0.6 copy-start.10
  127.7 0.6 copy-start.11
  127.7 0.7 copy-start

commit v4 on v3

v4 whole, which is shorter than its diff:
```python
import jax
import jax.numpy as jnp
from jax import lax
from jax.experimental import pallas as pl
from jax.experimental.pallas import tpu as pltpu
from jax.sharding import Mesh
from jax.sharding import PartitionSpec as P

SPACE = ("outer", "quad")
QUAD = 4
OFFSETS = (-2, -1, 1, 2)
CENTER = 0.5
HALF = 6.0
TILE = 256
STEP = 2048
BF = jnp.bfloat16
F32 = jnp.float32


def selection(low, count):
    width = low.shape[1]
    lines = lax.broadcasted_iota(jnp.int32, (TILE, width), 0).astype(F32).astype(BF)
    place = (low % TILE).astype(F32)
    tiles = []
    for tile in range(count // TILE):
        here = jnp.where(low // TILE == tile, place, -1.0).astype(BF)
        tiles.append(jnp.where(lines == here, jnp.ones((), BF), jnp.zeros((), BF)))
    return jnp.concatenate(tiles, axis=0)


def picked(values, chosen):
    return jnp.dot(values, chosen, preferred_element_type=F32)


def put_back(values, chosen):
    return lax.dot_general(values, chosen, (((1,), (1,)), ((), ())), preferred_element_type=F32)


def from_pieces(values, piece, count):
    return jnp.concatenate([values[:, i * piece : (i + 1) * piece] for i in range(count)], axis=0)


def take_columns(values, index, piece):
    rows, count = values.shape[0], values.shape[1] // piece
    both = picked(from_pieces(values, piece, count), selection(index % piece, piece))
    part = index // piece
    result = both[:rows]
    for i in range(1, count):
        result = jnp.where(part == i, both[i * rows : (i + 1) * rows], result)
    return result


def add_columns(values, index, piece, count):
    rows = values.shape[0]
    part = index // piece
    none = jnp.zeros((), values.dtype)
    spread = jnp.concatenate([jnp.where(part == i, values, none) for i in range(count)], axis=0)
    sums = put_back(spread, selection(index % piece, piece))
    return [sums[i * rows : (i + 1) * rows] for i in range(count)]


def prepare_kernel(values, inv_root, boundary, scaled_ref, rim_ref):
    scaled = (inv_root[...] * values[...].astype(F32)).astype(BF)
    scaled_ref[...] = scaled
    rim_ref[...] = take_columns(scaled, boundary[...], boundary.shape[1]).astype(BF)


def slot(odd, i):
    return jnp.where(odd == 1, len(OFFSETS) - 1 - i, i)


def own_gather_kernel(index, scaled, out_ref, table):
    rows = scaled.shape[0]
    count, piece = table.shape[0] // rows, table.shape[1]

    @pl.when(pl.program_id(0) == 0)
    def _():
        table[...] = from_pieces(scaled[...], piece, count)

    places = index[...]
    part = places // piece
    both = picked(table[...], selection(places % piece, piece))
    gathered = jnp.zeros((), F32)
    for i in range(count):
        gathered = jnp.where(part == i, both[i * rows : (i + 1) * rows], gathered)
    out_ref[...] = gathered.astype(BF)


def own_gather(scaled, index, piece):
    rows, owned = scaled.shape
    places = index.shape[1]
    return pl.pallas_call(
        own_gather_kernel,
        grid=(places // STEP,),
        in_specs=[
            pl.BlockSpec((1, STEP), lambda i: (0, i)),
            pl.BlockSpec(scaled.shape, lambda i: (0, 0)),
        ],
        out_specs=pl.BlockSpec((rows, STEP), lambda i: (0, i)),
        out_shape=jax.ShapeDtypeStruct((rows, places), BF),
        scratch_shapes=[pltpu.VMEM((owned // piece * rows, piece), BF)],
        name="own_gather",
    )(index, scaled)


def cells_kernel(first, odd, index, scale, kinetic, own, across, partner, past, term_ref, send_ref, keep_ref, table, acc):
    step = pl.program_id(0)
    rows, piece = partner.shape
    count = len(OFFSETS)

    @pl.when(step == 0)
    def _():
        for i, side in enumerate((across[1], across[0], partner[...], past[...])):
            low = pl.multiple_of(slot(odd[0], i) * rows, rows)
            table[pl.ds(low, rows)] = side

    places = index[...]
    chosen = selection(places % piece, piece)
    part = places // piece - first
    both = picked(table[...], chosen)
    gathered = own[...].astype(F32)
    for i in range(count):
        gathered = jnp.where(part == i, both[i * rows : (i + 1) * rows], gathered)
    gathered = gathered.astype(BF)
    terms = jnp.concatenate(
        [picked(gathered[:, i : i + TILE], kinetic[...]) for i in range(0, STEP, TILE)], axis=1
    )
    terms = terms * scale[...]
    term_ref[...] = terms.astype(BF)
    spread = jnp.concatenate([jnp.where(part == i, terms, 0.0).astype(BF) for i in range(count)], axis=0)
    sums = put_back(spread, chosen)

    @pl.when(step == 0)
    def _():
        acc[...] = sums

    @pl.when(step > 0)
    def _():
        acc[...] += sums

    @pl.when(step == pl.num_programs(0) - 1)
    def _():
        def side(i):
            low = pl.multiple_of(slot(odd[0], i) * rows, rows)
            return acc[pl.ds(low, rows)].astype(BF)

        send_ref[0] = side(3)
        send_ref[1] = side(2)
        keep_ref[0] = side(0)
        keep_ref[1] = side(1)


def cells(odd, own, across, partner, past, index, scale, kinetic, owned):
    rows, piece = partner.shape
    places = index.shape[1]
    count = len(OFFSETS)

    def kernel(*refs):
        cells_kernel(owned // piece, *refs)

    line = pl.BlockSpec((1, STEP), lambda i, odd: (0, i))
    wide = pl.BlockSpec((rows, STEP), lambda i, odd: (0, i))

    def whole(shape):
        return pl.BlockSpec(shape, lambda i, odd: (0,) * len(shape))

    pair = (2, rows, piece)
    return pl.pallas_call(
        kernel,
        grid_spec=pltpu.PrefetchScalarGridSpec(
            num_scalar_prefetch=1,
            grid=(places // STEP,),
            in_specs=[line, line, whole(kinetic.shape), wide, whole(pair), whole(partner.shape), whole(partner.shape)],
            out_specs=[wide, whole(pair), whole(pair)],
            scratch_shapes=[pltpu.VMEM((count * rows, piece), BF), pltpu.VMEM((count * rows, piece), F32)],
        ),
        out_shape=(
            jax.ShapeDtypeStruct((rows, places), BF),
            jax.ShapeDtypeStruct(pair, BF),
            jax.ShapeDtypeStruct(pair, BF),
        ),
        name="cells",
    )(odd, index, scale, kinetic, own, across, partner, past)


def own_sum_kernel(index, terms, out_ref, acc):
    step = pl.program_id(0)
    rows = terms.shape[0]
    piece = acc.shape[1]
    count = acc.shape[0] // rows
    places = index[...]
    part = places // piece
    values = terms[...].astype(F32)
    spread = jnp.concatenate([jnp.where(part == i, values, 0.0).astype(BF) for i in range(count)], axis=0)
    sums = put_back(spread, selection(places % piece, piece))

    @pl.when(step == 0)
    def _():
        acc[...] = sums

    @pl.when(step > 0)
    def _():
        acc[...] += sums

    @pl.when(step == pl.num_programs(0) - 1)
    def _():
        for i in range(count):
            out_ref[:, i * piece : (i + 1) * piece] = acc[i * rows : (i + 1) * rows]


def own_sum(terms, index, owned, piece):
    rows, places = terms.shape
    return pl.pallas_call(
        own_sum_kernel,
        grid=(places // STEP,),
        in_specs=[
            pl.BlockSpec((1, STEP), lambda i: (0, i)),
            pl.BlockSpec((rows, STEP), lambda i: (0, i)),
        ],
        out_specs=pl.BlockSpec((rows, owned), lambda i: (0, 0)),
        out_shape=jax.ShapeDtypeStruct((rows, owned), F32),
        scratch_shapes=[pltpu.VMEM((owned // piece * rows, piece), F32)],
        name="own_sum",
    )(index, terms)


def image_of(own, partner, across, past, scaled, inv_root, potential, boundary):
    back = partner[1].astype(F32) + across[1].astype(F32) + past[...].astype(F32)
    upper = back.astype(BF)
    lower = (back - upper.astype(F32)).astype(BF)
    rows, piece = back.shape
    sums = add_columns(jnp.concatenate([upper, lower], axis=0), boundary[...], piece, own.shape[1] // piece)
    total = own[...] + jnp.concatenate([part[:rows] + part[rows:] for part in sums], axis=1)
    return inv_root[...] * (total + potential[...] * scaled[...].astype(F32))


def first_kernel(own, partner, across, past, scaled, start, inv_root, potential, boundary, first_ref, scaled_ref, rim_ref):
    image = image_of(own, partner, across, past, scaled, inv_root, potential, boundary)
    first = ((image - CENTER * start[...].astype(F32)) / HALF).astype(BF)
    first_ref[...] = first
    scaled_new = (inv_root[...] * first.astype(F32)).astype(BF)
    scaled_ref[...] = scaled_new
    rim_ref[...] = take_columns(scaled_new, boundary[...], boundary.shape[1]).astype(BF)


def second_kernel(own, partner, across, past, scaled, start, first, inv_root, potential, boundary, out_ref, block_ref):
    image = image_of(own, partner, across, past, scaled, inv_root, potential, boundary)
    second = 2.0 * (image - CENTER * first[...].astype(F32)) / HALF - start[...].astype(F32)
    second = second.astype(BF)
    out_ref[...] = second
    width = block_ref.shape[2]
    for i in range(block_ref.shape[0]):
        block_ref[i] = second[:, i * width : (i + 1) * width]


def with_core(x):
    count = QUAD * lax.axis_size(SPACE[0])
    return lax.ppermute(x, SPACE, [(i, i ^ 1) for i in range(count)])


def with_chip(x):
    count = QUAD * lax.axis_size(SPACE[0])
    return lax.ppermute(x, SPACE, [(i, (i + 2 * (i % 2) - 1) % count) for i in range(count)])


def body(states_in, kinetic, cell_scale, cell_nodes, boundary, potential, inv_mass_root):
    nodes_per_cell = kinetic.shape[0]
    rows, owned = states_in.shape
    index = cell_nodes.T.reshape(1, -1)
    scale = jnp.repeat(cell_scale, nodes_per_cell).reshape(1, -1)
    stacked = jnp.kron(jnp.eye(TILE // nodes_per_cell, dtype=BF), kinetic.T)
    inv_root = inv_mass_root[None]
    potential = potential[None]
    boundary = boundary[None]
    width = boundary.shape[1]
    bands = lax.axis_size("band")
    odd = (lax.axis_index(SPACE[1]) % 2)[None]

    scaled, rim = pl.pallas_call(
        prepare_kernel,
        out_shape=(
            jax.ShapeDtypeStruct((rows, owned), BF),
            jax.ShapeDtypeStruct((rows, width), BF),
        ),
        name="prepare",
    )(states_in, inv_root, boundary)

    def operate(scaled, rim):
        partner = with_core(rim)
        across = with_chip(jnp.stack([rim, partner]))
        held, _ = lax.optimization_barrier((scaled, partner))
        edge, own = lax.optimization_barrier((across[0], own_gather(held, index, width)))
        past = with_core(edge)
        terms, send, keep = cells(odd, own, across, partner, past, index, scale, stacked, owned)
        partner = with_core(send)
        across = with_chip(jnp.stack([keep[0], (keep[1].astype(F32) + partner[0].astype(F32)).astype(BF)]))
        held, _ = lax.optimization_barrier((terms, partner))
        edge, own = lax.optimization_barrier((across[0], own_sum(held, index, owned, width)))
        past = with_core(edge)
        return own, partner, across, past

    arrived = operate(scaled, rim)
    first, scaled_first, rim = pl.pallas_call(
        first_kernel,
        out_shape=(
            jax.ShapeDtypeStruct((rows, owned), BF),
            jax.ShapeDtypeStruct((rows, owned), BF),
            jax.ShapeDtypeStruct((rows, width), BF),
        ),
        name="first",
    )(*arrived, scaled, states_in, inv_root, potential, boundary)
    arrived = operate(scaled_first, rim)
    filtered, blocks = pl.pallas_call(
        second_kernel,
        out_shape=(
            jax.ShapeDtypeStruct((rows, owned), BF),
            jax.ShapeDtypeStruct((bands, rows, owned // bands), BF),
        ),
        name="second",
    )(*arrived, scaled_first, states_in, first, inv_root, potential, boundary)

    outer = lax.axis_size(SPACE[0])
    node_total = owned * outer * QUAD
    regrouped = lax.all_to_all(blocks, "band", 0, 0, tiled=True).reshape(bands * rows, -1)
    partial_sum = lax.dot_general(regrouped, regrouped, (((1,), (1,)), ((), ())), preferred_element_type=F32)
    states = partial_sum.shape[0]
    blocks = partial_sum.astype(BF).reshape(bands * QUAD, states // (bands * QUAD), states)
    sums = lax.all_to_all(blocks, ("band", SPACE[1]), 0, 0, tiled=True).astype(F32).sum(axis=0)
    spread = jnp.broadcast_to(sums.astype(BF)[None], (outer, *sums.shape))
    total = lax.all_to_all(spread, SPACE[0], 0, 0, tiled=True).astype(F32).sum(axis=0)
    margin = lax.all_gather(total / node_total, SPACE[1], axis=0, tiled=True)
    return filtered, margin


def solution(mesh):
    bands = mesh.shape["band"]
    split = Mesh(mesh.devices.reshape(-1, QUAD, bands), (*SPACE, "band"))
    in_specs = (P("band", SPACE), P(), P(SPACE), P(None, SPACE), P(SPACE), P(SPACE), P(SPACE))
    out_specs = (P("band", SPACE), P("band", None))
    return jax.shard_map(body, mesh=split, in_specs=in_specs, out_specs=out_specs, check_vma=False)
```

time: 189 us -> 188 us (level)
  Pallas kernels: 55.4 us -> 70.6 us
  blocking collectives: 66.6 us -> 51.9 us
  starting transfers between devices: 51.4 us -> 43.6 us
  other arithmetic: 0.25 us -> 3.84 us
  local copies, waits for them, and re-layouts: 6.69 us -> 9.1 us
    pallas_call x2 -> x6, Pallas kernels: 48 us -> 63.1 us  [the longest x2 29.9 us: cells(): pl.pallas_call(kernel, grid_spec=pltpu.PrefetchScalarGridSpec(num_scalar_...]
    all_gather x2 -> x0, blocking collectives: 10.5 us -> none  [exchange_out(): return (lax.all_gather(rim, SPACE[1], axis=0), far, farther)]
    all_to_all x2 -> x0, starting transfers between devices: 7.69 us -> none  [exchange_back(): return (lax.all_to_all(near, SPACE[1], 0, 0, tiled=True), far, farther)]
    all_to_all x1, blocking collectives: 18.3 us -> 14.1 us  [body(): lax.all_to_all(blocks, ('band', SPACE[1]), 0, 0, tiled=True).astype(F32)]
    all_to_all x1, blocking collectives: 17.4 us -> 15.1 us  [body(): lax.all_to_all(blocks, 'band', 0, 0, tiled=True).reshape(bands * rows, -1)]
    ppermute x8 -> x12, waiting for transfers between devices: 6.75 us -> 5.86 us  [the longest x8 5.85 us: with_core(): return lax.ppermute(x, SPACE, [(i, i ^ 1) for i in range(count)])]
    unnamed x37 -> x27, local copies, waits for them, and re-layouts: 4.03 us -> 3.14 us
    ppermute x8 -> x12, starting transfers between devices: 43.7 us -> 43.6 us  [the longest x8 35.9 us: with_core(): return lax.ppermute(x, SPACE, [(i, i ^ 1) for i in range(count)])]
  transfers between devices with their start and end apart: 10 -> 12, of which waited for: 2 -> 7; matrix products, arithmetic and copies ran while one was open for 1% -> 3% of each run, Pallas kernels for 0% -> 18%
where the time goes in v4:
time: 188 us; the launch traced here: 186 us
  Pallas kernels  70.6 us (38%)
  blocking collectives  51.9 us (28%)
  starting transfers between devices  43.6 us (23%)
  local copies, waits for them, and re-layouts  9.1 us (5%)
  waiting for transfers between devices  5.86 us (3%)
  other arithmetic  3.84 us (2%)
    ppermute x8, starting transfers between devices, with_core(): return lax.ppermute(x, SPACE, [(i, i ^ 1) for i in range(count)])  35.9 us
    pallas_call x2, Pallas kernels, cells(): pl.pallas_call(kernel, grid_spec=pltpu.PrefetchScalarGridSpec(num_scalar_...  29.9 us
    pallas_call x2, Pallas kernels, own_sum(): pl.pallas_call(own_sum_kernel, grid=(places // STEP,), in_specs=[pl.Block...  17.6 us
    all_to_all x1, blocking collectives, body(): lax.all_to_all(spread, SPACE[0], 0, 0, tiled=True).astype(F32).sum(axis=0)  15.6 us
    pallas_call x2, Pallas kernels, own_gather(): pl.pallas_call(own_gather_kernel, grid=(places // STEP,), in_specs=[pl.Bl...  15.5 us
    all_to_all x1, blocking collectives, body(): lax.all_to_all(blocks, 'band', 0, 0, tiled=True).reshape(bands * rows, -1)  15.1 us
    all_to_all x1, blocking collectives, body(): lax.all_to_all(blocks, ('band', SPACE[1]), 0, 0, tiled=True).astype(F32)  14.1 us
    ppermute x4, starting transfers between devices, with_chip(): lax.ppermute(x, SPACE, [(i, (i + 2 * (i % 2) - 1) % count) for i in range...  7.68 us
  transfers between devices with their start and end apart: 12, of which 7 were waited for; matrix products, arithmetic and copies ran while one was open for 3% of the time, Pallas kernels for 18%

profile of v4, /device:TPU:1, one launch (start us, length us, event | category | flops | bytes accessed | tf_op | source)
XLA Modules:
  0.0 186.0 jit_solution(1932643620613400034)
XLA Ops:
  0.6 0.0 copy-start.12
  0.6 1.9 %prepare.1 = (bf16[64,2048]{1,0:T(8,128)(2,1)}, bf16[64,512]{1,0:T(8,128)(2,1)}) custom-call(bf16[64,2048]{1,0:T(8,128)(2,1)} %start.3, f32[1,2048]{1,0:T(1,128)} %bitcast.26, s32[1,512]{1,0:T(1,128)} %bitcast.34), custom_call_target="tpu_custom_call" | custom-call | tf_op jit(solution)/shard_map/prepare/pallas_call | solution.py:279
  2.6 8.7 %collective-permute-start = (bf16[64,512]{1,0:T(8,128)(2,1)}, bf16[64,512]{1,0:T(8,128)(2,1)S(1)}, u32[]{:S(2)}, u32[]{:S(2)}) collective-permute-start(bf16[64,512]{1,0:T(8,128)(2,1)} %get-tuple-element.27), channel_id=1, source_target_pairs={{0,4},{4,0},{8,12},{12,8},{16,20},{20,16},{24,28},{28,24},{32,36},... | collective-permute-start | bytes 196616 | tf_op jit(solution)/shard_map/ppermute | solution.py:258
  11.3 1.1 collective-permute-done.refs_6_
  12.4 0.9 pad_maximum_fusion
  13.3 1.9 %collective-permute-start.1 = (bf16[2,64,512]{2,1,0:T(8,128)(2,1)S(1)}, bf16[2,64,512]{2,1,0:T(8,128)(2,1)S(1)}, u32[]{:S(2)}, u32[]{:S(2)}) collective-permute-start(bf16[2,64,512]{2,1,0:T(8,128)(2,1)S(1)} %pad_maximum_fusion), channel_id=1, source_target_pairs={{0,508},{4,8},{8,4},{12,16},{16,12},{20,24},{24,20},{28,32},{32,28... | collective-permute-start | bytes 393224 | tf_op jit(solution)/shard_map/ppermute | solution.py:263
  15.2 0.8 copy.14
  16.0 0.9 copy.13
  17.0 0.8 reshape.28.index.refs_1_
  17.7 7.8 %own_gather.2.refs_4_ = bf16[64,16384]{1,0:T(8,128)(2,1)} custom-call(s32[1,16384]{1,0:T(1,128)} %reshape.28.index.refs_1_, bf16[64,2048]{1,0:T(8,128)(2,1)} %get-tuple-element.29.scaled), custom_call_target="tpu_custom_call" | custom-call | tf_op jit(solution)/shard_map/own_gather/pallas_call | solution.py:92
  25.5 0.0 collective-permute-done.1.refs_5_
  25.5 4.1 %collective-permute-start.2 = (bf16[64,512]{1,0:T(8,128)(2,1)S(1)}, bf16[64,512]{1,0:T(8,128)(2,1)S(1)}, u32[]{:S(2)}, u32[]{:S(2)}) collective-permute-start(bf16[64,512]{1,0:T(8,128)(2,1)S(1)} %slice_bitcast_fusion.3), channel_id=1, source_target_pairs={{0,4},{4,0},{8,12},{12,8},{16,20},{20,16},{24,28},{28,24},{32,36},... | collective-permute-start | bytes 196616 | tf_op jit(solution)/shard_map/ppermute | solution.py:258
  29.7 0.2 broadcast_multiply_fusion
  29.8 0.0 copy-done.12
  29.8 0.1 broadcast_in_dim.26
  29.9 0.8 reshape_reshape.3.refs_2_
  30.7 0.9 mul.27.refs_3_
  31.6 0.0 copy-done.6
  31.6 0.0 collective-permute-done.2.refs_7_
  31.6 0.0 copy-done.1
  31.6 0.6 copy-done.8
  32.2 14.9 %cells.2 = (bf16[64,16384]{1,0:T(8,128)(2,1)}, bf16[2,64,512]{2,1,0:T(8,128)(2,1)}, bf16[2,64,512]{2,1,0:T(8,128)(2,1)}) custom-call(s32[1]{0:T(128)} %bitcast.refs_0_, s32[1,16384]{1,0:T(1,128)} %reshape.28.index.refs_1_, f32[1,16384]{1,0:T(1,128)} %reshape_reshape.3.refs_2_, bf16[256,256]{1,0:T(8,128)(2,1)} %mul.27.refs_3_, ...), custom_call_target="tpu_custom_call" | custom-call | tf_op jit(solution)/shard_map/cells/pallas_call | solution.py:168
  47.1 1.9 %collective-permute-start.3 = (bf16[2,64,512]{2,1,0:T(8,128)(2,1)}, bf16[2,64,512]{2,1,0:T(8,128)(2,1)S(1)}, u32[]{:S(2)}, u32[]{:S(2)}) collective-permute-start(bf16[2,64,512]{2,1,0:T(8,128)(2,1)} %get-tuple-element.33), channel_id=1, source_target_pairs={{0,4},{4,0},{8,12},{12,8},{16,20},{20,16},{24,28},{28,24},{32,36},... | collective-permute-start | bytes 393224 | tf_op jit(solution)/shard_map/ppermute | solution.py:258
  49.1 0.8 slice.31
  49.9 0.7 collective-permute-done.3.partner
  50.6 0.9 add_convert_fusion.1
  51.5 1.9 %collective-permute-start.4 = (bf16[2,64,512]{2,1,0:T(8,128)(2,1)S(1)}, bf16[2,64,512]{2,1,0:T(8,128)(2,1)S(1)}, u32[]{:S(2)}, u32[]{:S(2)}) collective-permute-start(bf16[2,64,512]{2,1,0:T(8,128)(2,1)S(1)} %pad_maximum_fusion.1), channel_id=1, source_target_pairs={{0,508},{4,8},{8,4},{12,16},{16,12},{20,24},{24,20},{28,32},{32,28... | collective-permute-start | bytes 393224 | tf_op jit(solution)/shard_map/ppermute | solution.py:263
  53.4 8.8 %own_sum.2.own = f32[64,2048]{1,0:T(8,128)} custom-call(s32[1,16384]{1,0:T(1,128)} %reshape.28.index.refs_1_, bf16[64,16384]{1,0:T(8,128)(2,1)} %get-tuple-element.35.terms), custom_call_target="tpu_custom_call" | custom-call | tf_op jit(solution)/shard_map/own_sum/pallas_call | solution.py:213
  62.3 0.0 collective-permute-done.4.across
  62.3 6.1 %collective-permute-start.5 = (bf16[64,512]{1,0:T(8,128)(2,1)S(1)}, bf16[64,512]{1,0:T(8,128)(2,1)S(1)}, u32[]{:S(2)}, u32[]{:S(2)}) collective-permute-start(bf16[64,512]{1,0:T(8,128)(2,1)S(1)} %slice_bitcast_fusion.2), channel_id=1, source_target_pairs={{0,4},{4,0},{8,12},{12,8},{16,20},{20,16},{24,28},{28,24},{32,36},... | collective-permute-start | bytes 196616 | tf_op jit(solution)/shard_map/ppermute | solution.py:258
  68.4 0.9 collective-permute-done.5.past
  69.3 0.0 copy-done.4
  69.3 0.0 copy-done.5
  69.3 0.6 copy-done.11
  69.9 2.8 %first.1 = (bf16[64,2048]{1,0:T(8,128)(2,1)}, bf16[64,2048]{1,0:T(8,128)(2,1)}, bf16[64,512]{1,0:T(8,128)(2,1)}) custom-call(f32[64,2048]{1,0:T(8,128)} %own_sum.2.own, bf16[2,64,512]{2,1,0:T(8,128)(2,1)} %copy-done.4, bf16[2,64,512]{2,1,0:T(8,128)(2,1)} %copy-done.5, bf16[64,512]{1,0:T(8,128)(2,1)} %copy-done.11, ...), custom_call_target="tpu_custom_call" | custom-call | tf_op jit(solution)/shard_map/first/pallas_call | solution.py:303
  72.7 2.2 %collective-permute-start.6 = (bf16[64,512]{1,0:T(8,128)(2,1)}, bf16[64,512]{1,0:T(8,128)(2,1)S(1)}, u32[]{:S(2)}, u32[]{:S(2)}) collective-permute-start(bf16[64,512]{1,0:T(8,128)(2,1)} %get-tuple-element.38), channel_id=1, source_target_pairs={{0,4},{4,0},{8,12},{12,8},{16,20},{20,16},{24,28},{28,24},{32,36},... | collective-permute-start | bytes 196616 | tf_op jit(solution)/shard_map/ppermute | solution.py:258
  74.9 1.1 collective-permute-done.6.refs_6_
  76.0 0.9 pad_maximum_fusion.2
  76.9 1.9 %collective-permute-start.7 = (bf16[2,64,512]{2,1,0:T(8,128)(2,1)S(1)}, bf16[2,64,512]{2,1,0:T(8,128)(2,1)S(1)}, u32[]{:S(2)}, u32[]{:S(2)}) collective-permute-start(bf16[2,64,512]{2,1,0:T(8,128)(2,1)S(1)} %pad_maximum_fusion.2), channel_id=1, source_target_pairs={{0,508},{4,8},{8,4},{12,16},{16,12},{20,24},{24,20},{28,32},{32,28... | collective-permute-start | bytes 393224 | tf_op jit(solution)/shard_map/ppermute | solution.py:263
  78.8 7.7 %own_gather.3.refs_4_ = bf16[64,16384]{1,0:T(8,128)(2,1)} custom-call(s32[1,16384]{1,0:T(1,128)} %reshape.28.index.refs_1_, bf16[64,2048]{1,0:T(8,128)(2,1)} %get-tuple-element.40.scaled), custom_call_target="tpu_custom_call" | custom-call | tf_op jit(solution)/shard_map/own_gather/pallas_call | solution.py:92
  86.6 0.0 collective-permute-done.7.refs_5_
  86.6 4.1 %collective-permute-start.8 = (bf16[64,512]{1,0:T(8,128)(2,1)S(1)}, bf16[64,512]{1,0:T(8,128)(2,1)S(1)}, u32[]{:S(2)}, u32[]{:S(2)}) collective-permute-start(bf16[64,512]{1,0:T(8,128)(2,1)S(1)} %slice_bitcast_fusion.1), channel_id=1, source_target_pairs={{0,4},{4,0},{8,12},{12,8},{16,20},{20,16},{24,28},{28,24},{32,36},... | collective-permute-start | bytes 196616 | tf_op jit(solution)/shard_map/ppermute | solution.py:258
  90.8 0.9 collective-permute-done.8.refs_7_
  91.6 0.0 copy-done.7
  91.6 0.0 copy-done.3
  91.6 0.6 copy-done.9
  92.3 15.0 %cells.3 = (bf16[64,16384]{1,0:T(8,128)(2,1)}, bf16[2,64,512]{2,1,0:T(8,128)(2,1)}, bf16[2,64,512]{2,1,0:T(8,128)(2,1)}) custom-call(s32[1]{0:T(128)} %bitcast.refs_0_, s32[1,16384]{1,0:T(1,128)} %reshape.28.index.refs_1_, f32[1,16384]{1,0:T(1,128)} %reshape_reshape.3.refs_2_, bf16[256,256]{1,0:T(8,128)(2,1)} %mul.27.refs_3_, ...), custom_call_target="tpu_custom_call" | custom-call | tf_op jit(solution)/shard_map/cells/pallas_call | solution.py:168
  107.2 2.2 %collective-permute-start.9 = (bf16[2,64,512]{2,1,0:T(8,128)(2,1)}, bf16[2,64,512]{2,1,0:T(8,128)(2,1)S(1)}, u32[]{:S(2)}, u32[]{:S(2)}) collective-permute-start(bf16[2,64,512]{2,1,0:T(8,128)(2,1)} %get-tuple-element.44), channel_id=1, source_target_pairs={{0,4},{4,0},{8,12},{12,8},{16,20},{20,16},{24,28},{28,24},{32,36},... | collective-permute-start | bytes 393224 | tf_op jit(solution)/shard_map/ppermute | solution.py:258
  109.5 0.8 slice.36
  110.3 0.3 collective-permute-done.9.partner
  110.7 0.9 add_convert_fusion
  111.6 1.9 %collective-permute-start.10 = (bf16[2,64,512]{2,1,0:T(8,128)(2,1)S(1)}, bf16[2,64,512]{2,1,0:T(8,128)(2,1)S(1)}, u32[]{:S(2)}, u32[]{:S(2)}) collective-permute-start(bf16[2,64,512]{2,1,0:T(8,128)(2,1)S(1)} %pad_maximum_fusion.3), channel_id=1, source_target_pairs={{0,508},{4,8},{8,4},{12,16},{16,12},{20,24},{24,20},{28,32},{32,28... | collective-permute-start | bytes 393224 | tf_op jit(solution)/shard_map/ppermute | solution.py:263
  113.5 8.8 %own_sum.3.own = f32[64,2048]{1,0:T(8,128)} custom-call(s32[1,16384]{1,0:T(1,128)} %reshape.28.index.refs_1_, bf16[64,16384]{1,0:T(8,128)(2,1)} %get-tuple-element.46.terms), custom_call_target="tpu_custom_call" | custom-call | tf_op jit(solution)/shard_map/own_sum/pallas_call | solution.py:213
  122.3 0.0 collective-permute-done.10.across
  122.4 6.4 %collective-permute-start.11 = (bf16[64,512]{1,0:T(8,128)(2,1)S(1)}, bf16[64,512]{1,0:T(8,128)(2,1)S(1)}, u32[]{:S(2)}, u32[]{:S(2)}) collective-permute-start(bf16[64,512]{1,0:T(8,128)(2,1)S(1)} %slice_bitcast_fusion), channel_id=1, source_target_pairs={{0,4},{4,0},{8,12},{12,8},{16,20},{20,16},{24,28},{28,24},{32,36},... | collective-permute-start | bytes 196616 | tf_op jit(solution)/shard_map/ppermute | solution.py:258
  128.7 0.9 collective-permute-done.11.past
  129.6 0.6 copy-done.10
  130.2 2.8 %second.1 = (bf16[64,2048]{1,0:T(8,128)(2,1)}, bf16[4,64,512]{2,1,0:T(8,128)(2,1)}) custom-call(f32[64,2048]{1,0:T(8,128)} %own_sum.3.own, bf16[2,64,512]{2,1,0:T(8,128)(2,1)} %copy-done, bf16[2,64,512]{2,1,0:T(8,128)(2,1)} %copy-done.2, bf16[64,512]{1,0:T(8,128)(2,1)} %copy-done.10, bf16[64,2048]{1,0:T(8,128)(2,1)} %get-tuple-element.40.scaled, ...), custom_call_target="tpu_custom_call" | custom-call | tf_op jit(solution)/shard_map/second/pallas_call | solution.py:313
  133.0 15.1 %all_to_all.15 = bf16[4,64,512]{2,1,0:T(8,128)(2,1)S(1)} all-to-all(bf16[4,64,512]{2,1,0:T(8,128)(2,1)} %get-tuple-element.51), channel_id=1, replica_groups=mesh['outer'=32,'quad'=4,'band'=4] {'band'}, dimensions={0} | all-to-all | bytes 524288 | tf_op jit(solution)/shard_map/all_to_all | solution.py:324
  148.1 0.3 convolution_convert_fusion
  148.4 14.1 %all_to_all.16 = bf16[16,16,256]{2,1,0:T(8,128)(2,1)S(1)} all-to-all(bf16[16,16,256]{2,1,0:T(8,128)(2,1)S(1)} %bitcast.23), channel_id=1, replica_groups=mesh['outer'=32,'quad'=4,'band'=4] {'band','quad'}, dimensions={0} | all-to-all | bytes 262144 | tf_op jit(solution)/shard_map/all_to_all | solution.py:328
  162.5 15.6 %all_to_all.17 = bf16[32,16,256]{2,1,0:T(8,128)(2,1)S(1)} all-to-all(bf16[32,16,256]{2,1,0:T(8,128)(2,1)S(1)} %broadcast_in_dim.30), channel_id=1, replica_groups=mesh['outer'=32,'quad'=4,'band'=4] {'outer'}, dimensions={0} | all-to-all | bytes 524288 | tf_op jit(solution)/shard_map/all_to_all | solution.py:330
  178.2 7.1 %all_gather.3 = f32[64,256]{1,0:T(8,128)S(1)} all-gather(f32[16,256]{1,0:T(8,128)S(1)} %broadcast_multiply_fusion.1), channel_id=1, replica_groups=mesh['outer'=32,'quad'=4,'band'=4] {'quad'}, dimensions={0}, use_global_device_ids=true | all-gather | bytes 81920 | tf_op jit(solution)/shard_map/all_gather | solution.py:331
  185.3 0.6 copy.16
  (25 shorter events, 0.2 us)
Async XLA Ops:
  0.6 29.2 %copy-start.12 = (f32[256]{0:T(256)S(1)}, f32[256]{0:T(256)}, u32[]{:S(2)}) copy-start(f32[256]{0:T(256)} %param.9) | copy-start | bytes 3076
  2.6 9.8 %collective-permute-start = (bf16[64,512]{1,0:T(8,128)(2,1)}, bf16[64,512]{1,0:T(8,128)(2,1)S(1)}, u32[]{:S(2)}, u32[]{:S(2)}) collective-permute-start(bf16[64,512]{1,0:T(8,128)(2,1)} %get-tuple-element.27), channel_id=1, source_target_pairs={{0,4},{4,0},{8,12},{12,8},{16,20},{20,16},{24,28},{28,24},{32,36},... | collective-permute-start | bytes 196616 | tf_op jit(solution)/shard_map/ppermute | solution.py:258
  12.4 19.2 %copy-start.6 = (bf16[64,512]{1,0:T(8,128)(2,1)}, bf16[64,512]{1,0:T(8,128)(2,1)S(1)}, u32[]{:S(2)}) copy-start(bf16[64,512]{1,0:T(8,128)(2,1)S(1)} %collective-permute-done.refs_6_) | copy-start | bytes 196612
  13.3 12.2 %collective-permute-start.1 = (bf16[2,64,512]{2,1,0:T(8,128)(2,1)S(1)}, bf16[2,64,512]{2,1,0:T(8,128)(2,1)S(1)}, u32[]{:S(2)}, u32[]{:S(2)}) collective-permute-start(bf16[2,64,512]{2,1,0:T(8,128)(2,1)S(1)} %pad_maximum_fusion), channel_id=1, source_target_pairs={{0,508},{4,8},{8,4},{12,16},{16,12},{20,24},{24,20},{28,32},{32,28... | collective-permute-start | bytes 393224 | tf_op jit(solution)/shard_map/ppermute | solution.py:263
  25.5 6.1 %copy-start.1 = (bf16[2,64,512]{2,1,0:T(8,128)(2,1)}, bf16[2,64,512]{2,1,0:T(8,128)(2,1)S(1)}, u32[]{:S(2)}) copy-start(bf16[2,64,512]{2,1,0:T(8,128)(2,1)S(1)} %collective-permute-done.1.refs_5_) | copy-start | bytes 393220
  25.5 6.1 %collective-permute-start.2 = (bf16[64,512]{1,0:T(8,128)(2,1)S(1)}, bf16[64,512]{1,0:T(8,128)(2,1)S(1)}, u32[]{:S(2)}, u32[]{:S(2)}) collective-permute-start(bf16[64,512]{1,0:T(8,128)(2,1)S(1)} %slice_bitcast_fusion.3), channel_id=1, source_target_pairs={{0,4},{4,0},{8,12},{12,8},{16,20},{20,16},{24,28},{28,24},{32,36},... | collective-permute-start | bytes 196616 | tf_op jit(solution)/shard_map/ppermute | solution.py:258
  31.6 0.6 copy-start.8
  47.1 3.4 %collective-permute-start.3 = (bf16[2,64,512]{2,1,0:T(8,128)(2,1)}, bf16[2,64,512]{2,1,0:T(8,128)(2,1)S(1)}, u32[]{:S(2)}, u32[]{:S(2)}) collective-permute-start(bf16[2,64,512]{2,1,0:T(8,128)(2,1)} %get-tuple-element.33), channel_id=1, source_target_pairs={{0,4},{4,0},{8,12},{12,8},{16,20},{20,16},{24,28},{28,24},{32,36},... | collective-permute-start | bytes 393224 | tf_op jit(solution)/shard_map/ppermute | solution.py:258
  50.6 18.7 %copy-start.4 = (bf16[2,64,512]{2,1,0:T(8,128)(2,1)}, bf16[2,64,512]{2,1,0:T(8,128)(2,1)S(1)}, u32[]{:S(2)}) copy-start(bf16[2,64,512]{2,1,0:T(8,128)(2,1)S(1)} %collective-permute-done.3.partner) | copy-start | bytes 393220
  51.5 10.8 %collective-permute-start.4 = (bf16[2,64,512]{2,1,0:T(8,128)(2,1)S(1)}, bf16[2,64,512]{2,1,0:T(8,128)(2,1)S(1)}, u32[]{:S(2)}, u32[]{:S(2)}) collective-permute-start(bf16[2,64,512]{2,1,0:T(8,128)(2,1)S(1)} %pad_maximum_fusion.1), channel_id=1, source_target_pairs={{0,508},{4,8},{8,4},{12,16},{16,12},{20,24},{24,20},{28,32},{32,28... | collective-permute-start | bytes 393224 | tf_op jit(solution)/shard_map/ppermute | solution.py:263
  62.3 7.0 %copy-start.5 = (bf16[2,64,512]{2,1,0:T(8,128)(2,1)}, bf16[2,64,512]{2,1,0:T(8,128)(2,1)S(1)}, u32[]{:S(2)}) copy-start(bf16[2,64,512]{2,1,0:T(8,128)(2,1)S(1)} %collective-permute-done.4.across) | copy-start | bytes 393220
  62.3 7.0 %collective-permute-start.5 = (bf16[64,512]{1,0:T(8,128)(2,1)S(1)}, bf16[64,512]{1,0:T(8,128)(2,1)S(1)}, u32[]{:S(2)}, u32[]{:S(2)}) collective-permute-start(bf16[64,512]{1,0:T(8,128)(2,1)S(1)} %slice_bitcast_fusion.2), channel_id=1, source_target_pairs={{0,4},{4,0},{8,12},{12,8},{16,20},{20,16},{24,28},{28,24},{32,36},... | collective-permute-start | bytes 196616 | tf_op jit(solution)/shard_map/ppermute | solution.py:258
  69.3 0.6 copy-start.11
  72.7 3.3 %collective-permute-start.6 = (bf16[64,512]{1,0:T(8,128)(2,1)}, bf16[64,512]{1,0:T(8,128)(2,1)S(1)}, u32[]{:S(2)}, u32[]{:S(2)}) collective-permute-start(bf16[64,512]{1,0:T(8,128)(2,1)} %get-tuple-element.38), channel_id=1, source_target_pairs={{0,4},{4,0},{8,12},{12,8},{16,20},{20,16},{24,28},{28,24},{32,36},... | collective-permute-start | bytes 196616 | tf_op jit(solution)/shard_map/ppermute | solution.py:258
  76.0 15.6 %copy-start.7 = (bf16[64,512]{1,0:T(8,128)(2,1)}, bf16[64,512]{1,0:T(8,128)(2,1)S(1)}, u32[]{:S(2)}) copy-start(bf16[64,512]{1,0:T(8,128)(2,1)S(1)} %collective-permute-done.6.refs_6_) | copy-start | bytes 196612
  76.9 9.7 %collective-permute-start.7 = (bf16[2,64,512]{2,1,0:T(8,128)(2,1)S(1)}, bf16[2,64,512]{2,1,0:T(8,128)(2,1)S(1)}, u32[]{:S(2)}, u32[]{:S(2)}) collective-permute-start(bf16[2,64,512]{2,1,0:T(8,128)(2,1)S(1)} %pad_maximum_fusion.2), channel_id=1, source_target_pairs={{0,508},{4,8},{8,4},{12,16},{16,12},{20,24},{24,20},{28,32},{32,28... | collective-permute-start | bytes 393224 | tf_op jit(solution)/shard_map/ppermute | solution.py:263
  86.6 5.1 %copy-start.3 = (bf16[2,64,512]{2,1,0:T(8,128)(2,1)}, bf16[2,64,512]{2,1,0:T(8,128)(2,1)S(1)}, u32[]{:S(2)}) copy-start(bf16[2,64,512]{2,1,0:T(8,128)(2,1)S(1)} %collective-permute-done.7.refs_5_) | copy-start | bytes 393220
  86.6 5.0 %collective-permute-start.8 = (bf16[64,512]{1,0:T(8,128)(2,1)S(1)}, bf16[64,512]{1,0:T(8,128)(2,1)S(1)}, u32[]{:S(2)}, u32[]{:S(2)}) collective-permute-start(bf16[64,512]{1,0:T(8,128)(2,1)S(1)} %slice_bitcast_fusion.1), channel_id=1, source_target_pairs={{0,4},{4,0},{8,12},{12,8},{16,20},{20,16},{24,28},{28,24},{32,36},... | collective-permute-start | bytes 196616 | tf_op jit(solution)/shard_map/ppermute | solution.py:258
  91.6 0.6 copy-start.9
  107.2 3.4 %collective-permute-start.9 = (bf16[2,64,512]{2,1,0:T(8,128)(2,1)}, bf16[2,64,512]{2,1,0:T(8,128)(2,1)S(1)}, u32[]{:S(2)}, u32[]{:S(2)}) collective-permute-start(bf16[2,64,512]{2,1,0:T(8,128)(2,1)} %get-tuple-element.44), channel_id=1, source_target_pairs={{0,4},{4,0},{8,12},{12,8},{16,20},{20,16},{24,28},{28,24},{32,36},... | collective-permute-start | bytes 393224 | tf_op jit(solution)/shard_map/ppermute | solution.py:258
  110.7 18.9 %copy-start = (bf16[2,64,512]{2,1,0:T(8,128)(2,1)}, bf16[2,64,512]{2,1,0:T(8,128)(2,1)S(1)}, u32[]{:S(2)}) copy-start(bf16[2,64,512]{2,1,0:T(8,128)(2,1)S(1)} %collective-permute-done.9.partner) | copy-start | bytes 393220
  111.6 10.7 %collective-permute-start.10 = (bf16[2,64,512]{2,1,0:T(8,128)(2,1)S(1)}, bf16[2,64,512]{2,1,0:T(8,128)(2,1)S(1)}, u32[]{:S(2)}, u32[]{:S(2)}) collective-permute-start(bf16[2,64,512]{2,1,0:T(8,128)(2,1)S(1)} %pad_maximum_fusion.3), channel_id=1, source_target_pairs={{0,508},{4,8},{8,4},{12,16},{16,12},{20,24},{24,20},{28,32},{32,28... | collective-permute-start | bytes 393224 | tf_op jit(solution)/shard_map/ppermute | solution.py:263
  122.3 7.3 %copy-start.2 = (bf16[2,64,512]{2,1,0:T(8,128)(2,1)}, bf16[2,64,512]{2,1,0:T(8,128)(2,1)S(1)}, u32[]{:S(2)}) copy-start(bf16[2,64,512]{2,1,0:T(8,128)(2,1)S(1)} %collective-permute-done.10.across) | copy-start | bytes 393220
  122.4 7.3 %collective-permute-start.11 = (bf16[64,512]{1,0:T(8,128)(2,1)S(1)}, bf16[64,512]{1,0:T(8,128)(2,1)S(1)}, u32[]{:S(2)}, u32[]{:S(2)}) collective-permute-start(bf16[64,512]{1,0:T(8,128)(2,1)S(1)} %slice_bitcast_fusion), channel_id=1, source_target_pairs={{0,4},{4,0},{8,12},{12,8},{16,20},{20,16},{24,28},{28,24},{32,36},... | collective-permute-start | bytes 196616 | tf_op jit(solution)/shard_map/ppermute | solution.py:258
  129.6 0.6 copy-start.10

commit v5 on v4

--- a/solution.py
+++ b/solution.py
@@ -13,6 +13,8 @@
 HALF = 6.0
 TILE = 256
 STEP = 2048
+OWN_STEP = 4096
+ROOM = 24 * 2**20
 BF = jnp.bfloat16
 F32 = jnp.float32
 
@@ -91,28 +93,40 @@
     places = index.shape[1]
     return pl.pallas_call(
         own_gather_kernel,
-        grid=(places // STEP,),
+        grid=(places // OWN_STEP,),
         in_specs=[
-            pl.BlockSpec((1, STEP), lambda i: (0, i)),
+            pl.BlockSpec((1, OWN_STEP), lambda i: (0, i)),
             pl.BlockSpec(scaled.shape, lambda i: (0, 0)),
         ],
-        out_specs=pl.BlockSpec((rows, STEP), lambda i: (0, i)),
+        out_specs=pl.BlockSpec((rows, OWN_STEP), lambda i: (0, i)),
         out_shape=jax.ShapeDtypeStruct((rows, places), BF),
         scratch_shapes=[pltpu.VMEM((owned // piece * rows, piece), BF)],
         name="own_gather",
+        compiler_params=pltpu.CompilerParams(vmem_limit_bytes=ROOM),
     )(index, scaled)
 
 
-def cells_kernel(first, odd, index, scale, kinetic, own, across, partner, past, term_ref, send_ref, keep_ref, table, acc):
+def cells_kernel(first, odd, index, scale, kinetic, own, across, chip, past, term_ref, send_ref, keep_ref, table, matrix, acc):
     step = pl.program_id(0)
-    rows, piece = partner.shape
+    _, rows, piece = chip.shape
     count = len(OFFSETS)
 
     @pl.when(step == 0)
     def _():
-        for i, side in enumerate((across[1], across[0], partner[...], past[...])):
-            low = pl.multiple_of(slot(odd[0], i) * rows, rows)
-            table[pl.ds(low, rows)] = side
+        @pl.when(odd[0] == 0)
+        def _():
+            for i, ghosts in enumerate((across[0], across[1], chip[1], past[0])):
+                table[i * rows : (i + 1) * rows] = ghosts
+
+        @pl.when(odd[0] == 1)
+        def _():
+            for i, ghosts in enumerate((past[1], chip[0], across[0], across[1])):
+                table[i * rows : (i + 1) * rows] = ghosts
+
+        matrix[...] = jnp.zeros_like(matrix)
+        nodes = kinetic.shape[0]
+        for i in range(TILE // nodes):
+            matrix[i * nodes : (i + 1) * nodes, i * nodes : (i + 1) * nodes] = kinetic[...]
 
     places = index[...]
     chosen = selection(places % piece, piece)
@@ -123,7 +137,7 @@
         gathered = jnp.where(part == i, both[i * rows : (i + 1) * rows], gathered)
     gathered = gathered.astype(BF)
     terms = jnp.concatenate(
-        [picked(gathered[:, i : i + TILE], kinetic[...]) for i in range(0, STEP, TILE)], axis=1
+        [put_back(gathered[:, i : i + TILE], matrix[...]) for i in range(0, STEP, TILE)], axis=1
     )
     terms = terms * scale[...]
     term_ref[...] = terms.astype(BF)
@@ -144,14 +158,15 @@
             low = pl.multiple_of(slot(odd[0], i) * rows, rows)
             return acc[pl.ds(low, rows)].astype(BF)
 
-        send_ref[0] = side(3)
-        send_ref[1] = side(2)
+        send_ref[0] = jnp.zeros((rows, piece), BF)
+        send_ref[1] = side(3)
+        send_ref[2] = side(2)
         keep_ref[0] = side(0)
         keep_ref[1] = side(1)
 
 
-def cells(odd, own, across, partner, past, index, scale, kinetic, owned):
-    rows, piece = partner.shape
+def cells(odd, own, across, chip, past, index, scale, kinetic, owned):
+    _, rows, piece = chip.shape
     places = index.shape[1]
     count = len(OFFSETS)
 
@@ -164,23 +179,24 @@
     def whole(shape):
         return pl.BlockSpec(shape, lambda i, odd: (0,) * len(shape))
 
-    pair = (2, rows, piece)
+    pair, triple = (2, rows, piece), (3, rows, piece)
     return pl.pallas_call(
         kernel,
         grid_spec=pltpu.PrefetchScalarGridSpec(
             num_scalar_prefetch=1,
             grid=(places // STEP,),
-            in_specs=[line, line, whole(kinetic.shape), wide, whole(pair), whole(partner.shape), whole(partner.shape)],
-            out_specs=[wide, whole(pair), whole(pair)],
-            scratch_shapes=[pltpu.VMEM((count * rows, piece), BF), pltpu.VMEM((count * rows, piece), F32)],
+            in_specs=[line, line, whole(kinetic.shape), wide, whole(pair), whole(pair), whole(pair)],
+            out_specs=[wide, whole(triple), whole(pair)],
+            scratch_shapes=[pltpu.VMEM((count * rows, piece), BF), pltpu.VMEM((TILE, TILE), BF), pltpu.VMEM((count * rows, piece), F32)],
         ),
         out_shape=(
             jax.ShapeDtypeStruct((rows, places), BF),
+            jax.ShapeDtypeStruct(triple, BF),
             jax.ShapeDtypeStruct(pair, BF),
-            jax.ShapeDtypeStruct(pair, BF),
         ),
         name="cells",
-    )(odd, index, scale, kinetic, own, across, partner, past)
+        compiler_params=pltpu.CompilerParams(vmem_limit_bytes=ROOM),
+    )(odd, index, scale, kinetic, own, across, chip, past)
 
 
 def own_sum_kernel(index, terms, out_ref, acc):
@@ -212,20 +228,21 @@
     rows, places = terms.shape
     return pl.pallas_call(
         own_sum_kernel,
-        grid=(places // STEP,),
+        grid=(places // OWN_STEP,),
         in_specs=[
-            pl.BlockSpec((1, STEP), lambda i: (0, i)),
-            pl.BlockSpec((rows, STEP), lambda i: (0, i)),
+            pl.BlockSpec((1, OWN_STEP), lambda i: (0, i)),
+            pl.BlockSpec((rows, OWN_STEP), lambda i: (0, i)),
         ],
         out_specs=pl.BlockSpec((rows, owned), lambda i: (0, 0)),
         out_shape=jax.ShapeDtypeStruct((rows, owned), F32),
         scratch_shapes=[pltpu.VMEM((owned // piece * rows, piece), F32)],
         name="own_sum",
+        compiler_params=pltpu.CompilerParams(vmem_limit_bytes=ROOM),
     )(index, terms)
 
 
 def image_of(own, partner, across, past, scaled, inv_root, potential, boundary):
-    back = partner[1].astype(F32) + across[1].astype(F32) + past[...].astype(F32)
+    back = partner[2].astype(F32) + across[1].astype(F32) + past[...].astype(F32)
     upper = back.astype(BF)
     lower = (back - upper.astype(F32)).astype(BF)
     rows, piece = back.shape
@@ -268,7 +285,6 @@
     rows, owned = states_in.shape
     index = cell_nodes.T.reshape(1, -1)
     scale = jnp.repeat(cell_scale, nodes_per_cell).reshape(1, -1)
-    stacked = jnp.kron(jnp.eye(TILE // nodes_per_cell, dtype=BF), kinetic.T)
     inv_root = inv_mass_root[None]
     potential = potential[None]
     boundary = boundary[None]
@@ -283,17 +299,18 @@
             jax.ShapeDtypeStruct((rows, width), BF),
         ),
         name="prepare",
+        compiler_params=pltpu.CompilerParams(vmem_limit_bytes=ROOM),
     )(states_in, inv_root, boundary)
 
     def operate(scaled, rim):
-        partner = with_core(rim)
-        across = with_chip(jnp.stack([rim, partner]))
-        held, _ = lax.optimization_barrier((scaled, partner))
-        edge, own = lax.optimization_barrier((across[0], own_gather(held, index, width)))
-        past = with_core(edge)
-        terms, send, keep = cells(odd, own, across, partner, past, index, scale, stacked, owned)
+        chip = lax.all_gather(rim, SPACE[1], axis=0, axis_index_groups=[[0, 1], [2, 3]])
+        across = with_chip(chip)
+        held, _ = lax.optimization_barrier((scaled, chip))
+        across, own = lax.optimization_barrier((across, own_gather(held, index, width)))
+        past = with_core(across)
+        terms, send, keep = cells(odd, own, across, chip, past, index, scale, kinetic, owned)
         partner = with_core(send)
-        across = with_chip(jnp.stack([keep[0], (keep[1].astype(F32) + partner[0].astype(F32)).astype(BF)]))
+        across = with_chip((keep.astype(F32) + partner[:2].astype(F32)).astype(BF))
         held, _ = lax.optimization_barrier((terms, partner))
         edge, own = lax.optimization_barrier((across[0], own_sum(held, index, owned, width)))
         past = with_core(edge)
@@ -308,6 +325,7 @@
             jax.ShapeDtypeStruct((rows, width), BF),
         ),
         name="first",
+        compiler_params=pltpu.CompilerParams(vmem_limit_bytes=ROOM),
     )(*arrived, scaled, states_in, inv_root, potential, boundary)
     arrived = operate(scaled_first, rim)
     filtered, blocks = pl.pallas_call(
@@ -317,6 +335,7 @@
             jax.ShapeDtypeStruct((bands, rows, owned // bands), BF),
         ),
         name="second",
+        compiler_params=pltpu.CompilerParams(vmem_limit_bytes=ROOM),
     )(*arrived, scaled_first, states_in, first, inv_root, potential, boundary)
 
     outer = lax.axis_size(SPACE[0])

time: 188 us -> 160 us (0.85)
  Pallas kernels: 70.6 us -> 52.2 us
  starting transfers between devices: 43.6 us -> 33.4 us
  blocking collectives: 51.9 us -> 62 us
  local copies, waits for them, and re-layouts: 9.1 us -> 4.3 us
  other arithmetic: 3.84 us -> 0.15 us
    pallas_call x4, Pallas kernels: 33.1 us -> 21.9 us  [the longest x2 11.2 us: own_sum(): pl.pallas_call(own_sum_kernel, grid=(places // OWN_STEP,), in_specs=[pl.B...]
    all_gather x0 -> x2, blocking collectives: none -> 10.3 us  [operate(): lax.all_gather(rim, SPACE[1], axis=0, axis_index_groups=[[0, 1], [2, 3]])]
    ppermute x8 -> x6, starting transfers between devices: 35.9 us -> 25.7 us  [with_core(): return lax.ppermute(x, SPACE, [(i, i ^ 1) for i in range(count)])]
    all_to_all x1, blocking collectives: 15.1 us -> 17.7 us  [body(): lax.all_to_all(blocks, 'band', 0, 0, tiled=True).reshape(bands * rows, -1)]
    pallas_call x2, Pallas kernels: 29.9 us -> 27.9 us  [cells(): pl.pallas_call(kernel, grid_spec=pltpu.PrefetchScalarGridSpec(num_scalar_...]
    pallas_call x1, Pallas kernels: 2.77 us -> 0.79 us  [body(): pl.pallas_call(first_kernel, out_shape=(jax.ShapeDtypeStruct((rows, owned...]
    ppermute x8 -> x6, waiting for transfers between devices: 5.85 us -> 5.54 us  [with_core(): return lax.ppermute(x, SPACE, [(i, i ^ 1) for i in range(count)])]
  transfers between devices with their start and end apart: 12 -> 10, of which waited for: 7 -> 7; matrix products, arithmetic and copies ran while one was open for 3% -> 1% of each run, Pallas kernels for 18% -> 14%
where the time goes in v5:
time: 160 us; the launch traced here: 159 us
  blocking collectives  62 us (39%)
  Pallas kernels  52.2 us (33%)
  starting transfers between devices  33.4 us (21%)
  waiting for transfers between devices  5.69 us (4%)
  local copies, waits for them, and re-layouts  4.3 us (3%)
    pallas_call x2, Pallas kernels, cells(): pl.pallas_call(kernel, grid_spec=pltpu.PrefetchScalarGridSpec(num_scalar_...  27.9 us
    ppermute x6, starting transfers between devices, with_core(): return lax.ppermute(x, SPACE, [(i, i ^ 1) for i in range(count)])  25.7 us
    all_to_all x1, blocking collectives, body(): lax.all_to_all(blocks, 'band', 0, 0, tiled=True).reshape(bands * rows, -1)  17.7 us
    all_to_all x1, blocking collectives, body(): lax.all_to_all(spread, SPACE[0], 0, 0, tiled=True).astype(F32).sum(axis=0)  14 us
    all_to_all x1, blocking collectives, body(): lax.all_to_all(blocks, ('band', SPACE[1]), 0, 0, tiled=True).astype(F32)  12.8 us
    pallas_call x2, Pallas kernels, own_sum(): pl.pallas_call(own_sum_kernel, grid=(places // OWN_STEP,), in_specs=[pl.B...  11.2 us
    pallas_call x2, Pallas kernels, own_gather(): pl.pallas_call(own_gather_kernel, grid=(places // OWN_STEP,), in_specs=[p...  10.7 us
    all_gather x2, blocking collectives, operate(): lax.all_gather(rim, SPACE[1], axis=0, axis_index_groups=[[0, 1], [2, 3]])  10.3 us
  transfers between devices with their start and end apart: 10, of which 7 were waited for; matrix products, arithmetic and copies ran while one was open for 1% of the time, Pallas kernels for 14%

profile of v5, /device:TPU:1, one launch (start us, length us, event | category | flops | bytes accessed | tf_op | source)
XLA Modules:
  0.0 158.9 jit_solution(13767842562661815699)
XLA Ops:
  0.6 0.0 copy-start.8
  0.6 0.0 copy-start
  0.7 0.9 copy-done
  1.6 0.0 copy-start.2
  1.6 0.7 copy-done.2
  2.3 0.0 copy-start.6
  2.3 0.7 copy-done.6
  3.0 0.0 copy-start.4
  3.0 0.3 prepare.1
  3.3 8.4 %all-gather = bf16[128,512]{1,0:T(8,128)(2,1)S(1)} all-gather(bf16[64,512]{1,0:T(8,128)(2,1)S(1)} %get-tuple-element.27), channel_id=2, replica_groups={{0,4},{8,12},{1,5},{9,13},{2,6},{10,14},{3,7},{11,15},{16,20},{24,28},{..., dimensions={0}, use_global_device_ids=true | all-gather | bytes 196608 | tf_op jit(solution)/shard_map/all_gather | solution.py:306
  11.7 1.9 %collective-permute-start = (bf16[2,64,512]{2,1,0:T(8,128)(2,1)S(1)}, bf16[2,64,512]{2,1,0:T(8,128)(2,1)S(1)}, u32[]{:S(2)}, u32[]{:S(2)}) collective-permute-start(bf16[2,64,512]{2,1,0:T(8,128)(2,1)S(1)} %bitcast.15), channel_id=1, source_target_pairs={{0,508},{4,8},{8,4},{12,16},{16,12},{20,24},{24,20},{28,32},{32,28... | collective-permute-start | bytes 393224 | tf_op jit(solution)/shard_map/ppermute | solution.py:280
  13.6 0.9 copy.11
  14.5 0.1 reshape.14.index.refs_1_
  14.7 5.3 %own_gather.2.refs_4_ = bf16[64,16384]{1,0:T(8,128)(2,1)S(1)} custom-call(s32[1,16384]{1,0:T(1,128)S(1)} %reshape.14.index.refs_1_, bf16[64,2048]{1,0:T(8,128)(2,1)S(1)} %get-tuple-element.29.scaled), custom_call_target="tpu_custom_call" | custom-call | tf_op jit(solution)/shard_map/own_gather/pallas_call | solution.py:94
  20.0 0.0 collective-permute-done.refs_5_
  20.1 4.4 %collective-permute-start.1 = (bf16[2,64,512]{2,1,0:T(8,128)(2,1)S(1)}, bf16[2,64,512]{2,1,0:T(8,128)(2,1)S(1)}, u32[]{:S(2)}, u32[]{:S(2)}) collective-permute-start(bf16[2,64,512]{2,1,0:T(8,128)(2,1)S(1)} %collective-permute-done.refs_5_), channel_id=1, source_target_pairs={{0,4},{4,0},{8,12},{12,8},{16,20},{20,16},{24,28},{28,24},{32,36},... | collective-permute-start | bytes 393224 | tf_op jit(solution)/shard_map/ppermute | solution.py:275
  24.5 0.0 copy-done.8
  24.5 0.1 broadcast_in_dim.22
  24.6 0.1 reshape_reshape.3.refs_2_
  24.7 0.7 collective-permute-done.1.refs_7_
  25.4 0.0 copy-done.4
  25.4 13.9 %cells.2 = (bf16[64,16384]{1,0:T(8,128)(2,1)S(1)}, bf16[3,64,512]{2,1,0:T(8,128)(2,1)S(1)}, bf16[2,64,512]{2,1,0:T(8,128)(2,1)S(1)}) custom-call(s32[1]{0:T(128)} %bitcast.refs_0_, s32[1,16384]{1,0:T(1,128)S(1)} %reshape.14.index.refs_1_, f32[1,16384]{1,0:T(1,128)S(1)} %reshape_reshape.3.refs_2_, bf16[64,64]{1,0:T(8,128)(2,1)S(1)} %copy-done.4, ...), custom_call_target="tpu_custom_call" | custom-call | tf_op jit(solution)/shard_map/cells/pallas_call | solution.py:183
  39.4 0.0 copy-start.1
  39.4 0.0 copy-start.3
  39.4 0.0 copy-start.5
  39.4 0.0 copy-start.7
  39.4 2.4 %collective-permute-start.2 = (bf16[3,64,512]{2,1,0:T(8,128)(2,1)S(1)}, bf16[3,64,512]{2,1,0:T(8,128)(2,1)S(1)}, u32[]{:S(2)}, u32[]{:S(2)}) collective-permute-start(bf16[3,64,512]{2,1,0:T(8,128)(2,1)S(1)} %get-tuple-element.33), channel_id=1, source_target_pairs={{0,4},{4,0},{8,12},{12,8},{16,20},{20,16},{24,28},{28,24},{32,36},... | collective-permute-start | bytes 589832 | tf_op jit(solution)/shard_map/ppermute | solution.py:275
  41.8 1.1 collective-permute-done.2.partner
  42.9 1.9 %collective-permute-start.3 = (bf16[2,64,512]{2,1,0:T(8,128)(2,1)S(1)}, bf16[2,64,512]{2,1,0:T(8,128)(2,1)S(1)}, u32[]{:S(2)}, u32[]{:S(2)}) collective-permute-start(bf16[2,64,512]{2,1,0:T(8,128)(2,1)S(1)} %add_convert_fusion.1), channel_id=1, source_target_pairs={{0,508},{4,8},{8,4},{12,16},{16,12},{20,24},{24,20},{28,32},{32,28... | collective-permute-start | bytes 393224 | tf_op jit(solution)/shard_map/ppermute | solution.py:280
  44.8 5.6 %own_sum.2.own = f32[64,2048]{1,0:T(8,128)S(1)} custom-call(s32[1,16384]{1,0:T(1,128)S(1)} %reshape.14.index.refs_1_, bf16[64,16384]{1,0:T(8,128)(2,1)S(1)} %get-tuple-element.35.terms), custom_call_target="tpu_custom_call" | custom-call | tf_op jit(solution)/shard_map/own_sum/pallas_call | solution.py:229
  50.5 0.1 collective-permute-done.3.across
  50.6 6.0 %collective-permute-start.4 = (bf16[64,512]{1,0:T(8,128)(2,1)S(1)}, bf16[64,512]{1,0:T(8,128)(2,1)S(1)}, u32[]{:S(2)}, u32[]{:S(2)}) collective-permute-start(bf16[64,512]{1,0:T(8,128)(2,1)S(1)} %slice_bitcast_fusion.1), channel_id=1, source_target_pairs={{0,4},{4,0},{8,12},{12,8},{16,20},{20,16},{24,28},{28,24},{32,36},... | collective-permute-start | bytes 196616 | tf_op jit(solution)/shard_map/ppermute | solution.py:275
  56.6 0.9 collective-permute-done.4.past
  57.5 0.0 copy-done.1
  57.5 0.0 copy-done.3
  57.5 0.0 copy-done.5
  57.5 0.0 copy-done.7
  57.5 0.8 first.1
  58.3 1.9 %all-gather.1 = bf16[128,512]{1,0:T(8,128)(2,1)S(1)} all-gather(bf16[64,512]{1,0:T(8,128)(2,1)S(1)} %get-tuple-element.38), channel_id=3, replica_groups={{0,4},{8,12},{1,5},{9,13},{2,6},{10,14},{3,7},{11,15},{16,20},{24,28},{..., dimensions={0}, use_global_device_ids=true | all-gather | bytes 196608 | tf_op jit(solution)/shard_map/all_gather | solution.py:306
  60.2 1.9 %collective-permute-start.5 = (bf16[2,64,512]{2,1,0:T(8,128)(2,1)S(1)}, bf16[2,64,512]{2,1,0:T(8,128)(2,1)S(1)}, u32[]{:S(2)}, u32[]{:S(2)}) collective-permute-start(bf16[2,64,512]{2,1,0:T(8,128)(2,1)S(1)} %bitcast.17), channel_id=1, source_target_pairs={{0,508},{4,8},{8,4},{12,16},{16,12},{20,24},{24,20},{28,32},{32,28... | collective-permute-start | bytes 393224 | tf_op jit(solution)/shard_map/ppermute | solution.py:280
  62.1 5.3 %own_gather.3.refs_4_ = bf16[64,16384]{1,0:T(8,128)(2,1)S(1)} custom-call(s32[1,16384]{1,0:T(1,128)S(1)} %reshape.14.index.refs_1_, bf16[64,2048]{1,0:T(8,128)(2,1)S(1)} %get-tuple-element.40.scaled), custom_call_target="tpu_custom_call" | custom-call | tf_op jit(solution)/shard_map/own_gather/pallas_call | solution.py:94
  67.5 0.0 collective-permute-done.5.refs_5_
  67.5 5.5 %collective-permute-start.6 = (bf16[2,64,512]{2,1,0:T(8,128)(2,1)S(1)}, bf16[2,64,512]{2,1,0:T(8,128)(2,1)S(1)}, u32[]{:S(2)}, u32[]{:S(2)}) collective-permute-start(bf16[2,64,512]{2,1,0:T(8,128)(2,1)S(1)} %collective-permute-done.5.refs_5_), channel_id=1, source_target_pairs={{0,4},{4,0},{8,12},{12,8},{16,20},{20,16},{24,28},{28,24},{32,36},... | collective-permute-start | bytes 393224 | tf_op jit(solution)/shard_map/ppermute | solution.py:275
  72.9 1.0 collective-permute-done.6.refs_7_
  73.9 13.9 %cells.3 = (bf16[64,16384]{1,0:T(8,128)(2,1)S(1)}, bf16[3,64,512]{2,1,0:T(8,128)(2,1)S(1)}, bf16[2,64,512]{2,1,0:T(8,128)(2,1)S(1)}) custom-call(s32[1]{0:T(128)} %bitcast.refs_0_, s32[1,16384]{1,0:T(1,128)S(1)} %reshape.14.index.refs_1_, f32[1,16384]{1,0:T(1,128)S(1)} %reshape_reshape.3.refs_2_, bf16[64,64]{1,0:T(8,128)(2,1)S(1)} %copy-done.4, ...), custom_call_target="tpu_custom_call" | custom-call | tf_op jit(solution)/shard_map/cells/pallas_call | solution.py:183
  87.9 2.3 %collective-permute-start.7 = (bf16[3,64,512]{2,1,0:T(8,128)(2,1)S(1)}, bf16[3,64,512]{2,1,0:T(8,128)(2,1)S(1)}, u32[]{:S(2)}, u32[]{:S(2)}) collective-permute-start(bf16[3,64,512]{2,1,0:T(8,128)(2,1)S(1)} %get-tuple-element.44), channel_id=1, source_target_pairs={{0,4},{4,0},{8,12},{12,8},{16,20},{20,16},{24,28},{28,24},{32,36},... | collective-permute-start | bytes 589832 | tf_op jit(solution)/shard_map/ppermute | solution.py:275
  90.1 1.1 collective-permute-done.7.partner
  91.2 1.9 %collective-permute-start.8 = (bf16[2,64,512]{2,1,0:T(8,128)(2,1)S(1)}, bf16[2,64,512]{2,1,0:T(8,128)(2,1)S(1)}, u32[]{:S(2)}, u32[]{:S(2)}) collective-permute-start(bf16[2,64,512]{2,1,0:T(8,128)(2,1)S(1)} %add_convert_fusion), channel_id=1, source_target_pairs={{0,508},{4,8},{8,4},{12,16},{16,12},{20,24},{24,20},{28,32},{32,28... | collective-permute-start | bytes 393224 | tf_op jit(solution)/shard_map/ppermute | solution.py:280
  93.2 5.6 %own_sum.3.own = f32[64,2048]{1,0:T(8,128)S(1)} custom-call(s32[1,16384]{1,0:T(1,128)S(1)} %reshape.14.index.refs_1_, bf16[64,16384]{1,0:T(8,128)(2,1)S(1)} %get-tuple-element.46.terms), custom_call_target="tpu_custom_call" | custom-call | tf_op jit(solution)/shard_map/own_sum/pallas_call | solution.py:229
  98.8 0.0 collective-permute-done.8.across
  98.8 5.2 %collective-permute-start.9 = (bf16[64,512]{1,0:T(8,128)(2,1)S(1)}, bf16[64,512]{1,0:T(8,128)(2,1)S(1)}, u32[]{:S(2)}, u32[]{:S(2)}) collective-permute-start(bf16[64,512]{1,0:T(8,128)(2,1)S(1)} %slice_bitcast_fusion), channel_id=1, source_target_pairs={{0,4},{4,0},{8,12},{12,8},{16,20},{20,16},{24,28},{28,24},{32,36},... | collective-permute-start | bytes 196616 | tf_op jit(solution)/shard_map/ppermute | solution.py:275
  104.0 0.9 collective-permute-done.9.past
  104.9 1.3 second.1
  106.2 17.7 %all_to_all.15 = bf16[4,64,512]{2,1,0:T(8,128)(2,1)S(1)} all-to-all(bf16[4,64,512]{2,1,0:T(8,128)(2,1)S(1)} %get-tuple-element.51), channel_id=1, replica_groups=mesh['outer'=32,'quad'=4,'band'=4] {'band'}, dimensions={0} | all-to-all | bytes 524288 | tf_op jit(solution)/shard_map/all_to_all | solution.py:343
  123.9 0.3 convolution_convert_fusion
  124.2 12.8 %all_to_all.16 = bf16[16,16,256]{2,1,0:T(8,128)(2,1)S(1)} all-to-all(bf16[16,16,256]{2,1,0:T(8,128)(2,1)S(1)} %bitcast.28), channel_id=1, replica_groups=mesh['outer'=32,'quad'=4,'band'=4] {'band','quad'}, dimensions={0} | all-to-all | bytes 262144 | tf_op jit(solution)/shard_map/all_to_all | solution.py:347
  137.1 14.0 %all_to_all.17 = bf16[32,16,256]{2,1,0:T(8,128)(2,1)S(1)} all-to-all(bf16[32,16,256]{2,1,0:T(8,128)(2,1)S(1)} %broadcast_in_dim.26), channel_id=1, replica_groups=mesh['outer'=32,'quad'=4,'band'=4] {'outer'}, dimensions={0} | all-to-all | bytes 524288 | tf_op jit(solution)/shard_map/all_to_all | solution.py:349
  151.2 7.1 %all_gather.19 = f32[64,256]{1,0:T(8,128)S(1)} all-gather(f32[16,256]{1,0:T(8,128)S(1)} %broadcast_multiply_fusion), channel_id=1, replica_groups=mesh['outer'=32,'quad'=4,'band'=4] {'quad'}, dimensions={0}, use_global_device_ids=true | all-gather | bytes 81920 | tf_op jit(solution)/shard_map/all_gather | solution.py:350
  158.3 0.6 copy.13
  (8 shorter events, 0.2 us)
Async XLA Ops:
  0.6 23.8 %copy-start.8 = (f32[256]{0:T(256)S(1)}, f32[256]{0:T(256)}, u32[]{:S(2)}) copy-start(f32[256]{0:T(256)} %param.9) | copy-start | bytes 3076
  0.6 1.0 copy-start
  1.6 0.7 copy-start.2
  2.3 0.7 copy-start.6
  3.0 22.4 %copy-start.4 = (bf16[64,64]{1,0:T(8,128)(2,1)S(1)}, bf16[64,64]{1,0:T(8,128)(2,1)}, u32[]{:S(2)}) copy-start(bf16[64,64]{1,0:T(8,128)(2,1)} %refs_3_.3) | copy-start | bytes 24580
  11.7 8.3 %collective-permute-start = (bf16[2,64,512]{2,1,0:T(8,128)(2,1)S(1)}, bf16[2,64,512]{2,1,0:T(8,128)(2,1)S(1)}, u32[]{:S(2)}, u32[]{:S(2)}) collective-permute-start(bf16[2,64,512]{2,1,0:T(8,128)(2,1)S(1)} %bitcast.15), channel_id=1, source_target_pairs={{0,508},{4,8},{8,4},{12,16},{16,12},{20,24},{24,20},{28,32},{32,28... | collective-permute-start | bytes 393224 | tf_op jit(solution)/shard_map/ppermute | solution.py:280
  20.1 5.4 %collective-permute-start.1 = (bf16[2,64,512]{2,1,0:T(8,128)(2,1)S(1)}, bf16[2,64,512]{2,1,0:T(8,128)(2,1)S(1)}, u32[]{:S(2)}, u32[]{:S(2)}) collective-permute-start(bf16[2,64,512]{2,1,0:T(8,128)(2,1)S(1)} %collective-permute-done.refs_5_), channel_id=1, source_target_pairs={{0,4},{4,0},{8,12},{12,8},{16,20},{20,16},{24,28},{28,24},{32,36},... | collective-permute-start | bytes 393224 | tf_op jit(solution)/shard_map/ppermute | solution.py:275
  39.4 18.1 %copy-start.1 = (bf16[64,2048]{1,0:T(8,128)(2,1)S(1)}, bf16[64,2048]{1,0:T(8,128)(2,1)}, u32[]{:S(2)}) copy-start(bf16[64,2048]{1,0:T(8,128)(2,1)} %start.3) | copy-start | bytes 786436
  39.4 18.1 %copy-start.3 = (f32[2048]{0:T(1024)S(1)}, f32[2048]{0:T(1024)}, u32[]{:S(2)}) copy-start(f32[2048]{0:T(1024)} %param.13) | copy-start | bytes 24580
  39.4 18.1 %copy-start.5 = (f32[2048]{0:T(1024)S(1)}, f32[2048]{0:T(1024)}, u32[]{:S(2)}) copy-start(f32[2048]{0:T(1024)} %param.12) | copy-start | bytes 24580
  39.4 18.1 %copy-start.7 = (s32[512]{0:T(512)S(1)}, s32[512]{0:T(512)}, u32[]{:S(2)}) copy-start(s32[512]{0:T(512)} %param.11) | copy-start | bytes 6148
  39.4 3.5 %collective-permute-start.2 = (bf16[3,64,512]{2,1,0:T(8,128)(2,1)S(1)}, bf16[3,64,512]{2,1,0:T(8,128)(2,1)S(1)}, u32[]{:S(2)}, u32[]{:S(2)}) collective-permute-start(bf16[3,64,512]{2,1,0:T(8,128)(2,1)S(1)} %get-tuple-element.33), channel_id=1, source_target_pairs={{0,4},{4,0},{8,12},{12,8},{16,20},{20,16},{24,28},{28,24},{32,36},... | collective-permute-start | bytes 589832 | tf_op jit(solution)/shard_map/ppermute | solution.py:275
  42.9 7.7 %collective-permute-start.3 = (bf16[2,64,512]{2,1,0:T(8,128)(2,1)S(1)}, bf16[2,64,512]{2,1,0:T(8,128)(2,1)S(1)}, u32[]{:S(2)}, u32[]{:S(2)}) collective-permute-start(bf16[2,64,512]{2,1,0:T(8,128)(2,1)S(1)} %add_convert_fusion.1), channel_id=1, source_target_pairs={{0,508},{4,8},{8,4},{12,16},{16,12},{20,24},{24,20},{28,32},{32,28... | collective-permute-start | bytes 393224 | tf_op jit(solution)/shard_map/ppermute | solution.py:280
  50.6 6.9 %collective-permute-start.4 = (bf16[64,512]{1,0:T(8,128)(2,1)S(1)}, bf16[64,512]{1,0:T(8,128)(2,1)S(1)}, u32[]{:S(2)}, u32[]{:S(2)}) collective-permute-start(bf16[64,512]{1,0:T(8,128)(2,1)S(1)} %slice_bitcast_fusion.1), channel_id=1, source_target_pairs={{0,4},{4,0},{8,12},{12,8},{16,20},{20,16},{24,28},{28,24},{32,36},... | collective-permute-start | bytes 196616 | tf_op jit(solution)/shard_map/ppermute | solution.py:275
  60.2 7.3 %collective-permute-start.5 = (bf16[2,64,512]{2,1,0:T(8,128)(2,1)S(1)}, bf16[2,64,512]{2,1,0:T(8,128)(2,1)S(1)}, u32[]{:S(2)}, u32[]{:S(2)}) collective-permute-start(bf16[2,64,512]{2,1,0:T(8,128)(2,1)S(1)} %bitcast.17), channel_id=1, source_target_pairs={{0,508},{4,8},{8,4},{12,16},{16,12},{20,24},{24,20},{28,32},{32,28... | collective-permute-start | bytes 393224 | tf_op jit(solution)/shard_map/ppermute | solution.py:280
  67.5 6.4 %collective-permute-start.6 = (bf16[2,64,512]{2,1,0:T(8,128)(2,1)S(1)}, bf16[2,64,512]{2,1,0:T(8,128)(2,1)S(1)}, u32[]{:S(2)}, u32[]{:S(2)}) collective-permute-start(bf16[2,64,512]{2,1,0:T(8,128)(2,1)S(1)} %collective-permute-done.5.refs_5_), channel_id=1, source_target_pairs={{0,4},{4,0},{8,12},{12,8},{16,20},{20,16},{24,28},{28,24},{32,36},... | collective-permute-start | bytes 393224 | tf_op jit(solution)/shard_map/ppermute | solution.py:275
  87.9 3.3 %collective-permute-start.7 = (bf16[3,64,512]{2,1,0:T(8,128)(2,1)S(1)}, bf16[3,64,512]{2,1,0:T(8,128)(2,1)S(1)}, u32[]{:S(2)}, u32[]{:S(2)}) collective-permute-start(bf16[3,64,512]{2,1,0:T(8,128)(2,1)S(1)} %get-tuple-element.44), channel_id=1, source_target_pairs={{0,4},{4,0},{8,12},{12,8},{16,20},{20,16},{24,28},{28,24},{32,36},... | collective-permute-start | bytes 589832 | tf_op jit(solution)/shard_map/ppermute | solution.py:275
  91.2 7.6 %collective-permute-start.8 = (bf16[2,64,512]{2,1,0:T(8,128)(2,1)S(1)}, bf16[2,64,512]{2,1,0:T(8,128)(2,1)S(1)}, u32[]{:S(2)}, u32[]{:S(2)}) collective-permute-start(bf16[2,64,512]{2,1,0:T(8,128)(2,1)S(1)} %add_convert_fusion), channel_id=1, source_target_pairs={{0,508},{4,8},{8,4},{12,16},{16,12},{20,24},{24,20},{28,32},{32,28... | collective-permute-start | bytes 393224 | tf_op jit(solution)/shard_map/ppermute | solution.py:280
  98.8 6.1 %collective-permute-start.9 = (bf16[64,512]{1,0:T(8,128)(2,1)S(1)}, bf16[64,512]{1,0:T(8,128)(2,1)S(1)}, u32[]{:S(2)}, u32[]{:S(2)}) collective-permute-start(bf16[64,512]{1,0:T(8,128)(2,1)S(1)} %slice_bitcast_fusion), channel_id=1, source_target_pairs={{0,4},{4,0},{8,12},{12,8},{16,20},{20,16},{24,28},{28,24},{32,36},... | collective-permute-start | bytes 196616 | tf_op jit(solution)/shard_map/ppermute | solution.py:275

commit v6 on v5

--- a/solution.py
+++ b/solution.py
@@ -106,7 +106,7 @@
     )(index, scaled)
 
 
-def cells_kernel(first, odd, index, scale, kinetic, own, across, chip, past, term_ref, send_ref, keep_ref, table, matrix, acc):
+def cells_kernel(first, odd, index, scale, kinetic, own, chip, around, term_ref, send_ref, keep_ref, table, matrix, acc):
     step = pl.program_id(0)
     _, rows, piece = chip.shape
     count = len(OFFSETS)
@@ -115,12 +115,12 @@
     def _():
         @pl.when(odd[0] == 0)
         def _():
-            for i, ghosts in enumerate((across[0], across[1], chip[1], past[0])):
+            for i, ghosts in enumerate((around[0, 0], around[0, 1], chip[1], around[1, 0])):
                 table[i * rows : (i + 1) * rows] = ghosts
 
         @pl.when(odd[0] == 1)
         def _():
-            for i, ghosts in enumerate((past[1], chip[0], across[0], across[1])):
+            for i, ghosts in enumerate((around[0, 1], chip[0], around[1, 0], around[1, 1])):
                 table[i * rows : (i + 1) * rows] = ghosts
 
         matrix[...] = jnp.zeros_like(matrix)
@@ -158,14 +158,13 @@
             low = pl.multiple_of(slot(odd[0], i) * rows, rows)
             return acc[pl.ds(low, rows)].astype(BF)
 
-        send_ref[0] = jnp.zeros((rows, piece), BF)
-        send_ref[1] = side(3)
-        send_ref[2] = side(2)
+        send_ref[0] = side(3)
+        send_ref[1] = side(2)
         keep_ref[0] = side(0)
         keep_ref[1] = side(1)
 
 
-def cells(odd, own, across, chip, past, index, scale, kinetic, owned):
+def cells(odd, own, chip, around, index, scale, kinetic, owned):
     _, rows, piece = chip.shape
     places = index.shape[1]
     count = len(OFFSETS)
@@ -179,24 +178,24 @@
     def whole(shape):
         return pl.BlockSpec(shape, lambda i, odd: (0,) * len(shape))
 
-    pair, triple = (2, rows, piece), (3, rows, piece)
+    pair = (2, rows, piece)
     return pl.pallas_call(
         kernel,
         grid_spec=pltpu.PrefetchScalarGridSpec(
             num_scalar_prefetch=1,
             grid=(places // STEP,),
-            in_specs=[line, line, whole(kinetic.shape), wide, whole(pair), whole(pair), whole(pair)],
-            out_specs=[wide, whole(triple), whole(pair)],
+            in_specs=[line, line, whole(kinetic.shape), wide, whole(pair), whole(around.shape)],
+            out_specs=[wide, whole(pair), whole(pair)],
             scratch_shapes=[pltpu.VMEM((count * rows, piece), BF), pltpu.VMEM((TILE, TILE), BF), pltpu.VMEM((count * rows, piece), F32)],
         ),
         out_shape=(
             jax.ShapeDtypeStruct((rows, places), BF),
-            jax.ShapeDtypeStruct(triple, BF),
             jax.ShapeDtypeStruct(pair, BF),
+            jax.ShapeDtypeStruct(pair, BF),
         ),
         name="cells",
         compiler_params=pltpu.CompilerParams(vmem_limit_bytes=ROOM),
-    )(odd, index, scale, kinetic, own, across, chip, past)
+    )(odd, index, scale, kinetic, own, chip, around)
 
 
 def own_sum_kernel(index, terms, out_ref, acc):
@@ -241,8 +240,9 @@
     )(index, terms)
 
 
-def image_of(own, partner, across, past, scaled, inv_root, potential, boundary):
-    back = partner[2].astype(F32) + across[1].astype(F32) + past[...].astype(F32)
+def image_of(odd, own, chip, across, past, scaled, inv_root, potential, boundary):
+    other = 1 - odd[0]
+    back = chip[other, 1].astype(F32) + across[1].astype(F32) + past[other].astype(F32)
     upper = back.astype(BF)
     lower = (back - upper.astype(F32)).astype(BF)
     rows, piece = back.shape
@@ -251,8 +251,8 @@
     return inv_root[...] * (total + potential[...] * scaled[...].astype(F32))
 
 
-def first_kernel(own, partner, across, past, scaled, start, inv_root, potential, boundary, first_ref, scaled_ref, rim_ref):
-    image = image_of(own, partner, across, past, scaled, inv_root, potential, boundary)
+def first_kernel(odd, own, chip, across, past, scaled, start, inv_root, potential, boundary, first_ref, scaled_ref, rim_ref):
+    image = image_of(odd, own, chip, across, past, scaled, inv_root, potential, boundary)
     first = ((image - CENTER * start[...].astype(F32)) / HALF).astype(BF)
     first_ref[...] = first
     scaled_new = (inv_root[...] * first.astype(F32)).astype(BF)
@@ -260,8 +260,8 @@
     rim_ref[...] = take_columns(scaled_new, boundary[...], boundary.shape[1]).astype(BF)
 
 
-def second_kernel(own, partner, across, past, scaled, start, first, inv_root, potential, boundary, out_ref, block_ref):
-    image = image_of(own, partner, across, past, scaled, inv_root, potential, boundary)
+def second_kernel(odd, own, chip, across, past, scaled, start, first, inv_root, potential, boundary, out_ref, block_ref):
+    image = image_of(odd, own, chip, across, past, scaled, inv_root, potential, boundary)
     second = 2.0 * (image - CENTER * first[...].astype(F32)) / HALF - start[...].astype(F32)
     second = second.astype(BF)
     out_ref[...] = second
@@ -270,9 +270,8 @@
         block_ref[i] = second[:, i * width : (i + 1) * width]
 
 
-def with_core(x):
-    count = QUAD * lax.axis_size(SPACE[0])
-    return lax.ppermute(x, SPACE, [(i, i ^ 1) for i in range(count)])
+def of_chip(x):
+    return lax.all_gather(x, SPACE[1], axis=0, axis_index_groups=[[0, 1], [2, 3]])
 
 
 def with_chip(x):
@@ -303,19 +302,21 @@
     )(states_in, inv_root, boundary)
 
     def operate(scaled, rim):
-        chip = lax.all_gather(rim, SPACE[1], axis=0, axis_index_groups=[[0, 1], [2, 3]])
+        chip = of_chip(rim)
         across = with_chip(chip)
         held, _ = lax.optimization_barrier((scaled, chip))
         across, own = lax.optimization_barrier((across, own_gather(held, index, width)))
-        past = with_core(across)
-        terms, send, keep = cells(odd, own, across, chip, past, index, scale, kinetic, owned)
-        partner = with_core(send)
-        across = with_chip((keep.astype(F32) + partner[:2].astype(F32)).astype(BF))
-        held, _ = lax.optimization_barrier((terms, partner))
-        edge, own = lax.optimization_barrier((across[0], own_sum(held, index, owned, width)))
-        past = with_core(edge)
-        return own, partner, across, past
-
+        terms, send, keep = cells(odd, own, chip, of_chip(across), index, scale, kinetic, owned)
+        chip = of_chip(send)
+        handed = lax.dynamic_index_in_dim(chip, 1 - odd[0], 0, keepdims=False)[:1]
+        handed = jnp.pad(handed, ((1, 0), (0, 0), (0, 0)))
+        across = with_chip((keep.astype(F32) + handed.astype(F32)).astype(BF))
+        held, _ = lax.optimization_barrier((terms, chip))
+        across, own = lax.optimization_barrier((across, own_sum(held, index, owned, width)))
+        return odd, own, chip, across, of_chip(across[0])
+
+    number = pl.BlockSpec(memory_space=pltpu.SMEM)
+    array = pl.BlockSpec(memory_space=pltpu.VMEM)
     arrived = operate(scaled, rim)
     first, scaled_first, rim = pl.pallas_call(
         first_kernel,
@@ -324,6 +325,7 @@
             jax.ShapeDtypeStruct((rows, owned), BF),
             jax.ShapeDtypeStruct((rows, width), BF),
         ),
+        in_specs=[number, *[array] * 9],
         name="first",
         compiler_params=pltpu.CompilerParams(vmem_limit_bytes=ROOM),
     )(*arrived, scaled, states_in, inv_root, potential, boundary)
@@ -334,6 +336,7 @@
             jax.ShapeDtypeStruct((rows, owned), BF),
             jax.ShapeDtypeStruct((bands, rows, owned // bands), BF),
         ),
+        in_specs=[number, *[array] * 10],
         name="second",
         compiler_params=pltpu.CompilerParams(vmem_limit_bytes=ROOM),
     )(*arrived, scaled_first, states_in, first, inv_root, potential, boundary)

time: 160 us -> 153 us (0.956)
  starting transfers between devices: 33.4 us -> 7.66 us
  blocking collectives: 62 us -> 85.9 us
  waiting for transfers between devices: 5.69 us -> 0.14 us
    ppermute x6 -> x0, starting transfers between devices: 25.7 us -> none  [with_core(): return lax.ppermute(x, SPACE, [(i, i ^ 1) for i in range(count)])]
    all_gather x2 -> x8, blocking collectives: 10.3 us -> 34.1 us  [of_chip(): lax.all_gather(x, SPACE[1], axis=0, axis_index_groups=[[0, 1], [2, 3]])]
    ppermute x6 -> x0, waiting for transfers between devices: 5.54 us -> none  [with_core(): return lax.ppermute(x, SPACE, [(i, i ^ 1) for i in range(count)])]
  transfers between devices with their start and end apart: 10 -> 4, of which waited for: 7 -> 1; matrix products, arithmetic and copies ran while one was open for 1% -> 1% of each run, Pallas kernels for 14% -> 14%
where the time goes in v6:
time: 153 us; the launch traced here: 152 us
  blocking collectives  85.9 us (56%)
  Pallas kernels  52.2 us (34%)
  starting transfers between devices  7.66 us (5%)
  local copies, waits for them, and re-layouts  4.98 us (3%)
    all_gather x8, blocking collectives, of_chip(): lax.all_gather(x, SPACE[1], axis=0, axis_index_groups=[[0, 1], [2, 3]])  34.1 us
    pallas_call x2, Pallas kernels, cells(): pl.pallas_call(kernel, grid_spec=pltpu.PrefetchScalarGridSpec(num_scalar_...  27.9 us
    all_to_all x1, blocking collectives, body(): lax.all_to_all(blocks, 'band', 0, 0, tiled=True).reshape(bands * rows, -1)  17.8 us
    all_to_all x1, blocking collectives, body(): lax.all_to_all(spread, SPACE[0], 0, 0, tiled=True).astype(F32).sum(axis=0)  14 us
    all_to_all x1, blocking collectives, body(): lax.all_to_all(blocks, ('band', SPACE[1]), 0, 0, tiled=True).astype(F32)  12.8 us
    pallas_call x2, Pallas kernels, own_sum(): pl.pallas_call(own_sum_kernel, grid=(places // OWN_STEP,), in_specs=[pl.B...  11.2 us
    pallas_call x2, Pallas kernels, own_gather(): pl.pallas_call(own_gather_kernel, grid=(places // OWN_STEP,), in_specs=[p...  10.7 us
    ppermute x4, starting transfers between devices, with_chip(): lax.ppermute(x, SPACE, [(i, (i + 2 * (i % 2) - 1) % count) for i in range...  7.66 us
  transfers between devices with their start and end apart: 4, of which 1 were waited for; matrix products, arithmetic and copies ran while one was open for 1% of the time, Pallas kernels for 14%

profile of v6, /device:TPU:1, one launch (start us, length us, event | category | flops | bytes accessed | tf_op | source)
XLA Modules:
  0.0 152.1 jit_solution(7338517060346309739)
XLA Ops:
  0.6 0.0 copy-start
  0.6 0.9 copy-done
  1.6 0.0 copy-start.2
  1.6 0.7 copy-done.2
  2.3 0.0 copy-start.6
  2.3 0.7 copy-done.6
  3.0 0.0 copy-start.4
  3.0 0.3 prepare.1
  3.3 8.4 %all-gather = bf16[128,512]{1,0:T(8,128)(2,1)S(1)} all-gather(bf16[64,512]{1,0:T(8,128)(2,1)S(1)} %get-tuple-element.27), channel_id=2, replica_groups={{0,4},{8,12},{1,5},{9,13},{2,6},{10,14},{3,7},{11,15},{16,20},{24,28},{..., dimensions={0}, use_global_device_ids=true | all-gather | bytes 196608 | tf_op jit(solution)/shard_map/all_gather | solution.py:274
  11.7 1.9 %collective-permute-start = (bf16[2,64,512]{2,1,0:T(8,128)(2,1)S(1)}, bf16[2,64,512]{2,1,0:T(8,128)(2,1)S(1)}, u32[]{:S(2)}, u32[]{:S(2)}) collective-permute-start(bf16[2,64,512]{2,1,0:T(8,128)(2,1)S(1)} %bitcast.25), channel_id=1, source_target_pairs={{0,508},{4,8},{8,4},{12,16},{16,12},{20,24},{24,20},{28,32},{32,28... | collective-permute-start | bytes 393224 | tf_op jit(solution)/shard_map/ppermute | solution.py:279
  13.6 0.8 broadcast_in_dim.22
  14.4 0.1 reshape_reshape.3.refs_2_
  14.5 0.9 copy.12
  15.5 0.1 reshape.16.index.refs_1_
  15.6 5.3 %own_gather.2.refs_4_ = bf16[64,16384]{1,0:T(8,128)(2,1)S(1)} custom-call(s32[1,16384]{1,0:T(1,128)S(1)} %reshape.16.index.refs_1_, bf16[64,2048]{1,0:T(8,128)(2,1)S(1)} %get-tuple-element.29.scaled), custom_call_target="tpu_custom_call" | custom-call | tf_op jit(solution)/shard_map/own_gather/pallas_call | solution.py:94
  21.0 0.0 collective-permute-done
  21.0 3.9 %all-gather.1 = bf16[4,64,512]{2,1,0:T(8,128)(2,1)S(1)} all-gather(bf16[2,64,512]{2,1,0:T(8,128)(2,1)S(1)} %collective-permute-done), channel_id=3, replica_groups={{0,4},{8,12},{1,5},{9,13},{2,6},{10,14},{3,7},{11,15},{16,20},{24,28},{..., dimensions={0}, use_global_device_ids=true | all-gather | bytes 393216 | tf_op jit(solution)/shard_map/all_gather | solution.py:274
  24.8 0.0 copy-done.4
  24.8 13.9 %cells.2 = (bf16[64,16384]{1,0:T(8,128)(2,1)S(1)}, bf16[2,64,512]{2,1,0:T(8,128)(2,1)S(1)}, bf16[2,64,512]{2,1,0:T(8,128)(2,1)S(1)}) custom-call(s32[1]{0:T(128)} %bitcast.refs_0_.odd, s32[1,16384]{1,0:T(1,128)S(1)} %reshape.16.index.refs_1_, f32[1,16384]{1,0:T(1,128)S(1)} %reshape_reshape.3.refs_2_, bf16[64,64]{1,0:T(8,128)(2,1)S(1)} %copy-done.4, ...), custom_call_target="tpu_custom_call" | custom-call | tf_op jit(solution)/shard_map/cells/pallas_call | solution.py:182
  38.8 0.0 copy-start.1
  38.8 0.0 copy-start.3
  38.8 0.0 copy-start.5
  38.8 0.0 copy-start.7
  38.8 2.1 %all-gather.2 = bf16[4,64,512]{2,1,0:T(8,128)(2,1)S(1)} all-gather(bf16[2,64,512]{2,1,0:T(8,128)(2,1)S(1)} %get-tuple-element.33), channel_id=4, replica_groups={{0,4},{8,12},{1,5},{9,13},{2,6},{10,14},{3,7},{11,15},{16,20},{24,28},{..., dimensions={0}, use_global_device_ids=true | all-gather | bytes 393216 | tf_op jit(solution)/shard_map/all_gather | solution.py:274
  41.0 1.9 %collective-permute-start.1 = (bf16[2,64,512]{2,1,0:T(8,128)(2,1)S(1)}, bf16[2,64,512]{2,1,0:T(8,128)(2,1)S(1)}, u32[]{:S(2)}, u32[]{:S(2)}) collective-permute-start(bf16[2,64,512]{2,1,0:T(8,128)(2,1)S(1)} %add_convert_fusion.1), channel_id=1, source_target_pairs={{0,508},{4,8},{8,4},{12,16},{16,12},{20,24},{24,20},{28,32},{32,28... | collective-permute-start | bytes 393224 | tf_op jit(solution)/shard_map/ppermute | solution.py:279
  42.9 5.6 %own_sum.2.own = f32[64,2048]{1,0:T(8,128)S(1)} custom-call(s32[1,16384]{1,0:T(1,128)S(1)} %reshape.16.index.refs_1_, bf16[64,16384]{1,0:T(8,128)(2,1)S(1)} %get-tuple-element.35.terms), custom_call_target="tpu_custom_call" | custom-call | tf_op jit(solution)/shard_map/own_sum/pallas_call | solution.py:228
  48.5 0.1 collective-permute-done.1.across
  48.7 5.9 %all_gather.51.past = bf16[2,64,512]{2,1,0:T(8,128)(2,1)S(1)} all-gather(bf16[1,64,512]{2,1,0:T(8,128)(2,1)S(1)} %slice.20), channel_id=1, replica_groups={{0,4},{8,12},{1,5},{9,13},{2,6},{10,14},{3,7},{11,15},{16,20},{24,28},{..., dimensions={0}, use_global_device_ids=true | all-gather | bytes 196608 | tf_op jit(solution)/shard_map/all_gather | solution.py:274
  54.5 0.0 copy-done.1
  54.5 0.0 copy-done.3
  54.5 0.0 copy-done.5
  54.5 0.0 copy-done.7
  54.5 0.8 first.1
  55.3 1.9 %all-gather.3 = bf16[128,512]{1,0:T(8,128)(2,1)S(1)} all-gather(bf16[64,512]{1,0:T(8,128)(2,1)S(1)} %get-tuple-element.38), channel_id=5, replica_groups={{0,4},{8,12},{1,5},{9,13},{2,6},{10,14},{3,7},{11,15},{16,20},{24,28},{..., dimensions={0}, use_global_device_ids=true | all-gather | bytes 196608 | tf_op jit(solution)/shard_map/all_gather | solution.py:274
  57.2 1.9 %collective-permute-start.2 = (bf16[2,64,512]{2,1,0:T(8,128)(2,1)S(1)}, bf16[2,64,512]{2,1,0:T(8,128)(2,1)S(1)}, u32[]{:S(2)}, u32[]{:S(2)}) collective-permute-start(bf16[2,64,512]{2,1,0:T(8,128)(2,1)S(1)} %bitcast.27), channel_id=1, source_target_pairs={{0,508},{4,8},{8,4},{12,16},{16,12},{20,24},{24,20},{28,32},{32,28... | collective-permute-start | bytes 393224 | tf_op jit(solution)/shard_map/ppermute | solution.py:279
  59.2 5.3 %own_gather.3.refs_4_ = bf16[64,16384]{1,0:T(8,128)(2,1)S(1)} custom-call(s32[1,16384]{1,0:T(1,128)S(1)} %reshape.16.index.refs_1_, bf16[64,2048]{1,0:T(8,128)(2,1)S(1)} %get-tuple-element.40.scaled), custom_call_target="tpu_custom_call" | custom-call | tf_op jit(solution)/shard_map/own_gather/pallas_call | solution.py:94
  64.5 0.0 collective-permute-done.2
  64.5 5.2 %all-gather.4 = bf16[4,64,512]{2,1,0:T(8,128)(2,1)S(1)} all-gather(bf16[2,64,512]{2,1,0:T(8,128)(2,1)S(1)} %collective-permute-done.2), channel_id=6, replica_groups={{0,4},{8,12},{1,5},{9,13},{2,6},{10,14},{3,7},{11,15},{16,20},{24,28},{..., dimensions={0}, use_global_device_ids=true | all-gather | bytes 393216 | tf_op jit(solution)/shard_map/all_gather | solution.py:274
  69.7 13.9 %cells.3 = (bf16[64,16384]{1,0:T(8,128)(2,1)S(1)}, bf16[2,64,512]{2,1,0:T(8,128)(2,1)S(1)}, bf16[2,64,512]{2,1,0:T(8,128)(2,1)S(1)}) custom-call(s32[1]{0:T(128)} %bitcast.refs_0_.odd, s32[1,16384]{1,0:T(1,128)S(1)} %reshape.16.index.refs_1_, f32[1,16384]{1,0:T(1,128)S(1)} %reshape_reshape.3.refs_2_, bf16[64,64]{1,0:T(8,128)(2,1)S(1)} %copy-done.4, ...), custom_call_target="tpu_custom_call" | custom-call | tf_op jit(solution)/shard_map/cells/pallas_call | solution.py:182
  83.6 2.0 %all-gather.5 = bf16[4,64,512]{2,1,0:T(8,128)(2,1)S(1)} all-gather(bf16[2,64,512]{2,1,0:T(8,128)(2,1)S(1)} %get-tuple-element.44), channel_id=7, replica_groups={{0,4},{8,12},{1,5},{9,13},{2,6},{10,14},{3,7},{11,15},{16,20},{24,28},{..., dimensions={0}, use_global_device_ids=true | all-gather | bytes 393216 | tf_op jit(solution)/shard_map/all_gather | solution.py:274
  85.7 1.9 %collective-permute-start.3 = (bf16[2,64,512]{2,1,0:T(8,128)(2,1)S(1)}, bf16[2,64,512]{2,1,0:T(8,128)(2,1)S(1)}, u32[]{:S(2)}, u32[]{:S(2)}) collective-permute-start(bf16[2,64,512]{2,1,0:T(8,128)(2,1)S(1)} %add_convert_fusion), channel_id=1, source_target_pairs={{0,508},{4,8},{8,4},{12,16},{16,12},{20,24},{24,20},{28,32},{32,28... | collective-permute-start | bytes 393224 | tf_op jit(solution)/shard_map/ppermute | solution.py:279
  87.6 5.6 %own_sum.3.own = f32[64,2048]{1,0:T(8,128)S(1)} custom-call(s32[1,16384]{1,0:T(1,128)S(1)} %reshape.16.index.refs_1_, bf16[64,16384]{1,0:T(8,128)(2,1)S(1)} %get-tuple-element.46.terms), custom_call_target="tpu_custom_call" | custom-call | tf_op jit(solution)/shard_map/own_sum/pallas_call | solution.py:228
  93.2 0.0 collective-permute-done.3.across
  93.3 4.8 %all_gather.58.past = bf16[2,64,512]{2,1,0:T(8,128)(2,1)S(1)} all-gather(bf16[1,64,512]{2,1,0:T(8,128)(2,1)S(1)} %slice.23), channel_id=1, replica_groups={{0,4},{8,12},{1,5},{9,13},{2,6},{10,14},{3,7},{11,15},{16,20},{24,28},{..., dimensions={0}, use_global_device_ids=true | all-gather | bytes 196608 | tf_op jit(solution)/shard_map/all_gather | solution.py:274
  98.1 1.3 second.1
  99.4 17.8 %all_to_all.15 = bf16[4,64,512]{2,1,0:T(8,128)(2,1)S(1)} all-to-all(bf16[4,64,512]{2,1,0:T(8,128)(2,1)S(1)} %get-tuple-element.51), channel_id=1, replica_groups=mesh['outer'=32,'quad'=4,'band'=4] {'band'}, dimensions={0} | all-to-all | bytes 524288 | tf_op jit(solution)/shard_map/all_to_all | solution.py:346
  117.1 0.3 convolution_convert_fusion
  117.4 12.8 %all_to_all.16 = bf16[16,16,256]{2,1,0:T(8,128)(2,1)S(1)} all-to-all(bf16[16,16,256]{2,1,0:T(8,128)(2,1)S(1)} %bitcast.38), channel_id=1, replica_groups=mesh['outer'=32,'quad'=4,'band'=4] {'band','quad'}, dimensions={0} | all-to-all | bytes 262144 | tf_op jit(solution)/shard_map/all_to_all | solution.py:350
  130.3 14.0 %all_to_all.17 = bf16[32,16,256]{2,1,0:T(8,128)(2,1)S(1)} all-to-all(bf16[32,16,256]{2,1,0:T(8,128)(2,1)S(1)} %broadcast_in_dim.26), channel_id=1, replica_groups=mesh['outer'=32,'quad'=4,'band'=4] {'outer'}, dimensions={0} | all-to-all | bytes 524288 | tf_op jit(solution)/shard_map/all_to_all | solution.py:352
  144.4 7.1 %all_gather.59 = f32[64,256]{1,0:T(8,128)S(1)} all-gather(f32[16,256]{1,0:T(8,128)S(1)} %broadcast_multiply_fusion), channel_id=1, replica_groups=mesh['outer'=32,'quad'=4,'band'=4] {'quad'}, dimensions={0}, use_global_device_ids=true | all-gather | bytes 81920 | tf_op jit(solution)/shard_map/all_gather | solution.py:353
  151.5 0.6 copy.14
  (10 shorter events, 0.2 us)
Async XLA Ops:
  0.6 1.0 copy-start
  1.6 0.7 copy-start.2
  2.3 0.7 copy-start.6
  3.0 21.9 %copy-start.4 = (bf16[64,64]{1,0:T(8,128)(2,1)S(1)}, bf16[64,64]{1,0:T(8,128)(2,1)}, u32[]{:S(2)}) copy-start(bf16[64,64]{1,0:T(8,128)(2,1)} %refs_3_.3) | copy-start | bytes 24580
  11.7 9.3 %collective-permute-start = (bf16[2,64,512]{2,1,0:T(8,128)(2,1)S(1)}, bf16[2,64,512]{2,1,0:T(8,128)(2,1)S(1)}, u32[]{:S(2)}, u32[]{:S(2)}) collective-permute-start(bf16[2,64,512]{2,1,0:T(8,128)(2,1)S(1)} %bitcast.25), channel_id=1, source_target_pairs={{0,508},{4,8},{8,4},{12,16},{16,12},{20,24},{24,20},{28,32},{32,28... | collective-permute-start | bytes 393224 | tf_op jit(solution)/shard_map/ppermute | solution.py:279
  38.8 15.8 %copy-start.1 = (bf16[64,2048]{1,0:T(8,128)(2,1)S(1)}, bf16[64,2048]{1,0:T(8,128)(2,1)}, u32[]{:S(2)}) copy-start(bf16[64,2048]{1,0:T(8,128)(2,1)} %start.3) | copy-start | bytes 786436
  38.8 15.7 %copy-start.3 = (f32[2048]{0:T(1024)S(1)}, f32[2048]{0:T(1024)}, u32[]{:S(2)}) copy-start(f32[2048]{0:T(1024)} %param.13) | copy-start | bytes 24580
  38.8 15.7 %copy-start.5 = (f32[2048]{0:T(1024)S(1)}, f32[2048]{0:T(1024)}, u32[]{:S(2)}) copy-start(f32[2048]{0:T(1024)} %param.12) | copy-start | bytes 24580
  38.8 15.7 %copy-start.7 = (s32[512]{0:T(512)S(1)}, s32[512]{0:T(512)}, u32[]{:S(2)}) copy-start(s32[512]{0:T(512)} %param.11) | copy-start | bytes 6148
  41.0 7.7 %collective-permute-start.1 = (bf16[2,64,512]{2,1,0:T(8,128)(2,1)S(1)}, bf16[2,64,512]{2,1,0:T(8,128)(2,1)S(1)}, u32[]{:S(2)}, u32[]{:S(2)}) collective-permute-start(bf16[2,64,512]{2,1,0:T(8,128)(2,1)S(1)} %add_convert_fusion.1), channel_id=1, source_target_pairs={{0,508},{4,8},{8,4},{12,16},{16,12},{20,24},{24,20},{28,32},{32,28... | collective-permute-start | bytes 393224 | tf_op jit(solution)/shard_map/ppermute | solution.py:279
  57.2 7.3 %collective-permute-start.2 = (bf16[2,64,512]{2,1,0:T(8,128)(2,1)S(1)}, bf16[2,64,512]{2,1,0:T(8,128)(2,1)S(1)}, u32[]{:S(2)}, u32[]{:S(2)}) collective-permute-start(bf16[2,64,512]{2,1,0:T(8,128)(2,1)S(1)} %bitcast.27), channel_id=1, source_target_pairs={{0,508},{4,8},{8,4},{12,16},{16,12},{20,24},{24,20},{28,32},{32,28... | collective-permute-start | bytes 393224 | tf_op jit(solution)/shard_map/ppermute | solution.py:279
  85.7 7.6 %collective-permute-start.3 = (bf16[2,64,512]{2,1,0:T(8,128)(2,1)S(1)}, bf16[2,64,512]{2,1,0:T(8,128)(2,1)S(1)}, u32[]{:S(2)}, u32[]{:S(2)}) collective-permute-start(bf16[2,64,512]{2,1,0:T(8,128)(2,1)S(1)} %add_convert_fusion), channel_id=1, source_target_pairs={{0,508},{4,8},{8,4},{12,16},{16,12},{20,24},{24,20},{28,32},{32,28... | collective-permute-start | bytes 393224 | tf_op jit(solution)/shard_map/ppermute | solution.py:279

commit v7 on v6

--- a/solution.py
+++ b/solution.py
@@ -12,8 +12,8 @@
 CENTER = 0.5
 HALF = 6.0
 TILE = 256
-STEP = 2048
-OWN_STEP = 4096
+STEP = 4096
+OWN_STEP = 8192
 ROOM = 24 * 2**20
 BF = jnp.bfloat16
 F32 = jnp.float32

time: 153 us -> 150 us (0.980)
  Pallas kernels: 52.2 us -> 48.4 us
    pallas_call x2, Pallas kernels: 27.9 us -> 26 us  [cells(): pl.pallas_call(kernel, grid_spec=pltpu.PrefetchScalarGridSpec(num_scalar_...]
  transfers between devices with their start and end apart: 4 -> 4, of which waited for: 1 -> 1; matrix products, arithmetic and copies ran while one was open for 1% -> 1% of each run, Pallas kernels for 14% -> 13%
where the time goes in v7:
time: 150 us
  blocking collectives  86.6 us (58%)
  Pallas kernels  48.4 us (32%)
  starting transfers between devices  7.66 us (5%)
  local copies, waits for them, and re-layouts  4.98 us (3%)
    all_gather x8, blocking collectives, of_chip(): lax.all_gather(x, SPACE[1], axis=0, axis_index_groups=[[0, 1], [2, 3]])  34.7 us
    pallas_call x2, Pallas kernels, cells(): pl.pallas_call(kernel, grid_spec=pltpu.PrefetchScalarGridSpec(num_scalar_...  26 us
    all_to_all x1, blocking collectives, body(): lax.all_to_all(blocks, 'band', 0, 0, tiled=True).reshape(bands * rows, -1)  18.3 us
    all_to_all x1, blocking collectives, body(): lax.all_to_all(spread, SPACE[0], 0, 0, tiled=True).astype(F32).sum(axis=0)  13.5 us
    all_to_all x1, blocking collectives, body(): lax.all_to_all(blocks, ('band', SPACE[1]), 0, 0, tiled=True).astype(F32)  13.1 us
    pallas_call x2, Pallas kernels, own_sum(): pl.pallas_call(own_sum_kernel, grid=(places // OWN_STEP,), in_specs=[pl.B...  10.1 us
    pallas_call x2, Pallas kernels, own_gather(): pl.pallas_call(own_gather_kernel, grid=(places // OWN_STEP,), in_specs=[p...  9.92 us
    ppermute x4, starting transfers between devices, with_chip(): lax.ppermute(x, SPACE, [(i, (i + 2 * (i % 2) - 1) % count) for i in range...  7.66 us
  transfers between devices with their start and end apart: 4, of which 1 were waited for; matrix products, arithmetic and copies ran while one was open for 1% of the time, Pallas kernels for 13%

profile of v7, /device:TPU:1, one launch (start us, length us, event | category | flops | bytes accessed | tf_op | source)
XLA Modules:
  0.0 149.5 jit_solution(11377443207351867521)
XLA Ops:
  0.6 0.0 copy-start
  0.6 0.9 copy-done
  1.6 0.0 copy-start.2
  1.6 0.7 copy-done.2
  2.3 0.0 copy-start.6
  2.3 0.7 copy-done.6
  3.0 0.0 copy-start.4
  3.0 0.3 prepare.1
  3.3 8.4 %all-gather = bf16[128,512]{1,0:T(8,128)(2,1)S(1)} all-gather(bf16[64,512]{1,0:T(8,128)(2,1)S(1)} %get-tuple-element.27), channel_id=2, replica_groups={{0,4},{8,12},{1,5},{9,13},{2,6},{10,14},{3,7},{11,15},{16,20},{24,28},{..., dimensions={0}, use_global_device_ids=true | all-gather | bytes 196608 | tf_op jit(solution)/shard_map/all_gather | solution.py:274
  11.7 1.9 %collective-permute-start = (bf16[2,64,512]{2,1,0:T(8,128)(2,1)S(1)}, bf16[2,64,512]{2,1,0:T(8,128)(2,1)S(1)}, u32[]{:S(2)}, u32[]{:S(2)}) collective-permute-start(bf16[2,64,512]{2,1,0:T(8,128)(2,1)S(1)} %bitcast.25), channel_id=1, source_target_pairs={{0,508},{4,8},{8,4},{12,16},{16,12},{20,24},{24,20},{28,32},{32,28... | collective-permute-start | bytes 393224 | tf_op jit(solution)/shard_map/ppermute | solution.py:279
  13.6 0.8 broadcast_in_dim.22
  14.4 0.1 reshape_reshape.3.refs_2_
  14.5 0.9 copy.12
  15.5 0.1 reshape.16.index.refs_1_
  15.6 5.0 %own_gather.2.refs_4_ = bf16[64,16384]{1,0:T(8,128)(2,1)S(1)} custom-call(s32[1,16384]{1,0:T(1,128)S(1)} %reshape.16.index.refs_1_, bf16[64,2048]{1,0:T(8,128)(2,1)S(1)} %get-tuple-element.29.scaled), custom_call_target="tpu_custom_call" | custom-call | tf_op jit(solution)/shard_map/own_gather/pallas_call | solution.py:94
  20.6 0.0 collective-permute-done
  20.6 3.9 %all-gather.1 = bf16[4,64,512]{2,1,0:T(8,128)(2,1)S(1)} all-gather(bf16[2,64,512]{2,1,0:T(8,128)(2,1)S(1)} %collective-permute-done), channel_id=3, replica_groups={{0,4},{8,12},{1,5},{9,13},{2,6},{10,14},{3,7},{11,15},{16,20},{24,28},{..., dimensions={0}, use_global_device_ids=true | all-gather | bytes 393216 | tf_op jit(solution)/shard_map/all_gather | solution.py:274
  24.4 0.0 copy-done.4
  24.4 13.0 %cells.2 = (bf16[64,16384]{1,0:T(8,128)(2,1)S(1)}, bf16[2,64,512]{2,1,0:T(8,128)(2,1)S(1)}, bf16[2,64,512]{2,1,0:T(8,128)(2,1)S(1)}) custom-call(s32[1]{0:T(128)} %bitcast.refs_0_.odd, s32[1,16384]{1,0:T(1,128)S(1)} %reshape.16.index.refs_1_, f32[1,16384]{1,0:T(1,128)S(1)} %reshape_reshape.3.refs_2_, bf16[64,64]{1,0:T(8,128)(2,1)S(1)} %copy-done.4, ...), custom_call_target="tpu_custom_call" | custom-call | tf_op jit(solution)/shard_map/cells/pallas_call | solution.py:182
  37.4 0.0 copy-start.1
  37.4 0.0 copy-start.3
  37.4 0.0 copy-start.5
  37.5 0.0 copy-start.7
  37.5 2.1 %all-gather.2 = bf16[4,64,512]{2,1,0:T(8,128)(2,1)S(1)} all-gather(bf16[2,64,512]{2,1,0:T(8,128)(2,1)S(1)} %get-tuple-element.33), channel_id=4, replica_groups={{0,4},{8,12},{1,5},{9,13},{2,6},{10,14},{3,7},{11,15},{16,20},{24,28},{..., dimensions={0}, use_global_device_ids=true | all-gather | bytes 393216 | tf_op jit(solution)/shard_map/all_gather | solution.py:274
  39.6 1.9 %collective-permute-start.1 = (bf16[2,64,512]{2,1,0:T(8,128)(2,1)S(1)}, bf16[2,64,512]{2,1,0:T(8,128)(2,1)S(1)}, u32[]{:S(2)}, u32[]{:S(2)}) collective-permute-start(bf16[2,64,512]{2,1,0:T(8,128)(2,1)S(1)} %add_convert_fusion.1), channel_id=1, source_target_pairs={{0,508},{4,8},{8,4},{12,16},{16,12},{20,24},{24,20},{28,32},{32,28... | collective-permute-start | bytes 393224 | tf_op jit(solution)/shard_map/ppermute | solution.py:279
  41.6 5.1 %own_sum.2.own = f32[64,2048]{1,0:T(8,128)S(1)} custom-call(s32[1,16384]{1,0:T(1,128)S(1)} %reshape.16.index.refs_1_, bf16[64,16384]{1,0:T(8,128)(2,1)S(1)} %get-tuple-element.35.terms), custom_call_target="tpu_custom_call" | custom-call | tf_op jit(solution)/shard_map/own_sum/pallas_call | solution.py:228
  46.6 0.7 collective-permute-done.1.across
  47.3 5.3 %all_gather.51.past = bf16[2,64,512]{2,1,0:T(8,128)(2,1)S(1)} all-gather(bf16[1,64,512]{2,1,0:T(8,128)(2,1)S(1)} %slice.20), channel_id=1, replica_groups={{0,4},{8,12},{1,5},{9,13},{2,6},{10,14},{3,7},{11,15},{16,20},{24,28},{..., dimensions={0}, use_global_device_ids=true | all-gather | bytes 196608 | tf_op jit(solution)/shard_map/all_gather | solution.py:274
  52.6 0.0 copy-done.1
  52.6 0.0 copy-done.3
  52.6 0.0 copy-done.5
  52.6 0.0 copy-done.7
  52.6 0.8 first.1
  53.4 1.9 %all-gather.3 = bf16[128,512]{1,0:T(8,128)(2,1)S(1)} all-gather(bf16[64,512]{1,0:T(8,128)(2,1)S(1)} %get-tuple-element.38), channel_id=5, replica_groups={{0,4},{8,12},{1,5},{9,13},{2,6},{10,14},{3,7},{11,15},{16,20},{24,28},{..., dimensions={0}, use_global_device_ids=true | all-gather | bytes 196608 | tf_op jit(solution)/shard_map/all_gather | solution.py:274
  55.3 1.9 %collective-permute-start.2 = (bf16[2,64,512]{2,1,0:T(8,128)(2,1)S(1)}, bf16[2,64,512]{2,1,0:T(8,128)(2,1)S(1)}, u32[]{:S(2)}, u32[]{:S(2)}) collective-permute-start(bf16[2,64,512]{2,1,0:T(8,128)(2,1)S(1)} %bitcast.27), channel_id=1, source_target_pairs={{0,508},{4,8},{8,4},{12,16},{16,12},{20,24},{24,20},{28,32},{32,28... | collective-permute-start | bytes 393224 | tf_op jit(solution)/shard_map/ppermute | solution.py:279
  57.3 5.0 %own_gather.3.refs_4_ = bf16[64,16384]{1,0:T(8,128)(2,1)S(1)} custom-call(s32[1,16384]{1,0:T(1,128)S(1)} %reshape.16.index.refs_1_, bf16[64,2048]{1,0:T(8,128)(2,1)S(1)} %get-tuple-element.40.scaled), custom_call_target="tpu_custom_call" | custom-call | tf_op jit(solution)/shard_map/own_gather/pallas_call | solution.py:94
  62.2 0.0 collective-permute-done.2
  62.2 5.8 %all-gather.4 = bf16[4,64,512]{2,1,0:T(8,128)(2,1)S(1)} all-gather(bf16[2,64,512]{2,1,0:T(8,128)(2,1)S(1)} %collective-permute-done.2), channel_id=6, replica_groups={{0,4},{8,12},{1,5},{9,13},{2,6},{10,14},{3,7},{11,15},{16,20},{24,28},{..., dimensions={0}, use_global_device_ids=true | all-gather | bytes 393216 | tf_op jit(solution)/shard_map/all_gather | solution.py:274
  68.0 13.0 %cells.3 = (bf16[64,16384]{1,0:T(8,128)(2,1)S(1)}, bf16[2,64,512]{2,1,0:T(8,128)(2,1)S(1)}, bf16[2,64,512]{2,1,0:T(8,128)(2,1)S(1)}) custom-call(s32[1]{0:T(128)} %bitcast.refs_0_.odd, s32[1,16384]{1,0:T(1,128)S(1)} %reshape.16.index.refs_1_, f32[1,16384]{1,0:T(1,128)S(1)} %reshape_reshape.3.refs_2_, bf16[64,64]{1,0:T(8,128)(2,1)S(1)} %copy-done.4, ...), custom_call_target="tpu_custom_call" | custom-call | tf_op jit(solution)/shard_map/cells/pallas_call | solution.py:182
  81.0 2.0 %all-gather.5 = bf16[4,64,512]{2,1,0:T(8,128)(2,1)S(1)} all-gather(bf16[2,64,512]{2,1,0:T(8,128)(2,1)S(1)} %get-tuple-element.44), channel_id=7, replica_groups={{0,4},{8,12},{1,5},{9,13},{2,6},{10,14},{3,7},{11,15},{16,20},{24,28},{..., dimensions={0}, use_global_device_ids=true | all-gather | bytes 393216 | tf_op jit(solution)/shard_map/all_gather | solution.py:274
  83.0 1.9 %collective-permute-start.3 = (bf16[2,64,512]{2,1,0:T(8,128)(2,1)S(1)}, bf16[2,64,512]{2,1,0:T(8,128)(2,1)S(1)}, u32[]{:S(2)}, u32[]{:S(2)}) collective-permute-start(bf16[2,64,512]{2,1,0:T(8,128)(2,1)S(1)} %add_convert_fusion), channel_id=1, source_target_pairs={{0,508},{4,8},{8,4},{12,16},{16,12},{20,24},{24,20},{28,32},{32,28... | collective-permute-start | bytes 393224 | tf_op jit(solution)/shard_map/ppermute | solution.py:279
  84.9 5.0 %own_sum.3.own = f32[64,2048]{1,0:T(8,128)S(1)} custom-call(s32[1,16384]{1,0:T(1,128)S(1)} %reshape.16.index.refs_1_, bf16[64,16384]{1,0:T(8,128)(2,1)S(1)} %get-tuple-element.46.terms), custom_call_target="tpu_custom_call" | custom-call | tf_op jit(solution)/shard_map/own_sum/pallas_call | solution.py:228
  90.0 0.0 collective-permute-done.3.across
  90.0 5.4 %all_gather.58.past = bf16[2,64,512]{2,1,0:T(8,128)(2,1)S(1)} all-gather(bf16[1,64,512]{2,1,0:T(8,128)(2,1)S(1)} %slice.23), channel_id=1, replica_groups={{0,4},{8,12},{1,5},{9,13},{2,6},{10,14},{3,7},{11,15},{16,20},{24,28},{..., dimensions={0}, use_global_device_ids=true | all-gather | bytes 196608 | tf_op jit(solution)/shard_map/all_gather | solution.py:274
  95.4 1.3 second.1
  96.7 18.3 %all_to_all.15 = bf16[4,64,512]{2,1,0:T(8,128)(2,1)S(1)} all-to-all(bf16[4,64,512]{2,1,0:T(8,128)(2,1)S(1)} %get-tuple-element.51), channel_id=1, replica_groups=mesh['outer'=32,'quad'=4,'band'=4] {'band'}, dimensions={0} | all-to-all | bytes 524288 | tf_op jit(solution)/shard_map/all_to_all | solution.py:346
  115.0 0.3 convolution_convert_fusion
  115.2 13.1 %all_to_all.16 = bf16[16,16,256]{2,1,0:T(8,128)(2,1)S(1)} all-to-all(bf16[16,16,256]{2,1,0:T(8,128)(2,1)S(1)} %bitcast.38), channel_id=1, replica_groups=mesh['outer'=32,'quad'=4,'band'=4] {'band','quad'}, dimensions={0} | all-to-all | bytes 262144 | tf_op jit(solution)/shard_map/all_to_all | solution.py:350
  128.3 13.5 %all_to_all.17 = bf16[32,16,256]{2,1,0:T(8,128)(2,1)S(1)} all-to-all(bf16[32,16,256]{2,1,0:T(8,128)(2,1)S(1)} %broadcast_in_dim.26), channel_id=1, replica_groups=mesh['outer'=32,'quad'=4,'band'=4] {'outer'}, dimensions={0} | all-to-all | bytes 524288 | tf_op jit(solution)/shard_map/all_to_all | solution.py:352
  141.9 7.0 %all_gather.59 = f32[64,256]{1,0:T(8,128)S(1)} all-gather(f32[16,256]{1,0:T(8,128)S(1)} %broadcast_multiply_fusion), channel_id=1, replica_groups=mesh['outer'=32,'quad'=4,'band'=4] {'quad'}, dimensions={0}, use_global_device_ids=true | all-gather | bytes 81920 | tf_op jit(solution)/shard_map/all_gather | solution.py:353
  148.9 0.6 copy.14
  (10 shorter events, 0.2 us)
Async XLA Ops:
  0.6 1.0 copy-start
  1.6 0.7 copy-start.2
  2.3 0.7 copy-start.6
  3.0 21.5 %copy-start.4 = (bf16[64,64]{1,0:T(8,128)(2,1)S(1)}, bf16[64,64]{1,0:T(8,128)(2,1)}, u32[]{:S(2)}) copy-start(bf16[64,64]{1,0:T(8,128)(2,1)} %refs_3_.3) | copy-start | bytes 24580
  11.7 8.9 %collective-permute-start = (bf16[2,64,512]{2,1,0:T(8,128)(2,1)S(1)}, bf16[2,64,512]{2,1,0:T(8,128)(2,1)S(1)}, u32[]{:S(2)}, u32[]{:S(2)}) collective-permute-start(bf16[2,64,512]{2,1,0:T(8,128)(2,1)S(1)} %bitcast.25), channel_id=1, source_target_pairs={{0,508},{4,8},{8,4},{12,16},{16,12},{20,24},{24,20},{28,32},{32,28... | collective-permute-start | bytes 393224 | tf_op jit(solution)/shard_map/ppermute | solution.py:279
  37.4 15.2 %copy-start.1 = (bf16[64,2048]{1,0:T(8,128)(2,1)S(1)}, bf16[64,2048]{1,0:T(8,128)(2,1)}, u32[]{:S(2)}) copy-start(bf16[64,2048]{1,0:T(8,128)(2,1)} %start.3) | copy-start | bytes 786436
  37.4 15.2 %copy-start.3 = (f32[2048]{0:T(1024)S(1)}, f32[2048]{0:T(1024)}, u32[]{:S(2)}) copy-start(f32[2048]{0:T(1024)} %param.13) | copy-start | bytes 24580
  37.4 15.2 %copy-start.5 = (f32[2048]{0:T(1024)S(1)}, f32[2048]{0:T(1024)}, u32[]{:S(2)}) copy-start(f32[2048]{0:T(1024)} %param.12) | copy-start | bytes 24580
  37.5 15.2 %copy-start.7 = (s32[512]{0:T(512)S(1)}, s32[512]{0:T(512)}, u32[]{:S(2)}) copy-start(s32[512]{0:T(512)} %param.11) | copy-start | bytes 6148
  39.6 7.7 %collective-permute-start.1 = (bf16[2,64,512]{2,1,0:T(8,128)(2,1)S(1)}, bf16[2,64,512]{2,1,0:T(8,128)(2,1)S(1)}, u32[]{:S(2)}, u32[]{:S(2)}) collective-permute-start(bf16[2,64,512]{2,1,0:T(8,128)(2,1)S(1)} %add_convert_fusion.1), channel_id=1, source_target_pairs={{0,508},{4,8},{8,4},{12,16},{16,12},{20,24},{24,20},{28,32},{32,28... | collective-permute-start | bytes 393224 | tf_op jit(solution)/shard_map/ppermute | solution.py:279
  55.3 6.9 %collective-permute-start.2 = (bf16[2,64,512]{2,1,0:T(8,128)(2,1)S(1)}, bf16[2,64,512]{2,1,0:T(8,128)(2,1)S(1)}, u32[]{:S(2)}, u32[]{:S(2)}) collective-permute-start(bf16[2,64,512]{2,1,0:T(8,128)(2,1)S(1)} %bitcast.27), channel_id=1, source_target_pairs={{0,508},{4,8},{8,4},{12,16},{16,12},{20,24},{24,20},{28,32},{32,28... | collective-permute-start | bytes 393224 | tf_op jit(solution)/shard_map/ppermute | solution.py:279
  83.0 7.0 %collective-permute-start.3 = (bf16[2,64,512]{2,1,0:T(8,128)(2,1)S(1)}, bf16[2,64,512]{2,1,0:T(8,128)(2,1)S(1)}, u32[]{:S(2)}, u32[]{:S(2)}) collective-permute-start(bf16[2,64,512]{2,1,0:T(8,128)(2,1)S(1)} %add_convert_fusion), channel_id=1, source_target_pairs={{0,508},{4,8},{8,4},{12,16},{16,12},{20,24},{24,20},{28,32},{32,28... | collective-permute-start | bytes 393224 | tf_op jit(solution)/shard_map/ppermute | solution.py:279
